TPU v7x, 32 devices: a whole 2x2x4 slice. The times are simulated.
32 devices in a mesh: grp: 2 (over y), stn: 4 (over z), chan: 4 (over x, core).
Axes of the slice: x: 2, y: 2, z: 4, core: 2. Of those that a mesh axis runs over, the one named last changes fastest.
Arguments:
- voltages: bfloat16 [256, 31, 8192], P(('grp', 'stn', 'chan')), parts along dimension 0, may hold values from -6 to 6
- taps: float32 [16, 8192], replicated, may hold values from -1.5 to 1.5
Outputs:
- visibilities: bfloat16 [8, 3, 256, 2, 1024], P(('grp', 'stn'), None, 'chan'), parts along dimension 0
There are 2 independent parts, one for each index of `grp`. A program takes and returns all parts, laid end to end along the dimension named above; an argument that names none is the same for every part. Nothing has to cross between parts.
All inputs are finite; a program needn't handle non-finite values.
Results may differ from a plain program's by a relative error of at most 0.0053.
Values may be sent and summed in bfloat16 or wider, within the bound.
No kernel may reach another device: no remote copies, remote signals or barrier semaphores. Data moves between devices by JAX's collectives and lax.ppermute only.
A program may use at most 64 MiB of HBM per device.

v0:
```python
import functools
import math

import jax
import jax.numpy as jnp
import numpy as np
from jax import lax
from jax.experimental import pallas as pl
from jax.experimental.pallas import tpu as pltpu
from jax.sharding import PartitionSpec as P


AVG = 16
LANES = 128
SUB = 8
f32 = jnp.float32
bf16 = jnp.bfloat16


def add(a, b):
    return b if a is None else a if b is None else a + b


def sub(a, b):
    if b is None:
        return a
    return -b if a is None else a - b


def turn(re, im, num, den):
    num %= den
    if num == 0:
        return re, im
    if 4 * num == den:
        return im, None if re is None else -re
    if 2 * num == den:
        return (None if re is None else -re), (None if im is None else -im)
    if 4 * num == 3 * den:
        return (None if im is None else -im), re
    c = math.cos(2 * math.pi * num / den)
    s = math.sin(2 * math.pi * num / den)
    if 8 * num == den or 8 * num == 5 * den:
        if im is None:
            return re * c, re * -s
        if re is None:
            return im * s, im * c
        return (re + im) * c, (im - re) * c
    if im is None:
        return re * c, re * -s
    if re is None:
        return im * s, im * c
    return re * c + im * s, im * c - re * s


def fft(values, needed):
    size = len(values)
    if size == 1:
        return values
    if all(im is None for _, im in values):
        half_need = size // 4 + 1 if size >= 4 else size // 2
        even = fft(values[0::2], min(half_need, size // 2))
        odd = fft(values[1::2], min(half_need, size // 2))

        def mirrored(part, k):
            n = size // 2
            if k < len(part):
                return part[k]
            re, im = part[n - k]
            return re, (None if im is None else -im)

        out = [None] * size
        for k in range(size // 2):
            if k >= needed and k + size // 2 >= needed:
                continue
            er, ei = mirrored(even, k)
            tr, ti = turn(*mirrored(odd, k), k, size)
            out[k] = (add(er, tr), add(ei, ti))
            out[k + size // 2] = (sub(er, tr), sub(ei, ti))
        return out[:needed]
    even = fft(values[0::2], size // 2)
    odd = fft(values[1::2], size // 2)
    out = [None] * size
    for k in range(size // 2):
        er, ei = even[k]
        tr, ti = turn(*odd[k], k, size)
        out[k] = (add(er, tr), add(ei, ti))
        out[k + size // 2] = (sub(er, tr), sub(ei, ti))
    return out[:needed]


def filtered(x, weights, spectra_count):
    tap_count = len(weights)

    def correlated(h, v, count):
        out = []
        for n in range(count):
            total = h[0] * v[n]
            for k in range(1, len(h)):
                total = total + h[k] * v[n + k]
            out.append(total)
        return out

    if tap_count % 2 or spectra_count % 2:
        return correlated(weights, x, spectra_count)
    even, odd = weights[0::2], weights[1::2]
    first, second = x[0::2], x[1::2]
    count = spectra_count // 2
    need = count + tap_count // 2 - 1
    shared = correlated([e + o for e, o in zip(even, odd)], second, count)
    left = correlated(even, [first[n] - second[n] for n in range(need)], count)
    right = correlated(odd, [first[n + 1] - second[n] for n in range(need)], count)
    out = []
    for n in range(count):
        out += [shared[n] + left[n], shared[n] + right[n]]
    return out


SKEW = SUB + 1


def spectra_kernel(tw_ref, t_ref, x_ref, taps_ref, *refs, sizes, sends, turned):
    inputs, frames, tiles, per_step, spectra_count, tap_count, stations, chans = sizes
    outs = refs[: len(sends)]
    w_ref, a_ref, f_ref, xp_ref, s_ref, z_ref, sems = refs[len(sends) :]
    half = tiles // 2
    kept = LANES // 2
    rows = (half + 1) * spectra_count
    pitch = rows + 4
    block = AVG * spectra_count
    parts = tiles // AVG
    step = pl.program_id(0)

    def one_tile(here, carry):
        lanes = pl.ds(pl.multiple_of(here * LANES, LANES), LANES)
        x = [x_ref[frame, :, lanes].astype(f32) for frame in range(frames)]
        weights = [jnp.broadcast_to(taps_ref[t : t + 1, lanes], (inputs, LANES)) for t in range(tap_count)]
        at = (step * per_step + here) * SUB
        for s, total in enumerate(filtered(x, weights, spectra_count)):
            w_ref[pl.ds(pl.multiple_of(s * tiles * SUB + at, SUB), inputs), :] = total
        return carry

    lax.fori_loop(0, per_step, one_tile, 0)

    @pl.when(step == pl.num_programs(0) - 1)
    def finish():
        radix = 8
        other = tiles // radix
        columns = radix // 2 + 1

        def one_spectrum(s, carry):
            base = s * tiles * SUB
            present = {}
            for b in range(other):
                got = [
                    (w_ref[pl.ds(pl.multiple_of(base + (other * a + b) * SUB, SUB), SUB), :], None)
                    for a in range(radix)
                ]
                for ka, (re, im) in enumerate(fft(got, columns)):
                    if ka:
                        re, im = turn(re, im, ka * b, tiles)
                    for c, value in enumerate((re, im)):
                        present[ka, b, c] = value is not None
                        if value is not None:
                            at = ((ka * other + b) * 2 + c) * SUB
                            a_ref[at : at + SUB, :] = value
            for ka in range(columns):
                got = []
                for b in range(other):
                    at = (ka * other + b) * 2 * SUB
                    got.append(
                        tuple(
                            a_ref[at + c * SUB : at + (c + 1) * SUB, :] if present[ka, b, c] else None
                            for c in range(2)
                        )
                    )
                need = other if 0 < ka else other // 2 + 1
                done = fft(got, need)
                for kb, (re, im) in enumerate(done):
                    direct = ka + radix * kb
                    if direct <= half:
                        k1, conj = direct, False
                    else:
                        k1, conj = tiles - direct, True
                        if k1 % radix == ka:
                            continue
                    if im is None:
                        im = jnp.zeros_like(re)
                    if conj:
                        im = -im
                    cos = tw_ref[k1 * 2 * SUB : (k1 * 2 + 1) * SUB, :]
                    sin = tw_ref[(k1 * 2 + 1) * SUB : (k1 * 2 + 2) * SUB, :]
                    where = k1 * spectra_count + s
                    f_ref[pl.ds(where, SUB, stride=pitch), :] = re * cos + im * sin
                    f_ref[pl.ds(SUB * pitch + where, SUB, stride=pitch), :] = im * cos - re * sin
            return carry

        lax.fori_loop(0, spectra_count, one_spectrum, 0)

        def one_input(one, carry):
            for c in range(2):
                value = f_ref[pl.ds((c * SUB + one) * pitch, rows), :]
                high = value.astype(bf16)
                xp_ref[:, c * LANES : (c + 1) * LANES] = high
                xp_ref[:, (2 + c) * LANES : (3 + c) * LANES] = (value - high.astype(f32)).astype(bf16)
            for j in range(parts):
                if j < parts // 2:
                    first = j * block
                    which = 0
                else:
                    first = ((parts - 1 - j) * AVG + 1) * spectra_count
                    which = 1
                high = xp_ref[first : first + block, : 2 * LANES]
                low = xp_ref[first : first + block, 2 * LANES :]
                dims = (((1,), (1,)), ((), ()))
                both = lax.dot_general(t_ref[which], high, dims, preferred_element_type=f32)
                more = lax.dot_general(t_ref[which, : 2 * kept], low, dims, preferred_element_type=f32)
                out = both[: 2 * kept] + (both[2 * kept :] + more)
                for c in range(2):
                    for h in range(block // LANES):
                        tile = (j * 2 + c) * (block // LANES) + h
                        s_ref[pl.ds(tile * kept * SKEW + one, kept, stride=SKEW), :] = out[
                            c * kept : (c + 1) * kept, h * LANES : (h + 1) * LANES
                        ]
            return carry

        lax.fori_loop(0, inputs, one_input, 0)

        wide = 2 * block // LANES
        near = math.gcd(kept // chans, 2)

        def staged(m):
            for j in range(parts):
                for tile in range(wide):
                    z_ref[m * parts + j, :, tile * LANES : (tile + 1) * LANES] = s_ref[
                        pl.ds(((j * wide + tile) * kept + m) * SKEW, inputs), :
                    ].astype(bf16)

        copies = []
        for dc in range(chans):
            chan = lax.rem(lax.axis_index("chan") + dc, chans) if turned else dc

            def some_rows(at, carry, chan=chan):
                for one in range(near):
                    staged(chan * (kept // chans) + at * near + one)
                return carry

            lax.fori_loop(0, kept // chans // near, some_rows, 0)
            for index, (dz, of, skip, count) in enumerate(sends):
                if of != dc:
                    continue
                first = chan * (kept // chans * parts) + skip
                if dz is not None:
                    station = lax.rem(lax.axis_index("stn") + dz, stations)
                    first = first + station * (kept // chans * parts // stations)
                copies.append(
                    pltpu.make_async_copy(z_ref.at[pl.ds(first, count)], outs[index], sems.at[index])
                )
                copies[-1].start()
        for copy in copies:
            copy.wait()


def tables(frame_len):
    tiles = frame_len // LANES
    half = tiles // 2
    kept = LANES // 2
    k1 = np.arange(half + 1)[:, None]
    p = np.arange(LANES)[None, :]
    angle = 2 * np.pi * ((k1 * p) % frame_len) / frame_len
    tw = np.stack([np.cos(angle), np.sin(angle)], axis=1)[:, :, None, :]
    tw = np.broadcast_to(tw, (half + 1, 2, SUB, LANES)).reshape(-1, LANES).astype(np.float32)

    def one(m, sign):
        theta = 2 * np.pi * ((m[:, None] * p) % LANES) / LANES
        cos, sin = np.cos(theta), np.sin(theta)
        full = np.concatenate(
            [np.concatenate([cos, sin], axis=1), sign * np.concatenate([-sin, cos], axis=1)], axis=0
        )
        full = (full * frame_len ** (-0.5)).astype(np.float32)
        high = full.astype(jnp.bfloat16)
        low = (full - high.astype(np.float32)).astype(jnp.bfloat16)
        return np.concatenate([high, low], axis=0)

    m = np.arange(kept)
    return tw, np.stack([one(m, 1.0), one(LANES - 1 - m, -1.0)])


HBM = pl.BlockSpec(memory_space=pl.ANY)


def make_spectra(voltages, taps, sends, stations, chans, turned):
    frames, inputs, frame_len = voltages.shape
    tap_count = taps.shape[0]
    spectra_count = frames - tap_count + 1
    tiles = frame_len // LANES
    half = tiles // 2
    rows = (half + 1) * spectra_count
    block = AVG * spectra_count
    groups = frame_len // 2 // AVG
    per_step = 8
    tw, t = tables(frame_len)
    sizes = (inputs, frames, tiles, per_step, spectra_count, tap_count, stations, chans)
    return pl.pallas_call(
        functools.partial(spectra_kernel, sizes=sizes, sends=sends, turned=turned),
        name="spectra",
        grid=(tiles // per_step,),
        in_specs=[
            pl.BlockSpec(tw.shape, lambda q: (0, 0)),
            pl.BlockSpec(t.shape, lambda q: (0, 0, 0)),
            pl.BlockSpec((frames, inputs, per_step * LANES), lambda q: (0, 0, q)),
            pl.BlockSpec((tap_count, per_step * LANES), lambda q: (0, q)),
        ],
        out_specs=[HBM] * len(sends),
        out_shape=[jax.ShapeDtypeStruct((count, inputs, 2 * block), bf16) for _, _, _, count in sends],
        scratch_shapes=[
            pltpu.VMEM((spectra_count * tiles * SUB, LANES), f32),
            pltpu.VMEM((5 * (tiles // 8) * 2 * SUB, LANES), f32),
            pltpu.VMEM((2 * SUB * (rows + 4), LANES), f32),
            pltpu.VMEM((rows, 4 * LANES), bf16),
            pltpu.VMEM((groups * (2 * block // LANES) * SKEW, LANES), f32),
            pltpu.VMEM((groups, inputs, 2 * block), bf16),
            pltpu.SemaphoreType.DMA((len(sends),)),
        ],
    )(jnp.asarray(tw), jnp.asarray(t), voltages, taps)


def lefts(own):
    wide = own.shape[1]
    return [own, jnp.concatenate([own[:, wide // 2 :], -own[:, : wide // 2]], axis=1)]


def tiles_of(blocks, slot, p_ref, q_ref, scale):
    target, rest = blocks
    block_inputs = target.shape[0]
    copies = LANES // block_inputs
    out_rows = block_inputs * block_inputs // LANES
    place = lax.broadcasted_iota(jnp.int32, (out_rows, LANES), 1) // block_inputs
    right = jnp.concatenate([target] * copies, axis=0)
    left = jnp.concatenate([piece for pair in rest for piece in pair], axis=0)
    out = lax.dot_general(left, right, (((1,), (1,)), ((), ())), preferred_element_type=f32)
    p_ref[slot, :, :] = out * scale
    tiles = []
    for d in range(len(rest)):
        for part in range(2):
            base = (2 * d + part) * block_inputs
            value = p_ref[slot, pl.ds(base, out_rows, stride=copies), :]
            for r in range(1, copies):
                value = jnp.where(place == r, p_ref[slot, pl.ds(base + r, out_rows, stride=copies), :], value)
            q_ref[slot, d, pl.ds(part, out_rows, stride=2), :] = value
        tiles.append(q_ref[slot, d].astype(bf16))
    return tiles


def correlate_kernel(r_ref, o_ref, p_ref, q_ref, *, sizes):
    stations, chans, reach, scale = sizes

    def one_target(target, carry):
        owns = []
        for d in range(reach):
            b = lax.rem(target - d + stations, stations)
            owns.append(jnp.concatenate([r_ref[c * stations + b, 0] for c in range(chans)], axis=0))
        tiles = tiles_of((owns[0], [lefts(own) for own in owns]), 0, p_ref, q_ref, scale)
        for d, tile in enumerate(tiles):
            o_ref[lax.rem(target - d + stations, stations), d, 0, :, :] = tile
        return carry

    lax.fori_loop(0, stations, one_target, 0)


def correlate(turned, stations, chans, reach, scale):
    sources, groups, inputs, wide = turned.shape
    block_inputs = chans * inputs
    out_rows = block_inputs * block_inputs // LANES
    return pl.pallas_call(
        functools.partial(correlate_kernel, sizes=(stations, chans, reach, scale)),
        name="correlate",
        grid=(groups,),
        in_specs=[pl.BlockSpec((sources, 1, inputs, wide), lambda g: (0, g, 0, 0))],
        out_specs=pl.BlockSpec((stations, reach, 1, 2 * out_rows, LANES), lambda g: (0, 0, g, 0, 0)),
        out_shape=jax.ShapeDtypeStruct((stations, reach, groups, 2 * out_rows, LANES), bf16),
        scratch_shapes=[
            pltpu.VMEM((1, reach * 2 * block_inputs, LANES), f32),
            pltpu.VMEM((1, reach, 2 * out_rows, LANES), f32),
        ],
    )(turned)


def pieces_kernel(*refs, sizes, pieces):
    blocks, chans, groups, distances, scale, per_step = sizes
    arrived = refs[: len(pieces)]
    outs = refs[len(pieces) : len(pieces) + blocks]
    r_ref, p_ref, q_ref, sems = refs[len(pieces) + blocks :]
    copies = []
    for index, (block, dc, mine, first) in enumerate(pieces):
        chan = lax.rem(lax.axis_index("chan") - dc + chans, chans)
        start = first + lax.axis_index("stn") * mine if mine else first
        copies.append(
            pltpu.make_async_copy(
                arrived[index].at[pl.ds(start, groups)], r_ref.at[block * chans + chan], sems.at[index]
            )
        )
        copies[-1].start()
    for copy in copies:
        copy.wait()

    def some_groups(at, carry):
        for one in range(per_step):
            g = at * per_step + one
            owns = [
                jnp.concatenate([r_ref[block * chans + c, g] for c in range(chans)], axis=0)
                for block in range(blocks)
            ]
            pairs = [lefts(own) for own in owns]
            for target in range(blocks):
                who = [(target - d) % blocks for d in distances]
                tiles = tiles_of(
                    (owns[target], [pairs[b] for b in who]), one * blocks + target, p_ref, q_ref, scale
                )
                for d, (b, tile) in enumerate(zip(who, tiles)):
                    outs[b][d, g, :, :] = tile
        return carry

    lax.fori_loop(0, groups // per_step, some_groups, 0)


def correlate_pieces(arrays, pieces, blocks, chans, groups, distances, scale, stays):
    inputs, wide = arrays[0].shape[1:]
    block_inputs = chans * inputs
    out_rows = block_inputs * block_inputs // LANES
    per_step = math.gcd(groups, 8 // blocks)
    sizes = (blocks, chans, groups, distances, scale, per_step)
    shape = (len(distances), groups, 2 * out_rows, LANES)
    vmem = pl.BlockSpec(memory_space=pltpu.VMEM)
    return pl.pallas_call(
        functools.partial(pieces_kernel, sizes=sizes, pieces=pieces),
        in_specs=[HBM if local else vmem for local in stays],
        out_specs=[vmem] * blocks,
        out_shape=[jax.ShapeDtypeStruct(shape, bf16)] * blocks,
        scratch_shapes=[
            pltpu.VMEM((blocks * chans, groups, inputs, wide), bf16),
            pltpu.VMEM((per_step * blocks, len(distances) * 2 * block_inputs, LANES), f32),
            pltpu.VMEM((per_step * blocks, len(distances), 2 * out_rows, LANES), f32),
            pltpu.SemaphoreType.DMA((len(pieces),)),
        ],
    )(*arrays)


def assemble_kernel(own_ref, *refs, stations, chunks):
    parts = refs[:-1]
    out_ref = refs[-1]
    out_ref[0, :, :, :] = own_ref[0]
    for dz in range(stations):
        host = lax.rem(lax.axis_index("stn") - dz + stations, stations)
        for chunk in range(chunks):
            part = parts[dz * chunks + chunk]
            count = part.shape[1]
            at = (host * chunks + chunk) * count
            for d in range(part.shape[0]):
                out_ref[d + 1, pl.ds(at, count), :, :] = part[d]


def assemble(own, parts, stations, chunks):
    reach = parts[0].shape[0] + 1
    vmem = pl.BlockSpec(memory_space=pltpu.VMEM)
    return pl.pallas_call(
        functools.partial(assemble_kernel, stations=stations, chunks=chunks),
        name="assemble",
        in_specs=[vmem] * (1 + len(parts)),
        out_specs=vmem,
        out_shape=jax.ShapeDtypeStruct((reach,) + own.shape[1:], bf16),
    )(own, *parts)


def shifted(value, stations, chans, dz, dc):
    pairs = [
        (z * chans + c, (z + dz) % stations * chans + (c + dc) % chans)
        for z in range(stations)
        for c in range(chans)
    ]
    return lax.ppermute(value, ("stn", "chan"), pairs)


def local(voltages, taps):
    inputs_here, frames, frame_len = voltages.shape
    spectra_count = frames - taps.shape[0] + 1
    stations = lax.axis_size("stn")
    chans = lax.axis_size("chan")
    reach = stations // 2 + 1
    block_inputs = chans * inputs_here
    pairs = block_inputs * block_inputs
    groups = frame_len // 2 // AVG
    here = groups // (stations * chans)
    scale = 1.0 / (spectra_count * AVG)
    frames_first = voltages.transpose(1, 0, 2)
    if not direct(stations, chans):
        sends = tuple((None, dc, 0, groups // chans) for dc in range(chans))
        slices = make_spectra(frames_first, taps, sends, stations, chans, False)
        send = jnp.concatenate(slices, axis=0).reshape(chans * stations, here, inputs_here, -1)
        turned = lax.all_to_all(send, ("chan", "stn"), 0, 0, tiled=True)
        tiles = correlate(turned, stations, chans, reach, scale)
        back = lax.all_to_all(tiles, "stn", 0, 0, tiled=True)
        out = back.transpose(1, 0, 2, 3, 4)
    else:
        part = here // CHUNKS
        sends = [(None, dc, 0, here * stations) for dc in range(chans)]
        for chunk in range(CHUNKS):
            sends += [(dz, dc, chunk * part, part) for dz in (2, 1, 3)[: stations - 1] for dc in range(chans)]
        sent = make_spectra(frames_first, taps, tuple(sends), stations, chans, True)
        whole, got = [], {}
        for (dz, dc, skip, _), value in zip(sends, sent):
            if dz is None:
                whole.append(shifted(value, stations, chans, 0, dc) if dc else value)
            else:
                got[dz, dc, skip // part] = shifted(value, stations, chans, dz, dc)
        stays = [dc == 0 for dc in range(chans)]
        pieces = [(0, dc, 0, 0) for dc in range(chans)]
        (own,) = correlate_pieces(whole, pieces, 1, chans, here * stations, (0,), scale, stays)
        distances = tuple(range(1, reach))
        back = {}
        for chunk in range(CHUNKS):
            pieces = [(0, dc, here, chunk * part) for dc in range(chans)]
            arrays = list(whole)
            for dz in range(1, stations):
                for dc in range(chans):
                    pieces.append((-dz % stations, dc, 0, 0))
                    arrays.append(got[dz, dc, chunk])
            outs = correlate_pieces(
                arrays, pieces, stations, chans, part, distances, scale, stays + [False] * (len(arrays) - chans)
            )
            for dz in range(stations):
                back[dz, chunk] = outs[0] if dz == 0 else shifted(outs[dz], stations, chans, dz, 0)
        out = assemble(
            own, [back[dz, chunk] for dz in range(stations) for chunk in range(CHUNKS)], stations, CHUNKS
        )
    out = out.reshape(reach, stations * here, pairs // LANES, 2, LANES)
    return out.transpose(0, 1, 3, 2, 4).reshape(1, reach, stations * here, 2, pairs)


CHUNKS = 2


def direct(stations, chans):
    return 2 < stations <= 4 and stations * chans <= 16


def solution(mesh):
    placed = (P(("grp", "stn", "chan"), None, None), P())

    return jax.shard_map(
        local,
        mesh=mesh,
        in_specs=placed,
        out_specs=P(("grp", "stn"), None, "chan", None, None),
        check_vma=False,
    )
```

profile of v0, /device:TPU:0, one launch (start us, length us, event | category | flops | bytes accessed | tf_op | source)
XLA Modules:
  0.0 111.4 jit_solution(13246646517936034975)
XLA Ops:
  0.0 15.5 %spectra.1 = (bf16[64,8,512]{2,1,0:T(8,128)(2,1)}, bf16[64,8,512]{2,1,0:T(8,128)(2,1)}, bf16[64,8,512]{2,1,0:T(8,128)(2,1)}, bf16[64,8,512]{2,1,0:T(8,128)(2,1)}...) custom-call(f32[528,128]{1,0:T(8,128)} %constant.4.clone.tw_ref, ...), custom_call_target="tpu_custom_call" | custom-call | tf_op jit(solution)/shard_map/spectra/pallas_call | solution.py:303
  15.5 3.1 %collective-permute-start.3 = (bf16[8,8,512]{2,1,0:T(8,128)(2,1)}, bf16[8,8,512]{2,1,0:T(8,128)(2,1)S(1)}, u32[]{:S(2)}, u32[]{:S(2)}) collective-permute-start(bf16[8,8,512]{2,1,0:T(8,128)(2,1)} %get-tuple-element.45), channel_id=1, source_target_pairs={{0,4},{1,5},{2,6},{3,7},{4,8},{5,9},{6,10},{7,11},{8,12},{9,13},{1... | collective-permute-start | bytes 196616 | tf_op jit(solution)/shard_map/ppermute | solution.py:480
  18.6 0.7 collective-permute-start.4
  19.3 2.5 %collective-permute-start.5 = (bf16[8,8,512]{2,1,0:T(8,128)(2,1)}, bf16[8,8,512]{2,1,0:T(8,128)(2,1)S(1)}, u32[]{:S(2)}, u32[]{:S(2)}) collective-permute-start(bf16[8,8,512]{2,1,0:T(8,128)(2,1)} %get-tuple-element.47), channel_id=1, source_target_pairs={{0,6},{1,7},{2,4},{3,5},{4,10},{5,11},{6,8},{7,9},{8,14},{9,15},{1... | collective-permute-start | bytes 196616 | tf_op jit(solution)/shard_map/ppermute | solution.py:480
  21.8 1.4 %collective-permute-start.6 = (bf16[8,8,512]{2,1,0:T(8,128)(2,1)}, bf16[8,8,512]{2,1,0:T(8,128)(2,1)S(1)}, u32[]{:S(2)}, u32[]{:S(2)}) collective-permute-start(bf16[8,8,512]{2,1,0:T(8,128)(2,1)} %get-tuple-element.48), channel_id=1, source_target_pairs={{0,7},{1,4},{2,5},{3,6},{4,11},{5,8},{6,9},{7,10},{8,15},{9,12},{1... | collective-permute-start | bytes 196616 | tf_op jit(solution)/shard_map/ppermute | solution.py:480
  23.2 2.6 %collective-permute-start.7 = (bf16[8,8,512]{2,1,0:T(8,128)(2,1)}, bf16[8,8,512]{2,1,0:T(8,128)(2,1)S(1)}, u32[]{:S(2)}, u32[]{:S(2)}) collective-permute-start(bf16[8,8,512]{2,1,0:T(8,128)(2,1)} %get-tuple-element.49), channel_id=1, source_target_pairs={{0,8},{1,9},{2,10},{3,11},{4,12},{5,13},{6,14},{7,15},{8,0},{9,1},... | collective-permute-start | bytes 196616 | tf_op jit(solution)/shard_map/ppermute | solution.py:480
  25.9 0.5 collective-permute-start
  26.4 0.1 collective-permute-done.5.refs_6_
  26.5 2.3 %collective-permute-start.1 = (bf16[64,8,512]{2,1,0:T(8,128)(2,1)}, bf16[64,8,512]{2,1,0:T(8,128)(2,1)S(1)}, u32[]{:S(2)}, u32[]{:S(2)}) collective-permute-start(bf16[64,8,512]{2,1,0:T(8,128)(2,1)} %get-tuple-element.43), channel_id=1, source_target_pairs={{0,2},{1,3},{2,0},{3,1},{4,6},{5,7},{6,4},{7,5},{8,10},{9,11},{10,... | collective-permute-start | bytes 1572872 | tf_op jit(solution)/shard_map/ppermute | solution.py:480
  28.8 1.6 %collective-permute-start.2 = (bf16[64,8,512]{2,1,0:T(8,128)(2,1)}, bf16[64,8,512]{2,1,0:T(8,128)(2,1)S(1)}, u32[]{:S(2)}, u32[]{:S(2)}) collective-permute-start(bf16[64,8,512]{2,1,0:T(8,128)(2,1)} %get-tuple-element.44), channel_id=1, source_target_pairs={{0,3},{1,0},{2,1},{3,2},{4,7},{5,4},{6,5},{7,6},{8,11},{9,8},{10,9... | collective-permute-start | bytes 1572872 | tf_op jit(solution)/shard_map/ppermute | solution.py:480
  30.4 2.5 %collective-permute-done.7.refs_8_ = bf16[8,8,512]{2,1,0:T(8,128)(2,1)S(1)} collective-permute-done((bf16[8,8,512]{2,1,0:T(8,128)(2,1)}, bf16[8,8,512]{2,1,0:T(8,128)(2,1)S(1)}, u32[]{:S(2)}, u32[]{:S(2)}) %collective-permute-start.7) | collective-permute-done | bytes 65568 | tf_op jit(solution)/shard_map/ppermute | solution.py:480
  32.9 1.4 %collective-permute-done.8.refs_9_ = bf16[8,8,512]{2,1,0:T(8,128)(2,1)S(1)} collective-permute-done((bf16[8,8,512]{2,1,0:T(8,128)(2,1)}, bf16[8,8,512]{2,1,0:T(8,128)(2,1)S(1)}, u32[]{:S(2)}, u32[]{:S(2)}) %collective-permute-start.8) | collective-permute-done | bytes 65568 | tf_op jit(solution)/shard_map/ppermute | solution.py:480
  34.4 1.1 collective-permute-start.15
  35.5 3.8 %collective-permute-done.9.refs_10_ = bf16[8,8,512]{2,1,0:T(8,128)(2,1)S(1)} collective-permute-done((bf16[8,8,512]{2,1,0:T(8,128)(2,1)}, bf16[8,8,512]{2,1,0:T(8,128)(2,1)S(1)}, u32[]{:S(2)}, u32[]{:S(2)}) %collective-permute-start.9) | collective-permute-done | bytes 65568 | tf_op jit(solution)/shard_map/ppermute | solution.py:480
  39.3 1.4 %collective-permute-done.15.refs_4_ = bf16[8,8,512]{2,1,0:T(8,128)(2,1)S(1)} collective-permute-done((bf16[8,8,512]{2,1,0:T(8,128)(2,1)}, bf16[8,8,512]{2,1,0:T(8,128)(2,1)S(1)}, u32[]{:S(2)}, u32[]{:S(2)}) %collective-permute-start.15) | collective-permute-done | bytes 65568 | tf_op jit(solution)/shard_map/ppermute | solution.py:480
  40.6 0.0 collective-permute-start.17
  40.7 5.3 %collective-permute-done.16.refs_5_ = bf16[8,8,512]{2,1,0:T(8,128)(2,1)S(1)} collective-permute-done((bf16[8,8,512]{2,1,0:T(8,128)(2,1)}, bf16[8,8,512]{2,1,0:T(8,128)(2,1)S(1)}, u32[]{:S(2)}, u32[]{:S(2)}) %collective-permute-start.16) | collective-permute-done | bytes 65568 | tf_op jit(solution)/shard_map/ppermute | solution.py:480
  46.0 2.0 %collective-permute-done.17.refs_6_ = bf16[8,8,512]{2,1,0:T(8,128)(2,1)S(1)} collective-permute-done((bf16[8,8,512]{2,1,0:T(8,128)(2,1)}, bf16[8,8,512]{2,1,0:T(8,128)(2,1)S(1)}, u32[]{:S(2)}, u32[]{:S(2)}) %collective-permute-start.17) | collective-permute-done | bytes 65568 | tf_op jit(solution)/shard_map/ppermute | solution.py:480
  47.9 4.2 %collective-permute-done.18.refs_7_ = bf16[8,8,512]{2,1,0:T(8,128)(2,1)S(1)} collective-permute-done((bf16[8,8,512]{2,1,0:T(8,128)(2,1)}, bf16[8,8,512]{2,1,0:T(8,128)(2,1)S(1)}, u32[]{:S(2)}, u32[]{:S(2)}) %collective-permute-start.18) | collective-permute-done | bytes 65568 | tf_op jit(solution)/shard_map/ppermute | solution.py:480
  52.1 2.7 %collective-permute-done.19.refs_8_ = bf16[8,8,512]{2,1,0:T(8,128)(2,1)S(1)} collective-permute-done((bf16[8,8,512]{2,1,0:T(8,128)(2,1)}, bf16[8,8,512]{2,1,0:T(8,128)(2,1)S(1)}, u32[]{:S(2)}, u32[]{:S(2)}) %collective-permute-start.19) | collective-permute-done | bytes 65568 | tf_op jit(solution)/shard_map/ppermute | solution.py:480
  54.8 4.4 %collective-permute-done.20.refs_9_ = bf16[8,8,512]{2,1,0:T(8,128)(2,1)S(1)} collective-permute-done((bf16[8,8,512]{2,1,0:T(8,128)(2,1)}, bf16[8,8,512]{2,1,0:T(8,128)(2,1)S(1)}, u32[]{:S(2)}, u32[]{:S(2)}) %collective-permute-start.20) | collective-permute-done | bytes 65568 | tf_op jit(solution)/shard_map/ppermute | solution.py:480
  59.2 3.0 %collective-permute-done.21.refs_10_ = bf16[8,8,512]{2,1,0:T(8,128)(2,1)S(1)} collective-permute-done((bf16[8,8,512]{2,1,0:T(8,128)(2,1)}, bf16[8,8,512]{2,1,0:T(8,128)(2,1)S(1)}, u32[]{:S(2)}, u32[]{:S(2)}) %collective-permute-start.21) | collective-permute-done | bytes 65568 | tf_op jit(solution)/shard_map/ppermute | solution.py:480
  62.2 2.5 %collective-permute-done.22.refs_11_ = bf16[8,8,512]{2,1,0:T(8,128)(2,1)S(1)} collective-permute-done((bf16[8,8,512]{2,1,0:T(8,128)(2,1)}, bf16[8,8,512]{2,1,0:T(8,128)(2,1)S(1)}, u32[]{:S(2)}, u32[]{:S(2)}) %collective-permute-start.22) | collective-permute-done | bytes 65568 | tf_op jit(solution)/shard_map/ppermute | solution.py:480
  64.7 2.0 %collective-permute-done.23.refs_12_ = bf16[8,8,512]{2,1,0:T(8,128)(2,1)S(1)} collective-permute-done((bf16[8,8,512]{2,1,0:T(8,128)(2,1)}, bf16[8,8,512]{2,1,0:T(8,128)(2,1)S(1)}, u32[]{:S(2)}, u32[]{:S(2)}) %collective-permute-start.23) | collective-permute-done | bytes 65568 | tf_op jit(solution)/shard_map/ppermute | solution.py:480
  66.7 1.2 %collective-permute-start.25 = (bf16[8,8,512]{2,1,0:T(8,128)(2,1)}, bf16[8,8,512]{2,1,0:T(8,128)(2,1)S(1)}, u32[]{:S(2)}, u32[]{:S(2)}) collective-permute-start(bf16[8,8,512]{2,1,0:T(8,128)(2,1)} %get-tuple-element.68), channel_id=1, source_target_pairs={{0,14},{1,15},{2,12},{3,13},{4,2},{5,3},{6,0},{7,1},{8,6},{9,7},{1... | collective-permute-start | bytes 196616 | tf_op jit(solution)/shard_map/ppermute | solution.py:480
  67.9 1.6 %collective-permute-done.24.refs_13_ = bf16[8,8,512]{2,1,0:T(8,128)(2,1)S(1)} collective-permute-done((bf16[8,8,512]{2,1,0:T(8,128)(2,1)}, bf16[8,8,512]{2,1,0:T(8,128)(2,1)S(1)}, u32[]{:S(2)}, u32[]{:S(2)}) %collective-permute-start.24) | collective-permute-done | bytes 65568 | tf_op jit(solution)/shard_map/ppermute | solution.py:480
  69.5 1.4 %collective-permute-start.26 = (bf16[8,8,512]{2,1,0:T(8,128)(2,1)}, bf16[8,8,512]{2,1,0:T(8,128)(2,1)S(1)}, u32[]{:S(2)}, u32[]{:S(2)}) collective-permute-start(bf16[8,8,512]{2,1,0:T(8,128)(2,1)} %get-tuple-element.69), channel_id=1, source_target_pairs={{0,15},{1,12},{2,13},{3,14},{4,3},{5,0},{6,1},{7,2},{8,7},{9,4},{1... | collective-permute-start | bytes 196616 | tf_op jit(solution)/shard_map/ppermute | solution.py:480
  70.9 1.2 %collective-permute-done.25.refs_14_ = bf16[8,8,512]{2,1,0:T(8,128)(2,1)S(1)} collective-permute-done((bf16[8,8,512]{2,1,0:T(8,128)(2,1)}, bf16[8,8,512]{2,1,0:T(8,128)(2,1)S(1)}, u32[]{:S(2)}, u32[]{:S(2)}) %collective-permute-start.25) | collective-permute-done | bytes 65568 | tf_op jit(solution)/shard_map/ppermute | solution.py:480
  72.1 1.3 %collective-permute-done.26.refs_15_ = bf16[8,8,512]{2,1,0:T(8,128)(2,1)S(1)} collective-permute-done((bf16[8,8,512]{2,1,0:T(8,128)(2,1)}, bf16[8,8,512]{2,1,0:T(8,128)(2,1)S(1)}, u32[]{:S(2)}, u32[]{:S(2)}) %collective-permute-start.26) | collective-permute-done | bytes 65568 | tf_op jit(solution)/shard_map/ppermute | solution.py:480
  73.4 2.9 %collective-permute-start.11 = (bf16[8,8,512]{2,1,0:T(8,128)(2,1)}, bf16[8,8,512]{2,1,0:T(8,128)(2,1)S(1)}, u32[]{:S(2)}, u32[]{:S(2)}) collective-permute-start(bf16[8,8,512]{2,1,0:T(8,128)(2,1)} %get-tuple-element.53), channel_id=1, source_target_pairs={{0,12},{1,13},{2,14},{3,15},{4,0},{5,1},{6,2},{7,3},{8,4},{9,5},{1... | collective-permute-start | bytes 196616 | tf_op jit(solution)/shard_map/ppermute | solution.py:480
  76.3 0.9 collective-permute-start.12
  77.2 0.8 collective-permute-start.13
  78.0 1.9 %collective-permute-start.14 = (bf16[8,8,512]{2,1,0:T(8,128)(2,1)}, bf16[8,8,512]{2,1,0:T(8,128)(2,1)S(1)}, u32[]{:S(2)}, u32[]{:S(2)}) collective-permute-start(bf16[8,8,512]{2,1,0:T(8,128)(2,1)} %get-tuple-element.56), channel_id=1, source_target_pairs={{0,15},{1,12},{2,13},{3,14},{4,3},{5,0},{6,1},{7,2},{8,7},{9,4},{1... | collective-permute-start | bytes 196616 | tf_op jit(solution)/shard_map/ppermute | solution.py:480
  80.0 5.6 %shard_map.48 = (bf16[2,8,16,128]{3,2,1,0:T(8,128)(2,1)}, bf16[2,8,16,128]{3,2,1,0:T(8,128)(2,1)}, bf16[2,8,16,128]{3,2,1,0:T(8,128)(2,1)}, bf16[2,8,16,128]{3,2,1,0:T(8,128)(2,1)}) custom-call(bf16[64,8,512]{2,1,0:T(8,128)(2,1)} %get-tuple-element.41.refs_0_, bf16[64,8,512]{2,1,0:T(8,128)(2,1)} %copy-done, bf16[64,8,512]{2,1,0:T(8,128)(2,1)} %copy-done.1, ...), custom_call_target="tpu_custom_call" | custom-call | tf_op jit(solution)/shard_map/pallas_call | solution.py:434
  85.6 0.7 collective-permute-start.28
  86.3 1.7 %collective-permute-start.30 = (bf16[2,8,16,128]{3,2,1,0:T(8,128)(2,1)}, bf16[2,8,16,128]{3,2,1,0:T(8,128)(2,1)S(1)}, u32[]{:S(2)}, u32[]{:S(2)}) collective-permute-start(bf16[2,8,16,128]{3,2,1,0:T(8,128)(2,1)} %get-tuple-element.74), channel_id=1, source_target_pairs={{0,8},{1,9},{2,10},{3,11},{4,12},{5,13},{6,14},{7,15},{8,0},{9,1},... | collective-permute-start | bytes 196616 | tf_op jit(solution)/shard_map/ppermute | solution.py:480
  88.1 2.3 %collective-permute-start.32 = (bf16[2,8,16,128]{3,2,1,0:T(8,128)(2,1)}, bf16[2,8,16,128]{3,2,1,0:T(8,128)(2,1)S(1)}, u32[]{:S(2)}, u32[]{:S(2)}) collective-permute-start(bf16[2,8,16,128]{3,2,1,0:T(8,128)(2,1)} %get-tuple-element.76), channel_id=1, source_target_pairs={{0,12},{1,13},{2,14},{3,15},{4,0},{5,1},{6,2},{7,3},{8,4},{9,5},{1... | collective-permute-start | bytes 196616 | tf_op jit(solution)/shard_map/ppermute | solution.py:480
  90.5 0.5 copy-done.24
  91.0 0.6 copy-done.27
  91.6 5.6 %shard_map.47 = (bf16[2,8,16,128]{3,2,1,0:T(8,128)(2,1)}, bf16[2,8,16,128]{3,2,1,0:T(8,128)(2,1)}, bf16[2,8,16,128]{3,2,1,0:T(8,128)(2,1)}, bf16[2,8,16,128]{3,2,1,0:T(8,128)(2,1)}) custom-call(bf16[64,8,512]{2,1,0:T(8,128)(2,1)} %get-tuple-element.41.refs_0_, bf16[64,8,512]{2,1,0:T(8,128)(2,1)} %copy-done, bf16[64,8,512]{2,1,0:T(8,128)(2,1)} %copy-done.1, ...), custom_call_target="tpu_custom_call" | custom-call | tf_op jit(solution)/shard_map/pallas_call | solution.py:434
  97.2 0.1 collective-permute-start.27
  97.3 1.3 %collective-permute-start.29 = (bf16[2,8,16,128]{3,2,1,0:T(8,128)(2,1)}, bf16[2,8,16,128]{3,2,1,0:T(8,128)(2,1)S(1)}, u32[]{:S(2)}, u32[]{:S(2)}) collective-permute-start(bf16[2,8,16,128]{3,2,1,0:T(8,128)(2,1)} %get-tuple-element.73), channel_id=1, source_target_pairs={{0,8},{1,9},{2,10},{3,11},{4,12},{5,13},{6,14},{7,15},{8,0},{9,1},... | collective-permute-start | bytes 196616 | tf_op jit(solution)/shard_map/ppermute | solution.py:480
  98.5 2.8 %collective-permute-start.31 = (bf16[2,8,16,128]{3,2,1,0:T(8,128)(2,1)}, bf16[2,8,16,128]{3,2,1,0:T(8,128)(2,1)S(1)}, u32[]{:S(2)}, u32[]{:S(2)}) collective-permute-start(bf16[2,8,16,128]{3,2,1,0:T(8,128)(2,1)} %get-tuple-element.75), channel_id=1, source_target_pairs={{0,12},{1,13},{2,14},{3,15},{4,0},{5,1},{6,2},{7,3},{8,4},{9,5},{1... | collective-permute-start | bytes 196616 | tf_op jit(solution)/shard_map/ppermute | solution.py:480
  101.4 7.1 %shard_map.46.own_ref = bf16[1,64,16,128]{3,2,1,0:T(8,128)(2,1)} custom-call(bf16[64,8,512]{2,1,0:T(8,128)(2,1)} %get-tuple-element.41.refs_0_, bf16[64,8,512]{2,1,0:T(8,128)(2,1)} %copy-done, bf16[64,8,512]{2,1,0:T(8,128)(2,1)} %copy-done.1, bf16[64,8,512]{2,1,0:T(8,128)(2,1)} %copy-done.2), custom_call_target="tpu_custom_call" | custom-call | tf_op jit(solution)/shard_map/pallas_call | solution.py:434
  108.7 0.5 copy-done.22
  109.2 0.1 copy-done.25
  109.3 0.0 copy-done.32
  109.3 2.0 %assemble.1 = bf16[3,64,16,128]{3,2,1,0:T(8,128)(2,1)} custom-call(bf16[1,64,16,128]{3,2,1,0:T(8,128)(2,1)} %shard_map.46.own_ref, bf16[2,8,16,128]{3,2,1,0:T(8,128)(2,1)} %get-tuple-element.57.refs_0_, bf16[2,8,16,128]{3,2,1,0:T(8,128)(2,1)} %get-tuple-element.70.refs_1_, bf16[2,8,16,128]{3,2,1,0:T(8,128)(2,1)} %copy-done.30, ...), custom_call_target="tpu_custom_call" | custom-call | tf_op jit(solution)/shard_map/assemble/pallas_call | solution.py:465
  (89 shorter events, 0.2 us)
Async XLA Ops:
  15.5 10.3 %collective-permute-start.3 = (bf16[8,8,512]{2,1,0:T(8,128)(2,1)}, bf16[8,8,512]{2,1,0:T(8,128)(2,1)S(1)}, u32[]{:S(2)}, u32[]{:S(2)}) collective-permute-start(bf16[8,8,512]{2,1,0:T(8,128)(2,1)} %get-tuple-element.45), channel_id=1, source_target_pairs={{0,4},{1,5},{2,6},{3,7},{4,8},{5,9},{6,10},{7,11},{8,12},{9,13},{1... | collective-permute-start | bytes 196616 | tf_op jit(solution)/shard_map/ppermute | solution.py:480
  18.6 7.2 %collective-permute-start.4 = (bf16[8,8,512]{2,1,0:T(8,128)(2,1)}, bf16[8,8,512]{2,1,0:T(8,128)(2,1)S(1)}, u32[]{:S(2)}, u32[]{:S(2)}) collective-permute-start(bf16[8,8,512]{2,1,0:T(8,128)(2,1)} %get-tuple-element.46), channel_id=1, source_target_pairs={{0,5},{1,6},{2,7},{3,4},{4,9},{5,10},{6,11},{7,8},{8,13},{9,14},{1... | collective-permute-start | bytes 196616 | tf_op jit(solution)/shard_map/ppermute | solution.py:480
  19.3 7.2 %collective-permute-start.5 = (bf16[8,8,512]{2,1,0:T(8,128)(2,1)}, bf16[8,8,512]{2,1,0:T(8,128)(2,1)S(1)}, u32[]{:S(2)}, u32[]{:S(2)}) collective-permute-start(bf16[8,8,512]{2,1,0:T(8,128)(2,1)} %get-tuple-element.47), channel_id=1, source_target_pairs={{0,6},{1,7},{2,4},{3,5},{4,10},{5,11},{6,8},{7,9},{8,14},{9,15},{1... | collective-permute-start | bytes 196616 | tf_op jit(solution)/shard_map/ppermute | solution.py:480
  21.8 6.9 %collective-permute-start.6 = (bf16[8,8,512]{2,1,0:T(8,128)(2,1)}, bf16[8,8,512]{2,1,0:T(8,128)(2,1)S(1)}, u32[]{:S(2)}, u32[]{:S(2)}) collective-permute-start(bf16[8,8,512]{2,1,0:T(8,128)(2,1)} %get-tuple-element.48), channel_id=1, source_target_pairs={{0,7},{1,4},{2,5},{3,6},{4,11},{5,8},{6,9},{7,10},{8,15},{9,12},{1... | collective-permute-start | bytes 196616 | tf_op jit(solution)/shard_map/ppermute | solution.py:480
  23.2 9.7 %collective-permute-start.7 = (bf16[8,8,512]{2,1,0:T(8,128)(2,1)}, bf16[8,8,512]{2,1,0:T(8,128)(2,1)S(1)}, u32[]{:S(2)}, u32[]{:S(2)}) collective-permute-start(bf16[8,8,512]{2,1,0:T(8,128)(2,1)} %get-tuple-element.49), channel_id=1, source_target_pairs={{0,8},{1,9},{2,10},{3,11},{4,12},{5,13},{6,14},{7,15},{8,0},{9,1},... | collective-permute-start | bytes 196616 | tf_op jit(solution)/shard_map/ppermute | solution.py:480
  25.8 64.5 %copy-start.3 = (bf16[8,8,512]{2,1,0:T(8,128)(2,1)}, bf16[8,8,512]{2,1,0:T(8,128)(2,1)S(1)}, u32[]{:S(2)}) copy-start(bf16[8,8,512]{2,1,0:T(8,128)(2,1)S(1)} %collective-permute-done.3.refs_4_) | copy-start | bytes 196612
  25.8 8.5 %collective-permute-start.8 = (bf16[8,8,512]{2,1,0:T(8,128)(2,1)}, bf16[8,8,512]{2,1,0:T(8,128)(2,1)S(1)}, u32[]{:S(2)}, u32[]{:S(2)}) collective-permute-start(bf16[8,8,512]{2,1,0:T(8,128)(2,1)} %get-tuple-element.50), channel_id=1, source_target_pairs={{0,9},{1,10},{2,11},{3,8},{4,13},{5,14},{6,15},{7,12},{8,1},{9,2},... | collective-permute-start | bytes 196616 | tf_op jit(solution)/shard_map/ppermute | solution.py:480
  25.9 64.5 %copy-start.4 = (bf16[8,8,512]{2,1,0:T(8,128)(2,1)}, bf16[8,8,512]{2,1,0:T(8,128)(2,1)S(1)}, u32[]{:S(2)}) copy-start(bf16[8,8,512]{2,1,0:T(8,128)(2,1)S(1)} %collective-permute-done.4.refs_5_) | copy-start | bytes 196612
  25.9 50.5 %collective-permute-start = (bf16[64,8,512]{2,1,0:T(8,128)(2,1)}, bf16[64,8,512]{2,1,0:T(8,128)(2,1)S(1)}, u32[]{:S(2)}, u32[]{:S(2)}) collective-permute-start(bf16[64,8,512]{2,1,0:T(8,128)(2,1)} %get-tuple-element.42), channel_id=1, source_target_pairs={{0,1},{1,2},{2,3},{3,0},{4,5},{5,6},{6,7},{7,4},{8,9},{9,10},{10,1... | collective-permute-start | bytes 1572872 | tf_op jit(solution)/shard_map/ppermute | solution.py:480
  26.5 63.9 %copy-start.5 = (bf16[8,8,512]{2,1,0:T(8,128)(2,1)}, bf16[8,8,512]{2,1,0:T(8,128)(2,1)S(1)}, u32[]{:S(2)}) copy-start(bf16[8,8,512]{2,1,0:T(8,128)(2,1)S(1)} %collective-permute-done.5.refs_6_) | copy-start | bytes 196612
  26.5 50.7 %collective-permute-start.1 = (bf16[64,8,512]{2,1,0:T(8,128)(2,1)}, bf16[64,8,512]{2,1,0:T(8,128)(2,1)S(1)}, u32[]{:S(2)}, u32[]{:S(2)}) collective-permute-start(bf16[64,8,512]{2,1,0:T(8,128)(2,1)} %get-tuple-element.43), channel_id=1, source_target_pairs={{0,2},{1,3},{2,0},{3,1},{4,6},{5,7},{6,4},{7,5},{8,10},{9,11},{10,... | collective-permute-start | bytes 1572872 | tf_op jit(solution)/shard_map/ppermute | solution.py:480
  28.8 61.6 %copy-start.6 = (bf16[8,8,512]{2,1,0:T(8,128)(2,1)}, bf16[8,8,512]{2,1,0:T(8,128)(2,1)S(1)}, u32[]{:S(2)}) copy-start(bf16[8,8,512]{2,1,0:T(8,128)(2,1)S(1)} %collective-permute-done.6.refs_7_) | copy-start | bytes 196612
  28.8 49.2 %collective-permute-start.2 = (bf16[64,8,512]{2,1,0:T(8,128)(2,1)}, bf16[64,8,512]{2,1,0:T(8,128)(2,1)S(1)}, u32[]{:S(2)}, u32[]{:S(2)}) collective-permute-start(bf16[64,8,512]{2,1,0:T(8,128)(2,1)} %get-tuple-element.44), channel_id=1, source_target_pairs={{0,3},{1,0},{2,1},{3,2},{4,7},{5,4},{6,5},{7,6},{8,11},{9,8},{10,9... | collective-permute-start | bytes 1572872 | tf_op jit(solution)/shard_map/ppermute | solution.py:480
  32.9 57.5 %copy-start.7 = (bf16[8,8,512]{2,1,0:T(8,128)(2,1)}, bf16[8,8,512]{2,1,0:T(8,128)(2,1)S(1)}, u32[]{:S(2)}) copy-start(bf16[8,8,512]{2,1,0:T(8,128)(2,1)S(1)} %collective-permute-done.7.refs_8_) | copy-start | bytes 196612
  32.9 6.3 %collective-permute-start.9 = (bf16[8,8,512]{2,1,0:T(8,128)(2,1)}, bf16[8,8,512]{2,1,0:T(8,128)(2,1)S(1)}, u32[]{:S(2)}, u32[]{:S(2)}) collective-permute-start(bf16[8,8,512]{2,1,0:T(8,128)(2,1)} %get-tuple-element.51), channel_id=1, source_target_pairs={{0,10},{1,11},{2,8},{3,9},{4,14},{5,15},{6,12},{7,13},{8,2},{9,3},... | collective-permute-start | bytes 196616 | tf_op jit(solution)/shard_map/ppermute | solution.py:480
  34.4 56.1 %copy-start.8 = (bf16[8,8,512]{2,1,0:T(8,128)(2,1)}, bf16[8,8,512]{2,1,0:T(8,128)(2,1)S(1)}, u32[]{:S(2)}) copy-start(bf16[8,8,512]{2,1,0:T(8,128)(2,1)S(1)} %collective-permute-done.8.refs_9_) | copy-start | bytes 196612
  34.4 6.3 %collective-permute-start.15 = (bf16[8,8,512]{2,1,0:T(8,128)(2,1)}, bf16[8,8,512]{2,1,0:T(8,128)(2,1)S(1)}, u32[]{:S(2)}, u32[]{:S(2)}) collective-permute-start(bf16[8,8,512]{2,1,0:T(8,128)(2,1)} %get-tuple-element.58), channel_id=1, source_target_pairs={{0,4},{1,5},{2,6},{3,7},{4,8},{5,9},{6,10},{7,11},{8,12},{9,13},{1... | collective-permute-start | bytes 196616 | tf_op jit(solution)/shard_map/ppermute | solution.py:480
  39.3 51.2 %copy-start.9 = (bf16[8,8,512]{2,1,0:T(8,128)(2,1)}, bf16[8,8,512]{2,1,0:T(8,128)(2,1)S(1)}, u32[]{:S(2)}) copy-start(bf16[8,8,512]{2,1,0:T(8,128)(2,1)S(1)} %collective-permute-done.9.refs_10_) | copy-start | bytes 196612
  39.3 6.7 %collective-permute-start.16 = (bf16[8,8,512]{2,1,0:T(8,128)(2,1)}, bf16[8,8,512]{2,1,0:T(8,128)(2,1)S(1)}, u32[]{:S(2)}, u32[]{:S(2)}) collective-permute-start(bf16[8,8,512]{2,1,0:T(8,128)(2,1)} %get-tuple-element.59), channel_id=1, source_target_pairs={{0,5},{1,6},{2,7},{3,4},{4,9},{5,10},{6,11},{7,8},{8,13},{9,14},{1... | collective-permute-start | bytes 196616 | tf_op jit(solution)/shard_map/ppermute | solution.py:480
  40.6 39.3 %copy-start.10 = (bf16[8,8,512]{2,1,0:T(8,128)(2,1)}, bf16[8,8,512]{2,1,0:T(8,128)(2,1)S(1)}, u32[]{:S(2)}) copy-start(bf16[8,8,512]{2,1,0:T(8,128)(2,1)S(1)} %collective-permute-done.15.refs_4_) | copy-start | bytes 196612
  40.6 7.3 %collective-permute-start.17 = (bf16[8,8,512]{2,1,0:T(8,128)(2,1)}, bf16[8,8,512]{2,1,0:T(8,128)(2,1)S(1)}, u32[]{:S(2)}, u32[]{:S(2)}) collective-permute-start(bf16[8,8,512]{2,1,0:T(8,128)(2,1)} %get-tuple-element.60), channel_id=1, source_target_pairs={{0,6},{1,7},{2,4},{3,5},{4,10},{5,11},{6,8},{7,9},{8,14},{9,15},{1... | collective-permute-start | bytes 196616 | tf_op jit(solution)/shard_map/ppermute | solution.py:480
  46.0 33.9 %copy-start.11 = (bf16[8,8,512]{2,1,0:T(8,128)(2,1)}, bf16[8,8,512]{2,1,0:T(8,128)(2,1)S(1)}, u32[]{:S(2)}) copy-start(bf16[8,8,512]{2,1,0:T(8,128)(2,1)S(1)} %collective-permute-done.16.refs_5_) | copy-start | bytes 196612
  46.0 6.2 %collective-permute-start.18 = (bf16[8,8,512]{2,1,0:T(8,128)(2,1)}, bf16[8,8,512]{2,1,0:T(8,128)(2,1)S(1)}, u32[]{:S(2)}, u32[]{:S(2)}) collective-permute-start(bf16[8,8,512]{2,1,0:T(8,128)(2,1)} %get-tuple-element.61), channel_id=1, source_target_pairs={{0,7},{1,4},{2,5},{3,6},{4,11},{5,8},{6,9},{7,10},{8,15},{9,12},{1... | collective-permute-start | bytes 196616 | tf_op jit(solution)/shard_map/ppermute | solution.py:480
  47.9 32.0 %copy-start.12 = (bf16[8,8,512]{2,1,0:T(8,128)(2,1)}, bf16[8,8,512]{2,1,0:T(8,128)(2,1)S(1)}, u32[]{:S(2)}) copy-start(bf16[8,8,512]{2,1,0:T(8,128)(2,1)S(1)} %collective-permute-done.17.refs_6_) | copy-start | bytes 196612
  47.9 6.9 %collective-permute-start.19 = (bf16[8,8,512]{2,1,0:T(8,128)(2,1)}, bf16[8,8,512]{2,1,0:T(8,128)(2,1)S(1)}, u32[]{:S(2)}, u32[]{:S(2)}) collective-permute-start(bf16[8,8,512]{2,1,0:T(8,128)(2,1)} %get-tuple-element.62), channel_id=1, source_target_pairs={{0,8},{1,9},{2,10},{3,11},{4,12},{5,13},{6,14},{7,15},{8,0},{9,1},... | collective-permute-start | bytes 196616 | tf_op jit(solution)/shard_map/ppermute | solution.py:480
  52.1 27.8 %copy-start.13 = (bf16[8,8,512]{2,1,0:T(8,128)(2,1)}, bf16[8,8,512]{2,1,0:T(8,128)(2,1)S(1)}, u32[]{:S(2)}) copy-start(bf16[8,8,512]{2,1,0:T(8,128)(2,1)S(1)} %collective-permute-done.18.refs_7_) | copy-start | bytes 196612
  52.1 7.1 %collective-permute-start.20 = (bf16[8,8,512]{2,1,0:T(8,128)(2,1)}, bf16[8,8,512]{2,1,0:T(8,128)(2,1)S(1)}, u32[]{:S(2)}, u32[]{:S(2)}) collective-permute-start(bf16[8,8,512]{2,1,0:T(8,128)(2,1)} %get-tuple-element.63), channel_id=1, source_target_pairs={{0,9},{1,10},{2,11},{3,8},{4,13},{5,14},{6,15},{7,12},{8,1},{9,2},... | collective-permute-start | bytes 196616 | tf_op jit(solution)/shard_map/ppermute | solution.py:480
  54.8 25.1 %copy-start.14 = (bf16[8,8,512]{2,1,0:T(8,128)(2,1)}, bf16[8,8,512]{2,1,0:T(8,128)(2,1)S(1)}, u32[]{:S(2)}) copy-start(bf16[8,8,512]{2,1,0:T(8,128)(2,1)S(1)} %collective-permute-done.19.refs_8_) | copy-start | bytes 196612
  54.8 7.4 %collective-permute-start.21 = (bf16[8,8,512]{2,1,0:T(8,128)(2,1)}, bf16[8,8,512]{2,1,0:T(8,128)(2,1)S(1)}, u32[]{:S(2)}, u32[]{:S(2)}) collective-permute-start(bf16[8,8,512]{2,1,0:T(8,128)(2,1)} %get-tuple-element.64), channel_id=1, source_target_pairs={{0,10},{1,11},{2,8},{3,9},{4,14},{5,15},{6,12},{7,13},{8,2},{9,3},... | collective-permute-start | bytes 196616 | tf_op jit(solution)/shard_map/ppermute | solution.py:480
  59.2 20.7 %copy-start.15 = (bf16[8,8,512]{2,1,0:T(8,128)(2,1)}, bf16[8,8,512]{2,1,0:T(8,128)(2,1)S(1)}, u32[]{:S(2)}) copy-start(bf16[8,8,512]{2,1,0:T(8,128)(2,1)S(1)} %collective-permute-done.20.refs_9_) | copy-start | bytes 196612
  59.2 5.4 %collective-permute-start.22 = (bf16[8,8,512]{2,1,0:T(8,128)(2,1)}, bf16[8,8,512]{2,1,0:T(8,128)(2,1)S(1)}, u32[]{:S(2)}, u32[]{:S(2)}) collective-permute-start(bf16[8,8,512]{2,1,0:T(8,128)(2,1)} %get-tuple-element.65), channel_id=1, source_target_pairs={{0,11},{1,8},{2,9},{3,10},{4,15},{5,12},{6,13},{7,14},{8,3},{9,0},... | collective-permute-start | bytes 196616 | tf_op jit(solution)/shard_map/ppermute | solution.py:480
  62.2 17.7 %copy-start.17 = (bf16[8,8,512]{2,1,0:T(8,128)(2,1)}, bf16[8,8,512]{2,1,0:T(8,128)(2,1)S(1)}, u32[]{:S(2)}) copy-start(bf16[8,8,512]{2,1,0:T(8,128)(2,1)S(1)} %collective-permute-done.21.refs_10_) | copy-start | bytes 196612
  62.2 4.5 %collective-permute-start.23 = (bf16[8,8,512]{2,1,0:T(8,128)(2,1)}, bf16[8,8,512]{2,1,0:T(8,128)(2,1)S(1)}, u32[]{:S(2)}, u32[]{:S(2)}) collective-permute-start(bf16[8,8,512]{2,1,0:T(8,128)(2,1)} %get-tuple-element.66), channel_id=1, source_target_pairs={{0,12},{1,13},{2,14},{3,15},{4,0},{5,1},{6,2},{7,3},{8,4},{9,5},{1... | collective-permute-start | bytes 196616 | tf_op jit(solution)/shard_map/ppermute | solution.py:480
  64.7 15.3 %copy-start.20 = (bf16[8,8,512]{2,1,0:T(8,128)(2,1)}, bf16[8,8,512]{2,1,0:T(8,128)(2,1)S(1)}, u32[]{:S(2)}) copy-start(bf16[8,8,512]{2,1,0:T(8,128)(2,1)S(1)} %collective-permute-done.22.refs_11_) | copy-start | bytes 196612
  64.7 4.8 %collective-permute-start.24 = (bf16[8,8,512]{2,1,0:T(8,128)(2,1)}, bf16[8,8,512]{2,1,0:T(8,128)(2,1)S(1)}, u32[]{:S(2)}, u32[]{:S(2)}) collective-permute-start(bf16[8,8,512]{2,1,0:T(8,128)(2,1)} %get-tuple-element.67), channel_id=1, source_target_pairs={{0,13},{1,14},{2,15},{3,12},{4,1},{5,2},{6,3},{7,0},{8,5},{9,6},{1... | collective-permute-start | bytes 196616 | tf_op jit(solution)/shard_map/ppermute | solution.py:480
  66.7 5.4 %collective-permute-start.25 = (bf16[8,8,512]{2,1,0:T(8,128)(2,1)}, bf16[8,8,512]{2,1,0:T(8,128)(2,1)S(1)}, u32[]{:S(2)}, u32[]{:S(2)}) collective-permute-start(bf16[8,8,512]{2,1,0:T(8,128)(2,1)} %get-tuple-element.68), channel_id=1, source_target_pairs={{0,14},{1,15},{2,12},{3,13},{4,2},{5,3},{6,0},{7,1},{8,6},{9,7},{1... | collective-permute-start | bytes 196616 | tf_op jit(solution)/shard_map/ppermute | solution.py:480
  69.5 3.9 %collective-permute-start.26 = (bf16[8,8,512]{2,1,0:T(8,128)(2,1)}, bf16[8,8,512]{2,1,0:T(8,128)(2,1)S(1)}, u32[]{:S(2)}, u32[]{:S(2)}) collective-permute-start(bf16[8,8,512]{2,1,0:T(8,128)(2,1)} %get-tuple-element.69), channel_id=1, source_target_pairs={{0,15},{1,12},{2,13},{3,14},{4,3},{5,0},{6,1},{7,2},{8,7},{9,4},{1... | collective-permute-start | bytes 196616 | tf_op jit(solution)/shard_map/ppermute | solution.py:480
  72.1 13.6 %collective-permute-start.10 = (bf16[8,8,512]{2,1,0:T(8,128)(2,1)}, bf16[8,8,512]{2,1,0:T(8,128)(2,1)S(1)}, u32[]{:S(2)}, u32[]{:S(2)}) collective-permute-start(bf16[8,8,512]{2,1,0:T(8,128)(2,1)} %get-tuple-element.52), channel_id=1, source_target_pairs={{0,11},{1,8},{2,9},{3,10},{4,15},{5,12},{6,13},{7,14},{8,3},{9,0},... | collective-permute-start | bytes 196616 | tf_op jit(solution)/shard_map/ppermute | solution.py:480
  73.4 12.9 %collective-permute-start.11 = (bf16[8,8,512]{2,1,0:T(8,128)(2,1)}, bf16[8,8,512]{2,1,0:T(8,128)(2,1)S(1)}, u32[]{:S(2)}, u32[]{:S(2)}) collective-permute-start(bf16[8,8,512]{2,1,0:T(8,128)(2,1)} %get-tuple-element.53), channel_id=1, source_target_pairs={{0,12},{1,13},{2,14},{3,15},{4,0},{5,1},{6,2},{7,3},{8,4},{9,5},{1... | collective-permute-start | bytes 196616 | tf_op jit(solution)/shard_map/ppermute | solution.py:480
  76.3 11.7 %collective-permute-start.12 = (bf16[8,8,512]{2,1,0:T(8,128)(2,1)}, bf16[8,8,512]{2,1,0:T(8,128)(2,1)S(1)}, u32[]{:S(2)}, u32[]{:S(2)}) collective-permute-start(bf16[8,8,512]{2,1,0:T(8,128)(2,1)} %get-tuple-element.54), channel_id=1, source_target_pairs={{0,13},{1,14},{2,15},{3,12},{4,1},{5,2},{6,3},{7,0},{8,5},{9,6},{1... | collective-permute-start | bytes 196616 | tf_op jit(solution)/shard_map/ppermute | solution.py:480
  77.2 13.2 %collective-permute-start.13 = (bf16[8,8,512]{2,1,0:T(8,128)(2,1)}, bf16[8,8,512]{2,1,0:T(8,128)(2,1)S(1)}, u32[]{:S(2)}, u32[]{:S(2)}) collective-permute-start(bf16[8,8,512]{2,1,0:T(8,128)(2,1)} %get-tuple-element.55), channel_id=1, source_target_pairs={{0,14},{1,15},{2,12},{3,13},{4,2},{5,3},{6,0},{7,1},{8,6},{9,7},{1... | collective-permute-start | bytes 196616 | tf_op jit(solution)/shard_map/ppermute | solution.py:480
  78.0 12.4 %collective-permute-start.14 = (bf16[8,8,512]{2,1,0:T(8,128)(2,1)}, bf16[8,8,512]{2,1,0:T(8,128)(2,1)S(1)}, u32[]{:S(2)}, u32[]{:S(2)}) collective-permute-start(bf16[8,8,512]{2,1,0:T(8,128)(2,1)} %get-tuple-element.56), channel_id=1, source_target_pairs={{0,15},{1,12},{2,13},{3,14},{4,3},{5,0},{6,1},{7,2},{8,7},{9,4},{1... | collective-permute-start | bytes 196616 | tf_op jit(solution)/shard_map/ppermute | solution.py:480
  85.6 12.9 %collective-permute-start.28 = (bf16[2,8,16,128]{3,2,1,0:T(8,128)(2,1)}, bf16[2,8,16,128]{3,2,1,0:T(8,128)(2,1)S(1)}, u32[]{:S(2)}, u32[]{:S(2)}) collective-permute-start(bf16[2,8,16,128]{3,2,1,0:T(8,128)(2,1)} %get-tuple-element.72), channel_id=1, source_target_pairs={{0,4},{1,5},{2,6},{3,7},{4,8},{5,9},{6,10},{7,11},{8,12},{9,13},{1... | collective-permute-start | bytes 196616 | tf_op jit(solution)/shard_map/ppermute | solution.py:480
  86.3 22.2 %collective-permute-start.30 = (bf16[2,8,16,128]{3,2,1,0:T(8,128)(2,1)}, bf16[2,8,16,128]{3,2,1,0:T(8,128)(2,1)S(1)}, u32[]{:S(2)}, u32[]{:S(2)}) collective-permute-start(bf16[2,8,16,128]{3,2,1,0:T(8,128)(2,1)} %get-tuple-element.74), channel_id=1, source_target_pairs={{0,8},{1,9},{2,10},{3,11},{4,12},{5,13},{6,14},{7,15},{8,0},{9,1},... | collective-permute-start | bytes 196616 | tf_op jit(solution)/shard_map/ppermute | solution.py:480
  88.1 20.5 %collective-permute-start.32 = (bf16[2,8,16,128]{3,2,1,0:T(8,128)(2,1)}, bf16[2,8,16,128]{3,2,1,0:T(8,128)(2,1)S(1)}, u32[]{:S(2)}, u32[]{:S(2)}) collective-permute-start(bf16[2,8,16,128]{3,2,1,0:T(8,128)(2,1)} %get-tuple-element.76), channel_id=1, source_target_pairs={{0,12},{1,13},{2,14},{3,15},{4,0},{5,1},{6,2},{7,3},{8,4},{9,5},{1... | collective-permute-start | bytes 196616 | tf_op jit(solution)/shard_map/ppermute | solution.py:480
  97.2 11.4 %collective-permute-start.27 = (bf16[2,8,16,128]{3,2,1,0:T(8,128)(2,1)}, bf16[2,8,16,128]{3,2,1,0:T(8,128)(2,1)S(1)}, u32[]{:S(2)}, u32[]{:S(2)}) collective-permute-start(bf16[2,8,16,128]{3,2,1,0:T(8,128)(2,1)} %get-tuple-element.71), channel_id=1, source_target_pairs={{0,4},{1,5},{2,6},{3,7},{4,8},{5,9},{6,10},{7,11},{8,12},{9,13},{1... | collective-permute-start | bytes 196616 | tf_op jit(solution)/shard_map/ppermute | solution.py:480
  97.3 11.3 %collective-permute-start.29 = (bf16[2,8,16,128]{3,2,1,0:T(8,128)(2,1)}, bf16[2,8,16,128]{3,2,1,0:T(8,128)(2,1)S(1)}, u32[]{:S(2)}, u32[]{:S(2)}) collective-permute-start(bf16[2,8,16,128]{3,2,1,0:T(8,128)(2,1)} %get-tuple-element.73), channel_id=1, source_target_pairs={{0,8},{1,9},{2,10},{3,11},{4,12},{5,13},{6,14},{7,15},{8,0},{9,1},... | collective-permute-start | bytes 196616 | tf_op jit(solution)/shard_map/ppermute | solution.py:480
  98.5 10.1 %collective-permute-start.31 = (bf16[2,8,16,128]{3,2,1,0:T(8,128)(2,1)}, bf16[2,8,16,128]{3,2,1,0:T(8,128)(2,1)S(1)}, u32[]{:S(2)}, u32[]{:S(2)}) collective-permute-start(bf16[2,8,16,128]{3,2,1,0:T(8,128)(2,1)} %get-tuple-element.75), channel_id=1, source_target_pairs={{0,12},{1,13},{2,14},{3,15},{4,0},{5,1},{6,2},{7,3},{8,4},{9,5},{1... | collective-permute-start | bytes 196616 | tf_op jit(solution)/shard_map/ppermute | solution.py:480
  (18 other events, 72.8 us)
where the time goes:
time: 112 us; the launch traced here: 111 us
  waiting for transfers between devices  39.4 us (35%)
  Pallas kernels  35.9 us (32%)
  starting transfers between devices  33.8 us (30%)
  local copies, waits for them, and re-layouts  1.88 us (2%)
    ppermute x33, waiting for transfers between devices, shifted(): return lax.ppermute(value, ('stn', 'chan'), pairs)  39.4 us
    ppermute x33, starting transfers between devices, shifted(): return lax.ppermute(value, ('stn', 'chan'), pairs)  33.8 us
    pallas_call x3, Pallas kernels, correlate_pieces(): pl.pallas_call(functools.partial(pieces_kernel, sizes=sizes, pieces=piece...  18.3 us
    pallas_call x1, Pallas kernels, make_spectra(): pl.pallas_call(functools.partial(spectra_kernel, sizes=sizes, sends=sends...  15.5 us
  transfers between devices with their start and end apart: 33, of which 16 were waited for; matrix products, arithmetic and copies ran while one was open for 0% of the time, Pallas kernels for 16%

commit v1 on v0

--- a/solution.py
+++ b/solution.py
@@ -237,7 +237,7 @@
 
         copies = []
         for dc in range(chans):
-            chan = lax.rem(lax.axis_index("chan") + dc, chans) if turned else dc
+            chan = lax.bitwise_xor(lax.axis_index("chan"), dc) if turned else dc
 
             def some_rows(at, carry, chan=chan):
                 for one in range(near):
@@ -250,7 +250,7 @@
                     continue
                 first = chan * (kept // chans * parts) + skip
                 if dz is not None:
-                    station = lax.rem(lax.axis_index("stn") + dz, stations)
+                    station = lax.bitwise_xor(lax.axis_index("stn"), dz)
                     first = first + station * (kept // chans * parts // stations)
                 copies.append(
                     pltpu.make_async_copy(z_ref.at[pl.ds(first, count)], outs[index], sems.at[index])
@@ -329,42 +329,54 @@
     return [own, jnp.concatenate([own[:, wide // 2 :], -own[:, : wide // 2]], axis=1)]
 
 
-def tiles_of(blocks, slot, p_ref, q_ref, scale):
-    target, rest = blocks
-    block_inputs = target.shape[0]
+def products(p_ref, slot, owns):
+    right = jnp.concatenate(owns, axis=0)
+    left = jnp.concatenate([piece for own in owns for piece in lefts(own)], axis=0)
+    out = lax.dot_general(left, right, (((1,), (1,)), ((), ())), preferred_element_type=f32)
+    p_ref[slot, :, : right.shape[0]] = out
+
+
+def tiles_of(p_ref, q_ref, slot, at, block, targets, block_inputs, scale):
     copies = LANES // block_inputs
     out_rows = block_inputs * block_inputs // LANES
     place = lax.broadcasted_iota(jnp.int32, (out_rows, LANES), 1) // block_inputs
-    right = jnp.concatenate([target] * copies, axis=0)
-    left = jnp.concatenate([piece for pair in rest for piece in pair], axis=0)
-    out = lax.dot_general(left, right, (((1,), (1,)), ((), ())), preferred_element_type=f32)
-    p_ref[slot, :, :] = out * scale
-    tiles = []
-    for d in range(len(rest)):
-        for part in range(2):
-            base = (2 * d + part) * block_inputs
-            value = p_ref[slot, pl.ds(base, out_rows, stride=copies), :]
-            for r in range(1, copies):
-                value = jnp.where(place == r, p_ref[slot, pl.ds(base + r, out_rows, stride=copies), :], value)
-            q_ref[slot, d, pl.ds(part, out_rows, stride=2), :] = value
-        tiles.append(q_ref[slot, d].astype(bf16))
-    return tiles
+    for part in range(2):
+        base = (2 * block + part) * block_inputs
+        rows = [p_ref[slot, pl.ds(base + r, out_rows, stride=copies), :] for r in range(copies)]
+        for index, target in enumerate(targets):
+            value = None
+            for r in range(copies):
+                shift = (r - target) % copies if isinstance(target, int) else lax.rem(r - target + copies, copies)
+                moved = rows[r]
+                if not (isinstance(shift, int) and shift == 0):
+                    moved = pltpu.roll(moved, shift * block_inputs, 1)
+                value = moved if r == 0 else jnp.where(place == r, moved, value)
+            q_ref[at + index, pl.ds(part, out_rows, stride=2), :] = value * scale
+    return [q_ref[at + index].astype(bf16) for index in range(len(targets))]
 
 
 def correlate_kernel(r_ref, o_ref, p_ref, q_ref, *, sizes):
     stations, chans, reach, scale = sizes
 
-    def one_target(target, carry):
-        owns = []
+    block_inputs = chans * r_ref.shape[2]
+
+    def one_block(b, carry):
+        def fetch(block):
+            return jnp.concatenate([r_ref[c * stations + block, 0] for c in range(chans)], axis=0)
+
+        own = fetch(b)
         for d in range(reach):
-            b = lax.rem(target - d + stations, stations)
-            owns.append(jnp.concatenate([r_ref[c * stations + b, 0] for c in range(chans)], axis=0))
-        tiles = tiles_of((owns[0], [lefts(own) for own in owns]), 0, p_ref, q_ref, scale)
-        for d, tile in enumerate(tiles):
-            o_ref[lax.rem(target - d + stations, stations), d, 0, :, :] = tile
+            other = lax.rem(b + d, stations)
+            right = fetch(other)
+            left = jnp.concatenate(lefts(own), axis=0)
+            p_ref[d, :, :block_inputs] = lax.dot_general(
+                left, right, (((1,), (1,)), ((), ())), preferred_element_type=f32
+            )
+            (tile,) = tiles_of(p_ref, q_ref, d, d, 0, [0], block_inputs, scale)
+            o_ref[b, d, 0, :, :] = tile
         return carry
 
-    lax.fori_loop(0, stations, one_target, 0)
+    lax.fori_loop(0, stations, one_block, 0)
 
 
 def correlate(turned, stations, chans, reach, scale):
@@ -379,8 +391,8 @@
         out_specs=pl.BlockSpec((stations, reach, 1, 2 * out_rows, LANES), lambda g: (0, 0, g, 0, 0)),
         out_shape=jax.ShapeDtypeStruct((stations, reach, groups, 2 * out_rows, LANES), bf16),
         scratch_shapes=[
-            pltpu.VMEM((1, reach * 2 * block_inputs, LANES), f32),
-            pltpu.VMEM((1, reach, 2 * out_rows, LANES), f32),
+            pltpu.VMEM((reach, 2 * block_inputs, LANES), f32),
+            pltpu.VMEM((reach, 2 * out_rows, LANES), f32),
         ],
     )(turned)
 
@@ -390,9 +402,12 @@
     arrived = refs[: len(pieces)]
     outs = refs[len(pieces) : len(pieces) + blocks]
     r_ref, p_ref, q_ref, sems = refs[len(pieces) + blocks :]
+    here = lax.axis_index("stn") if blocks > 1 else 0
+    block_inputs = chans * r_ref.shape[2]
     copies = []
-    for index, (block, dc, mine, first) in enumerate(pieces):
-        chan = lax.rem(lax.axis_index("chan") - dc + chans, chans)
+    for index, (dz, dc, mine, first) in enumerate(pieces):
+        chan = lax.bitwise_xor(lax.axis_index("chan"), dc)
+        block = lax.bitwise_xor(here, dz) if blocks > 1 else 0
         start = first + lax.axis_index("stn") * mine if mine else first
         copies.append(
             pltpu.make_async_copy(
@@ -410,14 +425,14 @@
                 jnp.concatenate([r_ref[block * chans + c, g] for c in range(chans)], axis=0)
                 for block in range(blocks)
             ]
-            pairs = [lefts(own) for own in owns]
-            for target in range(blocks):
-                who = [(target - d) % blocks for d in distances]
-                tiles = tiles_of(
-                    (owns[target], [pairs[b] for b in who]), one * blocks + target, p_ref, q_ref, scale
-                )
-                for d, (b, tile) in enumerate(zip(who, tiles)):
-                    outs[b][d, g, :, :] = tile
+            products(p_ref, one, owns)
+            for turn_by in range(blocks):
+                block = lax.bitwise_xor(here, turn_by) if blocks > 1 else 0
+                targets = [lax.rem(block + d, blocks) if blocks > 1 else 0 for d in distances]
+                first = (one * blocks + turn_by) * len(distances)
+                tiles = tiles_of(p_ref, q_ref, one, first, block, targets, block_inputs, scale)
+                for d, tile in enumerate(tiles):
+                    outs[turn_by][d, g, :, :] = tile
         return carry
 
     lax.fori_loop(0, groups // per_step, some_groups, 0)
@@ -438,8 +453,8 @@
         out_shape=[jax.ShapeDtypeStruct(shape, bf16)] * blocks,
         scratch_shapes=[
             pltpu.VMEM((blocks * chans, groups, inputs, wide), bf16),
-            pltpu.VMEM((per_step * blocks, len(distances) * 2 * block_inputs, LANES), f32),
-            pltpu.VMEM((per_step * blocks, len(distances), 2 * out_rows, LANES), f32),
+            pltpu.VMEM((per_step, blocks * 2 * block_inputs, LANES), f32),
+            pltpu.VMEM((per_step * blocks * len(distances), 2 * out_rows, LANES), f32),
             pltpu.SemaphoreType.DMA((len(pieces),)),
         ],
     )(*arrays)
@@ -450,7 +465,7 @@
     out_ref = refs[-1]
     out_ref[0, :, :, :] = own_ref[0]
     for dz in range(stations):
-        host = lax.rem(lax.axis_index("stn") - dz + stations, stations)
+        host = lax.bitwise_xor(lax.axis_index("stn"), dz)
         for chunk in range(chunks):
             part = parts[dz * chunks + chunk]
             count = part.shape[1]
@@ -473,7 +488,7 @@
 
 def shifted(value, stations, chans, dz, dc):
     pairs = [
-        (z * chans + c, (z + dz) % stations * chans + (c + dc) % chans)
+        (z * chans + c, (z ^ dz) * chans + (c ^ dc))
         for z in range(stations)
         for c in range(chans)
     ]
@@ -503,15 +518,14 @@
     else:
         part = here // CHUNKS
         sends = [(None, dc, 0, here * stations) for dc in range(chans)]
-        for chunk in range(CHUNKS):
-            sends += [(dz, dc, chunk * part, part) for dz in (2, 1, 3)[: stations - 1] for dc in range(chans)]
+        sends += [(dz, dc, 0, here) for dz in (2, 1, 3) for dc in range(chans)]
         sent = make_spectra(frames_first, taps, tuple(sends), stations, chans, True)
-        whole, got = [], {}
-        for (dz, dc, skip, _), value in zip(sends, sent):
+        whole, far = [], {}
+        for (dz, dc, _, _), value in zip(sends, sent):
             if dz is None:
                 whole.append(shifted(value, stations, chans, 0, dc) if dc else value)
             else:
-                got[dz, dc, skip // part] = shifted(value, stations, chans, dz, dc)
+                far[dz, dc] = shifted(value, stations, chans, dz, dc)
         stays = [dc == 0 for dc in range(chans)]
         pieces = [(0, dc, 0, 0) for dc in range(chans)]
         (own,) = correlate_pieces(whole, pieces, 1, chans, here * stations, (0,), scale, stays)
@@ -519,14 +533,10 @@
         back = {}
         for chunk in range(CHUNKS):
             pieces = [(0, dc, here, chunk * part) for dc in range(chans)]
-            arrays = list(whole)
-            for dz in range(1, stations):
-                for dc in range(chans):
-                    pieces.append((-dz % stations, dc, 0, 0))
-                    arrays.append(got[dz, dc, chunk])
-            outs = correlate_pieces(
-                arrays, pieces, stations, chans, part, distances, scale, stays + [False] * (len(arrays) - chans)
-            )
+            pieces += [(dz, dc, 0, chunk * part) for dz, dc in far]
+            arrays = whole + list(far.values())
+            inside = stays + [False] * len(far)
+            outs = correlate_pieces(arrays, pieces, stations, chans, part, distances, scale, inside)
             for dz in range(stations):
                 back[dz, chunk] = outs[0] if dz == 0 else shifted(outs[dz], stations, chans, dz, 0)
         out = assemble(
@@ -540,7 +550,7 @@
 
 
 def direct(stations, chans):
-    return 2 < stations <= 4 and stations * chans <= 16
+    return stations == 4 and chans in (1, 2, 4)
 
 
 def solution(mesh):

time: 112 us -> 111 us (level)
  waiting for transfers between devices: 39.4 us -> 37.4 us
  starting transfers between devices: 33.8 us -> 35.3 us
    ppermute x33 -> x21, waiting for transfers between devices: 39.4 us -> 37.4 us  [shifted(): return lax.ppermute(value, ('stn', 'chan'), pairs)]
    ppermute x33 -> x21, starting transfers between devices: 33.8 us -> 35.3 us  [shifted(): return lax.ppermute(value, ('stn', 'chan'), pairs)]
  transfers between devices with their start and end apart: 33 -> 21, of which waited for: 16 -> 11; matrix products, arithmetic and copies ran while one was open for 0% -> 0% of each run, Pallas kernels for 16% -> 11%
where the time goes in v1:
time: 111 us; the launch traced here: 110 us
  waiting for transfers between devices  37.4 us (34%)
  Pallas kernels  35.7 us (32%)
  starting transfers between devices  35.3 us (32%)
  local copies, waits for them, and re-layouts  1.72 us (2%)
    ppermute x21, waiting for transfers between devices, shifted(): return lax.ppermute(value, ('stn', 'chan'), pairs)  37.4 us
    ppermute x21, starting transfers between devices, shifted(): return lax.ppermute(value, ('stn', 'chan'), pairs)  35.3 us
    pallas_call x3, Pallas kernels, correlate_pieces(): pl.pallas_call(functools.partial(pieces_kernel, sizes=sizes, pieces=piece...  18.3 us
    pallas_call x1, Pallas kernels, make_spectra(): pl.pallas_call(functools.partial(spectra_kernel, sizes=sizes, sends=sends...  15.4 us
  transfers between devices with their start and end apart: 21, of which 11 were waited for; matrix products, arithmetic and copies ran while one was open for 0% of the time, Pallas kernels for 11%

profile of v1, /device:TPU:0, one launch (start us, length us, event | category | flops | bytes accessed | tf_op | source)
XLA Modules:
  0.0 110.4 jit_solution(15356166526474738588)
XLA Ops:
  0.0 15.4 %spectra.1 = (bf16[64,8,512]{2,1,0:T(8,128)(2,1)}, bf16[64,8,512]{2,1,0:T(8,128)(2,1)}, bf16[64,8,512]{2,1,0:T(8,128)(2,1)}, bf16[64,8,512]{2,1,0:T(8,128)(2,1)}...) custom-call(f32[528,128]{1,0:T(8,128)} %constant.4.clone.tw_ref, ...), custom_call_target="tpu_custom_call" | custom-call | tf_op jit(solution)/shard_map/spectra/pallas_call | solution.py:303
  15.4 3.5 %collective-permute-start.10 = (bf16[16,8,512]{2,1,0:T(8,128)(2,1)}, bf16[16,8,512]{2,1,0:T(8,128)(2,1)S(1)}, u32[]{:S(2)}, u32[]{:S(2)}) collective-permute-start(bf16[16,8,512]{2,1,0:T(8,128)(2,1)} %get-tuple-element.40), channel_id=1, source_target_pairs={{0,7},{1,6},{2,5},{3,4},{4,3},{5,2},{6,1},{7,0},{8,15},{9,14},{10,... | collective-permute-start | bytes 393224 | tf_op jit(solution)/shard_map/ppermute | solution.py:495
  18.9 2.5 %collective-permute-start.11 = (bf16[16,8,512]{2,1,0:T(8,128)(2,1)}, bf16[16,8,512]{2,1,0:T(8,128)(2,1)S(1)}, u32[]{:S(2)}, u32[]{:S(2)}) collective-permute-start(bf16[16,8,512]{2,1,0:T(8,128)(2,1)} %get-tuple-element.41), channel_id=1, source_target_pairs={{0,12},{1,13},{2,14},{3,15},{4,8},{5,9},{6,10},{7,11},{8,4},{9,5},... | collective-permute-start | bytes 393224 | tf_op jit(solution)/shard_map/ppermute | solution.py:495
  21.4 1.3 %collective-permute-start.12 = (bf16[16,8,512]{2,1,0:T(8,128)(2,1)}, bf16[16,8,512]{2,1,0:T(8,128)(2,1)S(1)}, u32[]{:S(2)}, u32[]{:S(2)}) collective-permute-start(bf16[16,8,512]{2,1,0:T(8,128)(2,1)} %get-tuple-element.42), channel_id=1, source_target_pairs={{0,13},{1,12},{2,15},{3,14},{4,9},{5,8},{6,11},{7,10},{8,5},{9,4},... | collective-permute-start | bytes 393224 | tf_op jit(solution)/shard_map/ppermute | solution.py:495
  22.7 2.4 %collective-permute-start.13 = (bf16[16,8,512]{2,1,0:T(8,128)(2,1)}, bf16[16,8,512]{2,1,0:T(8,128)(2,1)S(1)}, u32[]{:S(2)}, u32[]{:S(2)}) collective-permute-start(bf16[16,8,512]{2,1,0:T(8,128)(2,1)} %get-tuple-element.43), channel_id=1, source_target_pairs={{0,14},{1,15},{2,12},{3,13},{4,10},{5,11},{6,8},{7,9},{8,6},{9,7},... | collective-permute-start | bytes 393224 | tf_op jit(solution)/shard_map/ppermute | solution.py:495
  25.2 1.7 %collective-permute-start.14 = (bf16[16,8,512]{2,1,0:T(8,128)(2,1)}, bf16[16,8,512]{2,1,0:T(8,128)(2,1)S(1)}, u32[]{:S(2)}, u32[]{:S(2)}) collective-permute-start(bf16[16,8,512]{2,1,0:T(8,128)(2,1)} %get-tuple-element.44), channel_id=1, source_target_pairs={{0,15},{1,14},{2,13},{3,12},{4,11},{5,10},{6,9},{7,8},{8,7},{9,6},... | collective-permute-start | bytes 393224 | tf_op jit(solution)/shard_map/ppermute | solution.py:495
  26.9 0.0 collective-permute-done.10.refs_11_
  26.9 1.9 %collective-permute-done.11.refs_12_ = bf16[16,8,512]{2,1,0:T(8,128)(2,1)S(1)} collective-permute-done((bf16[16,8,512]{2,1,0:T(8,128)(2,1)}, bf16[16,8,512]{2,1,0:T(8,128)(2,1)S(1)}, u32[]{:S(2)}, u32[]{:S(2)}) %collective-permute-start.11) | collective-permute-done | bytes 131104 | tf_op jit(solution)/shard_map/ppermute | solution.py:495
  28.8 0.0 collective-permute-start
  28.9 2.7 %collective-permute-done.12.refs_13_ = bf16[16,8,512]{2,1,0:T(8,128)(2,1)S(1)} collective-permute-done((bf16[16,8,512]{2,1,0:T(8,128)(2,1)}, bf16[16,8,512]{2,1,0:T(8,128)(2,1)S(1)}, u32[]{:S(2)}, u32[]{:S(2)}) %collective-permute-start.12) | collective-permute-done | bytes 131104 | tf_op jit(solution)/shard_map/ppermute | solution.py:495
  31.6 0.4 collective-permute-start.1
  32.0 2.6 %collective-permute-done.13.refs_14_ = bf16[16,8,512]{2,1,0:T(8,128)(2,1)S(1)} collective-permute-done((bf16[16,8,512]{2,1,0:T(8,128)(2,1)}, bf16[16,8,512]{2,1,0:T(8,128)(2,1)S(1)}, u32[]{:S(2)}, u32[]{:S(2)}) %collective-permute-start.13) | collective-permute-done | bytes 131104 | tf_op jit(solution)/shard_map/ppermute | solution.py:495
  34.6 1.0 collective-permute-start.2
  35.5 1.6 %collective-permute-done.14.refs_15_ = bf16[16,8,512]{2,1,0:T(8,128)(2,1)S(1)} collective-permute-done((bf16[16,8,512]{2,1,0:T(8,128)(2,1)}, bf16[16,8,512]{2,1,0:T(8,128)(2,1)S(1)}, u32[]{:S(2)}, u32[]{:S(2)}) %collective-permute-start.14) | collective-permute-done | bytes 131104 | tf_op jit(solution)/shard_map/ppermute | solution.py:495
  37.2 12.8 %collective-permute-start.4 = (bf16[16,8,512]{2,1,0:T(8,128)(2,1)}, bf16[16,8,512]{2,1,0:T(8,128)(2,1)S(1)}, u32[]{:S(2)}, u32[]{:S(2)}) collective-permute-start(bf16[16,8,512]{2,1,0:T(8,128)(2,1)} %get-tuple-element.34), channel_id=1, source_target_pairs={{0,9},{1,8},{2,11},{3,10},{4,13},{5,12},{6,15},{7,14},{8,1},{9,0},... | collective-permute-start | bytes 393224 | tf_op jit(solution)/shard_map/ppermute | solution.py:495
  50.0 1.4 %collective-permute-done.3.refs_4_ = bf16[16,8,512]{2,1,0:T(8,128)(2,1)S(1)} collective-permute-done((bf16[16,8,512]{2,1,0:T(8,128)(2,1)}, bf16[16,8,512]{2,1,0:T(8,128)(2,1)S(1)}, u32[]{:S(2)}, u32[]{:S(2)}) %collective-permute-start.3) | collective-permute-done | bytes 131104 | tf_op jit(solution)/shard_map/ppermute | solution.py:495
  51.3 0.0 collective-permute-start.5
  51.3 8.2 %collective-permute-done.4.refs_5_ = bf16[16,8,512]{2,1,0:T(8,128)(2,1)S(1)} collective-permute-done((bf16[16,8,512]{2,1,0:T(8,128)(2,1)}, bf16[16,8,512]{2,1,0:T(8,128)(2,1)S(1)}, u32[]{:S(2)}, u32[]{:S(2)}) %collective-permute-start.4) | collective-permute-done | bytes 131104 | tf_op jit(solution)/shard_map/ppermute | solution.py:495
  59.5 0.3 collective-permute-start.6
  59.8 3.8 %collective-permute-done.5.refs_6_ = bf16[16,8,512]{2,1,0:T(8,128)(2,1)S(1)} collective-permute-done((bf16[16,8,512]{2,1,0:T(8,128)(2,1)}, bf16[16,8,512]{2,1,0:T(8,128)(2,1)S(1)}, u32[]{:S(2)}, u32[]{:S(2)}) %collective-permute-start.5) | collective-permute-done | bytes 131104 | tf_op jit(solution)/shard_map/ppermute | solution.py:495
  63.6 0.0 collective-permute-start.7
  63.6 6.2 %collective-permute-done.6.refs_7_ = bf16[16,8,512]{2,1,0:T(8,128)(2,1)S(1)} collective-permute-done((bf16[16,8,512]{2,1,0:T(8,128)(2,1)}, bf16[16,8,512]{2,1,0:T(8,128)(2,1)S(1)}, u32[]{:S(2)}, u32[]{:S(2)}) %collective-permute-start.6) | collective-permute-done | bytes 131104 | tf_op jit(solution)/shard_map/ppermute | solution.py:495
  69.8 0.0 collective-permute-start.8
  69.8 1.9 %collective-permute-done.7.refs_8_ = bf16[16,8,512]{2,1,0:T(8,128)(2,1)S(1)} collective-permute-done((bf16[16,8,512]{2,1,0:T(8,128)(2,1)}, bf16[16,8,512]{2,1,0:T(8,128)(2,1)S(1)}, u32[]{:S(2)}, u32[]{:S(2)}) %collective-permute-start.7) | collective-permute-done | bytes 131104 | tf_op jit(solution)/shard_map/ppermute | solution.py:495
  71.7 0.4 collective-permute-start.9
  72.1 3.5 %collective-permute-done.8.refs_9_ = bf16[16,8,512]{2,1,0:T(8,128)(2,1)S(1)} collective-permute-done((bf16[16,8,512]{2,1,0:T(8,128)(2,1)}, bf16[16,8,512]{2,1,0:T(8,128)(2,1)S(1)}, u32[]{:S(2)}, u32[]{:S(2)}) %collective-permute-start.8) | collective-permute-done | bytes 131104 | tf_op jit(solution)/shard_map/ppermute | solution.py:495
  75.6 3.6 %collective-permute-done.9.refs_10_ = bf16[16,8,512]{2,1,0:T(8,128)(2,1)S(1)} collective-permute-done((bf16[16,8,512]{2,1,0:T(8,128)(2,1)}, bf16[16,8,512]{2,1,0:T(8,128)(2,1)S(1)}, u32[]{:S(2)}, u32[]{:S(2)}) %collective-permute-start.9) | collective-permute-done | bytes 131104 | tf_op jit(solution)/shard_map/ppermute | solution.py:495
  79.4 0.5 copy-done.14
  79.9 0.2 copy-done
  80.1 0.2 copy-done.1
  80.3 0.1 copy-done.2
  80.4 6.1 %shard_map.48 = (bf16[2,8,16,128]{3,2,1,0:T(8,128)(2,1)}, bf16[2,8,16,128]{3,2,1,0:T(8,128)(2,1)}, bf16[2,8,16,128]{3,2,1,0:T(8,128)(2,1)}, bf16[2,8,16,128]{3,2,1,0:T(8,128)(2,1)}) custom-call(bf16[64,8,512]{2,1,0:T(8,128)(2,1)} %get-tuple-element.29.refs_0_, bf16[64,8,512]{2,1,0:T(8,128)(2,1)} %copy-done, bf16[64,8,512]{2,1,0:T(8,128)(2,1)} %copy-done.1, ...), custom_call_target="tpu_custom_call" | custom-call | tf_op jit(solution)/shard_map/pallas_call | solution.py:449
  86.5 0.3 collective-permute-start.16
  86.8 1.9 %collective-permute-start.18 = (bf16[2,8,16,128]{3,2,1,0:T(8,128)(2,1)}, bf16[2,8,16,128]{3,2,1,0:T(8,128)(2,1)S(1)}, u32[]{:S(2)}, u32[]{:S(2)}) collective-permute-start(bf16[2,8,16,128]{3,2,1,0:T(8,128)(2,1)} %get-tuple-element.50), channel_id=1, source_target_pairs={{0,8},{1,9},{2,10},{3,11},{4,12},{5,13},{6,14},{7,15},{8,0},{9,1},... | collective-permute-start | bytes 196616 | tf_op jit(solution)/shard_map/ppermute | solution.py:495
  88.7 2.3 %collective-permute-start.20 = (bf16[2,8,16,128]{3,2,1,0:T(8,128)(2,1)}, bf16[2,8,16,128]{3,2,1,0:T(8,128)(2,1)S(1)}, u32[]{:S(2)}, u32[]{:S(2)}) collective-permute-start(bf16[2,8,16,128]{3,2,1,0:T(8,128)(2,1)} %get-tuple-element.52), channel_id=1, source_target_pairs={{0,12},{1,13},{2,14},{3,15},{4,8},{5,9},{6,10},{7,11},{8,4},{9,5},... | collective-permute-start | bytes 196616 | tf_op jit(solution)/shard_map/ppermute | solution.py:495
  91.0 6.1 %shard_map.47 = (bf16[2,8,16,128]{3,2,1,0:T(8,128)(2,1)}, bf16[2,8,16,128]{3,2,1,0:T(8,128)(2,1)}, bf16[2,8,16,128]{3,2,1,0:T(8,128)(2,1)}, bf16[2,8,16,128]{3,2,1,0:T(8,128)(2,1)}) custom-call(bf16[64,8,512]{2,1,0:T(8,128)(2,1)} %get-tuple-element.29.refs_0_, bf16[64,8,512]{2,1,0:T(8,128)(2,1)} %copy-done, bf16[64,8,512]{2,1,0:T(8,128)(2,1)} %copy-done.1, ...), custom_call_target="tpu_custom_call" | custom-call | tf_op jit(solution)/shard_map/pallas_call | solution.py:449
  97.1 0.1 collective-permute-start.15
  97.1 2.1 %collective-permute-start.17 = (bf16[2,8,16,128]{3,2,1,0:T(8,128)(2,1)}, bf16[2,8,16,128]{3,2,1,0:T(8,128)(2,1)S(1)}, u32[]{:S(2)}, u32[]{:S(2)}) collective-permute-start(bf16[2,8,16,128]{3,2,1,0:T(8,128)(2,1)} %get-tuple-element.49), channel_id=1, source_target_pairs={{0,8},{1,9},{2,10},{3,11},{4,12},{5,13},{6,14},{7,15},{8,0},{9,1},... | collective-permute-start | bytes 196616 | tf_op jit(solution)/shard_map/ppermute | solution.py:495
  99.2 0.0 collective-permute-done.16.refs_3_
  99.2 2.3 %collective-permute-start.19 = (bf16[2,8,16,128]{3,2,1,0:T(8,128)(2,1)}, bf16[2,8,16,128]{3,2,1,0:T(8,128)(2,1)S(1)}, u32[]{:S(2)}, u32[]{:S(2)}) collective-permute-start(bf16[2,8,16,128]{3,2,1,0:T(8,128)(2,1)} %get-tuple-element.51), channel_id=1, source_target_pairs={{0,12},{1,13},{2,14},{3,15},{4,8},{5,9},{6,10},{7,11},{8,4},{9,5},... | collective-permute-start | bytes 196616 | tf_op jit(solution)/shard_map/ppermute | solution.py:495
  101.5 6.1 %shard_map.46.own_ref = bf16[1,64,16,128]{3,2,1,0:T(8,128)(2,1)} custom-call(bf16[64,8,512]{2,1,0:T(8,128)(2,1)} %get-tuple-element.29.refs_0_, bf16[64,8,512]{2,1,0:T(8,128)(2,1)} %copy-done, bf16[64,8,512]{2,1,0:T(8,128)(2,1)} %copy-done.1, bf16[64,8,512]{2,1,0:T(8,128)(2,1)} %copy-done.2), custom_call_target="tpu_custom_call" | custom-call | tf_op jit(solution)/shard_map/pallas_call | solution.py:449
  107.6 0.0 collective-permute-done.18.refs_5_
  107.7 0.0 collective-permute-done.17.refs_4_
  107.7 0.5 copy-done.16
  108.2 0.0 copy-done.17
  108.3 0.0 copy-done.18
  108.3 0.0 copy-done.19
  108.3 2.0 %assemble.1 = bf16[3,64,16,128]{3,2,1,0:T(8,128)(2,1)} custom-call(bf16[1,64,16,128]{3,2,1,0:T(8,128)(2,1)} %shard_map.46.own_ref, bf16[2,8,16,128]{3,2,1,0:T(8,128)(2,1)} %get-tuple-element.45.refs_0_, bf16[2,8,16,128]{3,2,1,0:T(8,128)(2,1)} %get-tuple-element.46.refs_1_, bf16[2,8,16,128]{3,2,1,0:T(8,128)(2,1)} %copy-done.18, ...), custom_call_target="tpu_custom_call" | custom-call | tf_op jit(solution)/shard_map/assemble/pallas_call | solution.py:480
  (41 shorter events, 0.1 us)
Async XLA Ops:
  15.4 11.5 %collective-permute-start.10 = (bf16[16,8,512]{2,1,0:T(8,128)(2,1)}, bf16[16,8,512]{2,1,0:T(8,128)(2,1)S(1)}, u32[]{:S(2)}, u32[]{:S(2)}) collective-permute-start(bf16[16,8,512]{2,1,0:T(8,128)(2,1)} %get-tuple-element.40), channel_id=1, source_target_pairs={{0,7},{1,6},{2,5},{3,4},{4,3},{5,2},{6,1},{7,0},{8,15},{9,14},{10,... | collective-permute-start | bytes 393224 | tf_op jit(solution)/shard_map/ppermute | solution.py:495
  18.9 9.9 %collective-permute-start.11 = (bf16[16,8,512]{2,1,0:T(8,128)(2,1)}, bf16[16,8,512]{2,1,0:T(8,128)(2,1)S(1)}, u32[]{:S(2)}, u32[]{:S(2)}) collective-permute-start(bf16[16,8,512]{2,1,0:T(8,128)(2,1)} %get-tuple-element.41), channel_id=1, source_target_pairs={{0,12},{1,13},{2,14},{3,15},{4,8},{5,9},{6,10},{7,11},{8,4},{9,5},... | collective-permute-start | bytes 393224 | tf_op jit(solution)/shard_map/ppermute | solution.py:495
  21.4 10.2 %collective-permute-start.12 = (bf16[16,8,512]{2,1,0:T(8,128)(2,1)}, bf16[16,8,512]{2,1,0:T(8,128)(2,1)S(1)}, u32[]{:S(2)}, u32[]{:S(2)}) collective-permute-start(bf16[16,8,512]{2,1,0:T(8,128)(2,1)} %get-tuple-element.42), channel_id=1, source_target_pairs={{0,13},{1,12},{2,15},{3,14},{4,9},{5,8},{6,11},{7,10},{8,5},{9,4},... | collective-permute-start | bytes 393224 | tf_op jit(solution)/shard_map/ppermute | solution.py:495
  22.7 11.9 %collective-permute-start.13 = (bf16[16,8,512]{2,1,0:T(8,128)(2,1)}, bf16[16,8,512]{2,1,0:T(8,128)(2,1)S(1)}, u32[]{:S(2)}, u32[]{:S(2)}) collective-permute-start(bf16[16,8,512]{2,1,0:T(8,128)(2,1)} %get-tuple-element.43), channel_id=1, source_target_pairs={{0,14},{1,15},{2,12},{3,13},{4,10},{5,11},{6,8},{7,9},{8,6},{9,7},... | collective-permute-start | bytes 393224 | tf_op jit(solution)/shard_map/ppermute | solution.py:495
  25.2 12.0 %collective-permute-start.14 = (bf16[16,8,512]{2,1,0:T(8,128)(2,1)}, bf16[16,8,512]{2,1,0:T(8,128)(2,1)S(1)}, u32[]{:S(2)}, u32[]{:S(2)}) collective-permute-start(bf16[16,8,512]{2,1,0:T(8,128)(2,1)} %get-tuple-element.44), channel_id=1, source_target_pairs={{0,15},{1,14},{2,13},{3,12},{4,11},{5,10},{6,9},{7,8},{8,7},{9,6},... | collective-permute-start | bytes 393224 | tf_op jit(solution)/shard_map/ppermute | solution.py:495
  26.9 52.4 %copy-start.3 = (bf16[16,8,512]{2,1,0:T(8,128)(2,1)}, bf16[16,8,512]{2,1,0:T(8,128)(2,1)S(1)}, u32[]{:S(2)}) copy-start(bf16[16,8,512]{2,1,0:T(8,128)(2,1)S(1)} %collective-permute-done.10.refs_11_) | copy-start | bytes 393220
  26.9 24.5 %collective-permute-start.3 = (bf16[16,8,512]{2,1,0:T(8,128)(2,1)}, bf16[16,8,512]{2,1,0:T(8,128)(2,1)S(1)}, u32[]{:S(2)}, u32[]{:S(2)}) collective-permute-start(bf16[16,8,512]{2,1,0:T(8,128)(2,1)} %get-tuple-element.33), channel_id=1, source_target_pairs={{0,8},{1,9},{2,10},{3,11},{4,12},{5,13},{6,14},{7,15},{8,0},{9,1},... | collective-permute-start | bytes 393224 | tf_op jit(solution)/shard_map/ppermute | solution.py:495
  28.8 50.4 %copy-start.4 = (bf16[16,8,512]{2,1,0:T(8,128)(2,1)}, bf16[16,8,512]{2,1,0:T(8,128)(2,1)S(1)}, u32[]{:S(2)}) copy-start(bf16[16,8,512]{2,1,0:T(8,128)(2,1)S(1)} %collective-permute-done.11.refs_12_) | copy-start | bytes 393220
  28.8 50.4 %collective-permute-start = (bf16[64,8,512]{2,1,0:T(8,128)(2,1)}, bf16[64,8,512]{2,1,0:T(8,128)(2,1)S(1)}, u32[]{:S(2)}, u32[]{:S(2)}) collective-permute-start(bf16[64,8,512]{2,1,0:T(8,128)(2,1)} %get-tuple-element.30), channel_id=1, source_target_pairs={{0,1},{1,0},{2,3},{3,2},{4,5},{5,4},{6,7},{7,6},{8,9},{9,8},{10,11... | collective-permute-start | bytes 1572872 | tf_op jit(solution)/shard_map/ppermute | solution.py:495
  31.6 47.7 %copy-start.5 = (bf16[16,8,512]{2,1,0:T(8,128)(2,1)}, bf16[16,8,512]{2,1,0:T(8,128)(2,1)S(1)}, u32[]{:S(2)}) copy-start(bf16[16,8,512]{2,1,0:T(8,128)(2,1)S(1)} %collective-permute-done.12.refs_13_) | copy-start | bytes 393220
  31.6 47.6 %collective-permute-start.1 = (bf16[64,8,512]{2,1,0:T(8,128)(2,1)}, bf16[64,8,512]{2,1,0:T(8,128)(2,1)S(1)}, u32[]{:S(2)}, u32[]{:S(2)}) collective-permute-start(bf16[64,8,512]{2,1,0:T(8,128)(2,1)} %get-tuple-element.31), channel_id=1, source_target_pairs={{0,2},{1,3},{2,0},{3,1},{4,6},{5,7},{6,4},{7,5},{8,10},{9,11},{10,... | collective-permute-start | bytes 1572872 | tf_op jit(solution)/shard_map/ppermute | solution.py:495
  34.6 44.7 %copy-start.6 = (bf16[16,8,512]{2,1,0:T(8,128)(2,1)}, bf16[16,8,512]{2,1,0:T(8,128)(2,1)S(1)}, u32[]{:S(2)}) copy-start(bf16[16,8,512]{2,1,0:T(8,128)(2,1)S(1)} %collective-permute-done.13.refs_14_) | copy-start | bytes 393220
  34.6 44.7 %collective-permute-start.2 = (bf16[64,8,512]{2,1,0:T(8,128)(2,1)}, bf16[64,8,512]{2,1,0:T(8,128)(2,1)S(1)}, u32[]{:S(2)}, u32[]{:S(2)}) collective-permute-start(bf16[64,8,512]{2,1,0:T(8,128)(2,1)} %get-tuple-element.32), channel_id=1, source_target_pairs={{0,3},{1,2},{2,1},{3,0},{4,7},{5,6},{6,5},{7,4},{8,11},{9,10},{10,... | collective-permute-start | bytes 1572872 | tf_op jit(solution)/shard_map/ppermute | solution.py:495
  37.2 42.1 %copy-start.7 = (bf16[16,8,512]{2,1,0:T(8,128)(2,1)}, bf16[16,8,512]{2,1,0:T(8,128)(2,1)S(1)}, u32[]{:S(2)}) copy-start(bf16[16,8,512]{2,1,0:T(8,128)(2,1)S(1)} %collective-permute-done.14.refs_15_) | copy-start | bytes 393220
  37.2 22.4 %collective-permute-start.4 = (bf16[16,8,512]{2,1,0:T(8,128)(2,1)}, bf16[16,8,512]{2,1,0:T(8,128)(2,1)S(1)}, u32[]{:S(2)}, u32[]{:S(2)}) collective-permute-start(bf16[16,8,512]{2,1,0:T(8,128)(2,1)} %get-tuple-element.34), channel_id=1, source_target_pairs={{0,9},{1,8},{2,11},{3,10},{4,13},{5,12},{6,15},{7,14},{8,1},{9,0},... | collective-permute-start | bytes 393224 | tf_op jit(solution)/shard_map/ppermute | solution.py:495
  51.3 28.0 %copy-start.8 = (bf16[16,8,512]{2,1,0:T(8,128)(2,1)}, bf16[16,8,512]{2,1,0:T(8,128)(2,1)S(1)}, u32[]{:S(2)}) copy-start(bf16[16,8,512]{2,1,0:T(8,128)(2,1)S(1)} %collective-permute-done.3.refs_4_) | copy-start | bytes 393220
  51.3 12.2 %collective-permute-start.5 = (bf16[16,8,512]{2,1,0:T(8,128)(2,1)}, bf16[16,8,512]{2,1,0:T(8,128)(2,1)S(1)}, u32[]{:S(2)}, u32[]{:S(2)}) collective-permute-start(bf16[16,8,512]{2,1,0:T(8,128)(2,1)} %get-tuple-element.35), channel_id=1, source_target_pairs={{0,10},{1,11},{2,8},{3,9},{4,14},{5,15},{6,12},{7,13},{8,2},{9,3},... | collective-permute-start | bytes 393224 | tf_op jit(solution)/shard_map/ppermute | solution.py:495
  59.5 19.8 %copy-start.9 = (bf16[16,8,512]{2,1,0:T(8,128)(2,1)}, bf16[16,8,512]{2,1,0:T(8,128)(2,1)S(1)}, u32[]{:S(2)}) copy-start(bf16[16,8,512]{2,1,0:T(8,128)(2,1)S(1)} %collective-permute-done.4.refs_5_) | copy-start | bytes 393220
  59.5 10.3 %collective-permute-start.6 = (bf16[16,8,512]{2,1,0:T(8,128)(2,1)}, bf16[16,8,512]{2,1,0:T(8,128)(2,1)S(1)}, u32[]{:S(2)}, u32[]{:S(2)}) collective-permute-start(bf16[16,8,512]{2,1,0:T(8,128)(2,1)} %get-tuple-element.36), channel_id=1, source_target_pairs={{0,11},{1,10},{2,9},{3,8},{4,15},{5,14},{6,13},{7,12},{8,3},{9,2},... | collective-permute-start | bytes 393224 | tf_op jit(solution)/shard_map/ppermute | solution.py:495
  63.6 15.7 %copy-start.10 = (bf16[16,8,512]{2,1,0:T(8,128)(2,1)}, bf16[16,8,512]{2,1,0:T(8,128)(2,1)S(1)}, u32[]{:S(2)}) copy-start(bf16[16,8,512]{2,1,0:T(8,128)(2,1)S(1)} %collective-permute-done.5.refs_6_) | copy-start | bytes 393220
  63.6 8.1 %collective-permute-start.7 = (bf16[16,8,512]{2,1,0:T(8,128)(2,1)}, bf16[16,8,512]{2,1,0:T(8,128)(2,1)S(1)}, u32[]{:S(2)}, u32[]{:S(2)}) collective-permute-start(bf16[16,8,512]{2,1,0:T(8,128)(2,1)} %get-tuple-element.37), channel_id=1, source_target_pairs={{0,4},{1,5},{2,6},{3,7},{4,0},{5,1},{6,2},{7,3},{8,12},{9,13},{10,... | collective-permute-start | bytes 393224 | tf_op jit(solution)/shard_map/ppermute | solution.py:495
  69.8 9.5 %copy-start.11 = (bf16[16,8,512]{2,1,0:T(8,128)(2,1)}, bf16[16,8,512]{2,1,0:T(8,128)(2,1)S(1)}, u32[]{:S(2)}) copy-start(bf16[16,8,512]{2,1,0:T(8,128)(2,1)S(1)} %collective-permute-done.6.refs_7_) | copy-start | bytes 393220
  69.8 5.8 %collective-permute-start.8 = (bf16[16,8,512]{2,1,0:T(8,128)(2,1)}, bf16[16,8,512]{2,1,0:T(8,128)(2,1)S(1)}, u32[]{:S(2)}, u32[]{:S(2)}) collective-permute-start(bf16[16,8,512]{2,1,0:T(8,128)(2,1)} %get-tuple-element.38), channel_id=1, source_target_pairs={{0,5},{1,4},{2,7},{3,6},{4,1},{5,0},{6,3},{7,2},{8,13},{9,12},{10,... | collective-permute-start | bytes 393224 | tf_op jit(solution)/shard_map/ppermute | solution.py:495
  71.7 7.6 %copy-start.12 = (bf16[16,8,512]{2,1,0:T(8,128)(2,1)}, bf16[16,8,512]{2,1,0:T(8,128)(2,1)S(1)}, u32[]{:S(2)}) copy-start(bf16[16,8,512]{2,1,0:T(8,128)(2,1)S(1)} %collective-permute-done.7.refs_8_) | copy-start | bytes 393220
  71.7 7.5 %collective-permute-start.9 = (bf16[16,8,512]{2,1,0:T(8,128)(2,1)}, bf16[16,8,512]{2,1,0:T(8,128)(2,1)S(1)}, u32[]{:S(2)}, u32[]{:S(2)}) collective-permute-start(bf16[16,8,512]{2,1,0:T(8,128)(2,1)} %get-tuple-element.39), channel_id=1, source_target_pairs={{0,6},{1,7},{2,4},{3,5},{4,2},{5,3},{6,0},{7,1},{8,14},{9,15},{10,... | collective-permute-start | bytes 393224 | tf_op jit(solution)/shard_map/ppermute | solution.py:495
  75.6 3.8 %copy-start.13 = (bf16[16,8,512]{2,1,0:T(8,128)(2,1)}, bf16[16,8,512]{2,1,0:T(8,128)(2,1)S(1)}, u32[]{:S(2)}) copy-start(bf16[16,8,512]{2,1,0:T(8,128)(2,1)S(1)} %collective-permute-done.8.refs_9_) | copy-start | bytes 393220
  79.2 0.7 copy-start.14
  79.2 0.8 copy-start
  79.2 1.0 copy-start.1
  79.2 1.2 %copy-start.2 = (bf16[64,8,512]{2,1,0:T(8,128)(2,1)}, bf16[64,8,512]{2,1,0:T(8,128)(2,1)S(1)}, u32[]{:S(2)}) copy-start(bf16[64,8,512]{2,1,0:T(8,128)(2,1)S(1)} %collective-permute-done.2.refs_3_) | copy-start | bytes 1572868
  86.5 12.7 %collective-permute-start.16 = (bf16[2,8,16,128]{3,2,1,0:T(8,128)(2,1)}, bf16[2,8,16,128]{3,2,1,0:T(8,128)(2,1)S(1)}, u32[]{:S(2)}, u32[]{:S(2)}) collective-permute-start(bf16[2,8,16,128]{3,2,1,0:T(8,128)(2,1)} %get-tuple-element.48), channel_id=1, source_target_pairs={{0,4},{1,5},{2,6},{3,7},{4,0},{5,1},{6,2},{7,3},{8,12},{9,13},{10,... | collective-permute-start | bytes 196616 | tf_op jit(solution)/shard_map/ppermute | solution.py:495
  86.8 20.8 %collective-permute-start.18 = (bf16[2,8,16,128]{3,2,1,0:T(8,128)(2,1)}, bf16[2,8,16,128]{3,2,1,0:T(8,128)(2,1)S(1)}, u32[]{:S(2)}, u32[]{:S(2)}) collective-permute-start(bf16[2,8,16,128]{3,2,1,0:T(8,128)(2,1)} %get-tuple-element.50), channel_id=1, source_target_pairs={{0,8},{1,9},{2,10},{3,11},{4,12},{5,13},{6,14},{7,15},{8,0},{9,1},... | collective-permute-start | bytes 196616 | tf_op jit(solution)/shard_map/ppermute | solution.py:495
  88.7 19.0 %collective-permute-start.20 = (bf16[2,8,16,128]{3,2,1,0:T(8,128)(2,1)}, bf16[2,8,16,128]{3,2,1,0:T(8,128)(2,1)S(1)}, u32[]{:S(2)}, u32[]{:S(2)}) collective-permute-start(bf16[2,8,16,128]{3,2,1,0:T(8,128)(2,1)} %get-tuple-element.52), channel_id=1, source_target_pairs={{0,12},{1,13},{2,14},{3,15},{4,8},{5,9},{6,10},{7,11},{8,4},{9,5},... | collective-permute-start | bytes 196616 | tf_op jit(solution)/shard_map/ppermute | solution.py:495
  97.1 10.6 %collective-permute-start.15 = (bf16[2,8,16,128]{3,2,1,0:T(8,128)(2,1)}, bf16[2,8,16,128]{3,2,1,0:T(8,128)(2,1)S(1)}, u32[]{:S(2)}, u32[]{:S(2)}) collective-permute-start(bf16[2,8,16,128]{3,2,1,0:T(8,128)(2,1)} %get-tuple-element.47), channel_id=1, source_target_pairs={{0,4},{1,5},{2,6},{3,7},{4,0},{5,1},{6,2},{7,3},{8,12},{9,13},{10,... | collective-permute-start | bytes 196616 | tf_op jit(solution)/shard_map/ppermute | solution.py:495
  97.1 10.5 %collective-permute-start.17 = (bf16[2,8,16,128]{3,2,1,0:T(8,128)(2,1)}, bf16[2,8,16,128]{3,2,1,0:T(8,128)(2,1)S(1)}, u32[]{:S(2)}, u32[]{:S(2)}) collective-permute-start(bf16[2,8,16,128]{3,2,1,0:T(8,128)(2,1)} %get-tuple-element.49), channel_id=1, source_target_pairs={{0,8},{1,9},{2,10},{3,11},{4,12},{5,13},{6,14},{7,15},{8,0},{9,1},... | collective-permute-start | bytes 196616 | tf_op jit(solution)/shard_map/ppermute | solution.py:495
  99.2 8.5 %copy-start.15 = (bf16[2,8,16,128]{3,2,1,0:T(8,128)(2,1)}, bf16[2,8,16,128]{3,2,1,0:T(8,128)(2,1)S(1)}, u32[]{:S(2)}) copy-start(bf16[2,8,16,128]{3,2,1,0:T(8,128)(2,1)S(1)} %collective-permute-done.16.refs_3_) | copy-start | bytes 196612
  99.2 8.5 %collective-permute-start.19 = (bf16[2,8,16,128]{3,2,1,0:T(8,128)(2,1)}, bf16[2,8,16,128]{3,2,1,0:T(8,128)(2,1)S(1)}, u32[]{:S(2)}, u32[]{:S(2)}) collective-permute-start(bf16[2,8,16,128]{3,2,1,0:T(8,128)(2,1)} %get-tuple-element.51), channel_id=1, source_target_pairs={{0,12},{1,13},{2,14},{3,15},{4,8},{5,9},{6,10},{7,11},{8,4},{9,5},... | collective-permute-start | bytes 196616 | tf_op jit(solution)/shard_map/ppermute | solution.py:495
  107.6 0.6 copy-start.16
  107.6 0.6 copy-start.17
  107.7 0.6 copy-start.18
  107.7 0.7 copy-start.19
  107.7 0.6 copy-start.20

commit v2 on v1

--- a/solution.py
+++ b/solution.py
@@ -401,22 +401,24 @@
     blocks, chans, groups, distances, scale, per_step = sizes
     arrived = refs[: len(pieces)]
     outs = refs[len(pieces) : len(pieces) + blocks]
-    r_ref, p_ref, q_ref, sems = refs[len(pieces) + blocks :]
+    r_ref, p_ref, q_ref = refs[len(pieces) + blocks :]
     here = lax.axis_index("stn") if blocks > 1 else 0
     block_inputs = chans * r_ref.shape[2]
-    copies = []
-    for index, (dz, dc, mine, first) in enumerate(pieces):
-        chan = lax.bitwise_xor(lax.axis_index("chan"), dc)
-        block = lax.bitwise_xor(here, dz) if blocks > 1 else 0
-        start = first + lax.axis_index("stn") * mine if mine else first
-        copies.append(
-            pltpu.make_async_copy(
-                arrived[index].at[pl.ds(start, groups)], r_ref.at[block * chans + chan], sems.at[index]
-            )
-        )
-        copies[-1].start()
-    for copy in copies:
-        copy.wait()
+    together = math.gcd(groups, 8)
+
+    def collect(at, carry):
+        for index, (dz, dc, mine, first) in enumerate(pieces):
+            chan = lax.bitwise_xor(lax.axis_index("chan"), dc)
+            block = lax.bitwise_xor(here, dz) if blocks > 1 else 0
+            start = first + at * together
+            if mine:
+                start = start + lax.axis_index("stn") * mine
+            r_ref[block * chans + chan, pl.ds(at * together, together), :, :] = arrived[index][
+                pl.ds(start, together), :, :
+            ]
+        return carry
+
+    lax.fori_loop(0, groups // together, collect, 0)
 
     def some_groups(at, carry):
         for one in range(per_step):
@@ -438,7 +440,7 @@
     lax.fori_loop(0, groups // per_step, some_groups, 0)
 
 
-def correlate_pieces(arrays, pieces, blocks, chans, groups, distances, scale, stays):
+def correlate_pieces(arrays, pieces, blocks, chans, groups, distances, scale):
     inputs, wide = arrays[0].shape[1:]
     block_inputs = chans * inputs
     out_rows = block_inputs * block_inputs // LANES
@@ -448,14 +450,13 @@
     vmem = pl.BlockSpec(memory_space=pltpu.VMEM)
     return pl.pallas_call(
         functools.partial(pieces_kernel, sizes=sizes, pieces=pieces),
-        in_specs=[HBM if local else vmem for local in stays],
+        in_specs=[vmem] * len(arrays),
         out_specs=[vmem] * blocks,
         out_shape=[jax.ShapeDtypeStruct(shape, bf16)] * blocks,
         scratch_shapes=[
             pltpu.VMEM((blocks * chans, groups, inputs, wide), bf16),
             pltpu.VMEM((per_step, blocks * 2 * block_inputs, LANES), f32),
             pltpu.VMEM((per_step * blocks * len(distances), 2 * out_rows, LANES), f32),
-            pltpu.SemaphoreType.DMA((len(pieces),)),
         ],
     )(*arrays)
 
@@ -526,17 +527,15 @@
                 whole.append(shifted(value, stations, chans, 0, dc) if dc else value)
             else:
                 far[dz, dc] = shifted(value, stations, chans, dz, dc)
-        stays = [dc == 0 for dc in range(chans)]
         pieces = [(0, dc, 0, 0) for dc in range(chans)]
-        (own,) = correlate_pieces(whole, pieces, 1, chans, here * stations, (0,), scale, stays)
+        (own,) = correlate_pieces(whole, pieces, 1, chans, here * stations, (0,), scale)
         distances = tuple(range(1, reach))
         back = {}
         for chunk in range(CHUNKS):
             pieces = [(0, dc, here, chunk * part) for dc in range(chans)]
             pieces += [(dz, dc, 0, chunk * part) for dz, dc in far]
             arrays = whole + list(far.values())
-            inside = stays + [False] * len(far)
-            outs = correlate_pieces(arrays, pieces, stations, chans, part, distances, scale, inside)
+            outs = correlate_pieces(arrays, pieces, stations, chans, part, distances, scale)
             for dz in range(stations):
                 back[dz, chunk] = outs[0] if dz == 0 else shifted(outs[dz], stations, chans, dz, 0)
         out = assemble(

time: 111 us -> 107 us (0.964)
  Pallas kernels: 35.7 us -> 32.6 us
    pallas_call x3, Pallas kernels: 18.3 us -> 15.2 us  [correlate_pieces(): pl.pallas_call(functools.partial(pieces_kernel, sizes=sizes, pieces=piece...]
  transfers between devices with their start and end apart: 21 -> 21, of which waited for: 11 -> 11; matrix products, arithmetic and copies ran while one was open for 0% -> 0% of each run, Pallas kernels for 11% -> 10%
where the time goes in v2:
time: 107 us
  waiting for transfers between devices  37.4 us (35%)
  starting transfers between devices  35.2 us (33%)
  Pallas kernels  32.6 us (30%)
  local copies, waits for them, and re-layouts  1.73 us (2%)
    ppermute x21, waiting for transfers between devices, shifted(): return lax.ppermute(value, ('stn', 'chan'), pairs)  37.4 us
    ppermute x21, starting transfers between devices, shifted(): return lax.ppermute(value, ('stn', 'chan'), pairs)  35.2 us
    pallas_call x1, Pallas kernels, make_spectra(): pl.pallas_call(functools.partial(spectra_kernel, sizes=sizes, sends=sends...  15.4 us
    pallas_call x3, Pallas kernels, correlate_pieces(): pl.pallas_call(functools.partial(pieces_kernel, sizes=sizes, pieces=piece...  15.2 us
  transfers between devices with their start and end apart: 21, of which 11 were waited for; matrix products, arithmetic and copies ran while one was open for 0% of the time, Pallas kernels for 10%

profile of v2, /device:TPU:0, one launch (start us, length us, event | category | flops | bytes accessed | tf_op | source)
XLA Modules:
  0.0 107.1 jit_solution(14894980630728765388)
XLA Ops:
  0.0 15.4 %spectra.1 = (bf16[64,8,512]{2,1,0:T(8,128)(2,1)}, bf16[64,8,512]{2,1,0:T(8,128)(2,1)}, bf16[64,8,512]{2,1,0:T(8,128)(2,1)}, bf16[64,8,512]{2,1,0:T(8,128)(2,1)}...) custom-call(f32[528,128]{1,0:T(8,128)} %constant.4.clone.tw_ref, ...), custom_call_target="tpu_custom_call" | custom-call | tf_op jit(solution)/shard_map/spectra/pallas_call | solution.py:303
  15.4 3.5 %collective-permute-start.10 = (bf16[16,8,512]{2,1,0:T(8,128)(2,1)}, bf16[16,8,512]{2,1,0:T(8,128)(2,1)S(1)}, u32[]{:S(2)}, u32[]{:S(2)}) collective-permute-start(bf16[16,8,512]{2,1,0:T(8,128)(2,1)} %get-tuple-element.40), channel_id=1, source_target_pairs={{0,7},{1,6},{2,5},{3,4},{4,3},{5,2},{6,1},{7,0},{8,15},{9,14},{10,... | collective-permute-start | bytes 393224 | tf_op jit(solution)/shard_map/ppermute | solution.py:496
  18.9 2.5 %collective-permute-start.11 = (bf16[16,8,512]{2,1,0:T(8,128)(2,1)}, bf16[16,8,512]{2,1,0:T(8,128)(2,1)S(1)}, u32[]{:S(2)}, u32[]{:S(2)}) collective-permute-start(bf16[16,8,512]{2,1,0:T(8,128)(2,1)} %get-tuple-element.41), channel_id=1, source_target_pairs={{0,12},{1,13},{2,14},{3,15},{4,8},{5,9},{6,10},{7,11},{8,4},{9,5},... | collective-permute-start | bytes 393224 | tf_op jit(solution)/shard_map/ppermute | solution.py:496
  21.4 1.3 %collective-permute-start.12 = (bf16[16,8,512]{2,1,0:T(8,128)(2,1)}, bf16[16,8,512]{2,1,0:T(8,128)(2,1)S(1)}, u32[]{:S(2)}, u32[]{:S(2)}) collective-permute-start(bf16[16,8,512]{2,1,0:T(8,128)(2,1)} %get-tuple-element.42), channel_id=1, source_target_pairs={{0,13},{1,12},{2,15},{3,14},{4,9},{5,8},{6,11},{7,10},{8,5},{9,4},... | collective-permute-start | bytes 393224 | tf_op jit(solution)/shard_map/ppermute | solution.py:496
  22.7 2.4 %collective-permute-start.13 = (bf16[16,8,512]{2,1,0:T(8,128)(2,1)}, bf16[16,8,512]{2,1,0:T(8,128)(2,1)S(1)}, u32[]{:S(2)}, u32[]{:S(2)}) collective-permute-start(bf16[16,8,512]{2,1,0:T(8,128)(2,1)} %get-tuple-element.43), channel_id=1, source_target_pairs={{0,14},{1,15},{2,12},{3,13},{4,10},{5,11},{6,8},{7,9},{8,6},{9,7},... | collective-permute-start | bytes 393224 | tf_op jit(solution)/shard_map/ppermute | solution.py:496
  25.2 1.7 %collective-permute-start.14 = (bf16[16,8,512]{2,1,0:T(8,128)(2,1)}, bf16[16,8,512]{2,1,0:T(8,128)(2,1)S(1)}, u32[]{:S(2)}, u32[]{:S(2)}) collective-permute-start(bf16[16,8,512]{2,1,0:T(8,128)(2,1)} %get-tuple-element.44), channel_id=1, source_target_pairs={{0,15},{1,14},{2,13},{3,12},{4,11},{5,10},{6,9},{7,8},{8,7},{9,6},... | collective-permute-start | bytes 393224 | tf_op jit(solution)/shard_map/ppermute | solution.py:496
  26.9 0.0 collective-permute-done.10.refs_11_
  26.9 0.0 collective-permute-start.3
  26.9 1.9 %collective-permute-done.11.refs_12_ = bf16[16,8,512]{2,1,0:T(8,128)(2,1)S(1)} collective-permute-done((bf16[16,8,512]{2,1,0:T(8,128)(2,1)}, bf16[16,8,512]{2,1,0:T(8,128)(2,1)S(1)}, u32[]{:S(2)}, u32[]{:S(2)}) %collective-permute-start.11) | collective-permute-done | bytes 131104 | tf_op jit(solution)/shard_map/ppermute | solution.py:496
  28.8 0.0 collective-permute-start
  28.9 2.7 %collective-permute-done.12.refs_13_ = bf16[16,8,512]{2,1,0:T(8,128)(2,1)S(1)} collective-permute-done((bf16[16,8,512]{2,1,0:T(8,128)(2,1)}, bf16[16,8,512]{2,1,0:T(8,128)(2,1)S(1)}, u32[]{:S(2)}, u32[]{:S(2)}) %collective-permute-start.12) | collective-permute-done | bytes 131104 | tf_op jit(solution)/shard_map/ppermute | solution.py:496
  31.6 0.4 collective-permute-start.1
  32.0 2.6 %collective-permute-done.13.refs_14_ = bf16[16,8,512]{2,1,0:T(8,128)(2,1)S(1)} collective-permute-done((bf16[16,8,512]{2,1,0:T(8,128)(2,1)}, bf16[16,8,512]{2,1,0:T(8,128)(2,1)S(1)}, u32[]{:S(2)}, u32[]{:S(2)}) %collective-permute-start.13) | collective-permute-done | bytes 131104 | tf_op jit(solution)/shard_map/ppermute | solution.py:496
  34.6 1.0 collective-permute-start.2
  35.5 1.6 %collective-permute-done.14.refs_15_ = bf16[16,8,512]{2,1,0:T(8,128)(2,1)S(1)} collective-permute-done((bf16[16,8,512]{2,1,0:T(8,128)(2,1)}, bf16[16,8,512]{2,1,0:T(8,128)(2,1)S(1)}, u32[]{:S(2)}, u32[]{:S(2)}) %collective-permute-start.14) | collective-permute-done | bytes 131104 | tf_op jit(solution)/shard_map/ppermute | solution.py:496
  37.2 12.8 %collective-permute-start.4 = (bf16[16,8,512]{2,1,0:T(8,128)(2,1)}, bf16[16,8,512]{2,1,0:T(8,128)(2,1)S(1)}, u32[]{:S(2)}, u32[]{:S(2)}) collective-permute-start(bf16[16,8,512]{2,1,0:T(8,128)(2,1)} %get-tuple-element.34), channel_id=1, source_target_pairs={{0,9},{1,8},{2,11},{3,10},{4,13},{5,12},{6,15},{7,14},{8,1},{9,0},... | collective-permute-start | bytes 393224 | tf_op jit(solution)/shard_map/ppermute | solution.py:496
  50.0 1.4 %collective-permute-done.3.refs_4_ = bf16[16,8,512]{2,1,0:T(8,128)(2,1)S(1)} collective-permute-done((bf16[16,8,512]{2,1,0:T(8,128)(2,1)}, bf16[16,8,512]{2,1,0:T(8,128)(2,1)S(1)}, u32[]{:S(2)}, u32[]{:S(2)}) %collective-permute-start.3) | collective-permute-done | bytes 131104 | tf_op jit(solution)/shard_map/ppermute | solution.py:496
  51.3 0.0 collective-permute-start.5
  51.3 8.2 %collective-permute-done.4.refs_5_ = bf16[16,8,512]{2,1,0:T(8,128)(2,1)S(1)} collective-permute-done((bf16[16,8,512]{2,1,0:T(8,128)(2,1)}, bf16[16,8,512]{2,1,0:T(8,128)(2,1)S(1)}, u32[]{:S(2)}, u32[]{:S(2)}) %collective-permute-start.4) | collective-permute-done | bytes 131104 | tf_op jit(solution)/shard_map/ppermute | solution.py:496
  59.5 0.3 collective-permute-start.6
  59.8 3.8 %collective-permute-done.5.refs_6_ = bf16[16,8,512]{2,1,0:T(8,128)(2,1)S(1)} collective-permute-done((bf16[16,8,512]{2,1,0:T(8,128)(2,1)}, bf16[16,8,512]{2,1,0:T(8,128)(2,1)S(1)}, u32[]{:S(2)}, u32[]{:S(2)}) %collective-permute-start.5) | collective-permute-done | bytes 131104 | tf_op jit(solution)/shard_map/ppermute | solution.py:496
  63.6 0.0 collective-permute-start.7
  63.6 6.2 %collective-permute-done.6.refs_7_ = bf16[16,8,512]{2,1,0:T(8,128)(2,1)S(1)} collective-permute-done((bf16[16,8,512]{2,1,0:T(8,128)(2,1)}, bf16[16,8,512]{2,1,0:T(8,128)(2,1)S(1)}, u32[]{:S(2)}, u32[]{:S(2)}) %collective-permute-start.6) | collective-permute-done | bytes 131104 | tf_op jit(solution)/shard_map/ppermute | solution.py:496
  69.8 0.0 collective-permute-start.8
  69.8 1.9 %collective-permute-done.7.refs_8_ = bf16[16,8,512]{2,1,0:T(8,128)(2,1)S(1)} collective-permute-done((bf16[16,8,512]{2,1,0:T(8,128)(2,1)}, bf16[16,8,512]{2,1,0:T(8,128)(2,1)S(1)}, u32[]{:S(2)}, u32[]{:S(2)}) %collective-permute-start.7) | collective-permute-done | bytes 131104 | tf_op jit(solution)/shard_map/ppermute | solution.py:496
  71.7 0.4 collective-permute-start.9
  72.1 3.5 %collective-permute-done.8.refs_9_ = bf16[16,8,512]{2,1,0:T(8,128)(2,1)S(1)} collective-permute-done((bf16[16,8,512]{2,1,0:T(8,128)(2,1)}, bf16[16,8,512]{2,1,0:T(8,128)(2,1)S(1)}, u32[]{:S(2)}, u32[]{:S(2)}) %collective-permute-start.8) | collective-permute-done | bytes 131104 | tf_op jit(solution)/shard_map/ppermute | solution.py:496
  75.6 3.6 %collective-permute-done.9.refs_10_ = bf16[16,8,512]{2,1,0:T(8,128)(2,1)S(1)} collective-permute-done((bf16[16,8,512]{2,1,0:T(8,128)(2,1)}, bf16[16,8,512]{2,1,0:T(8,128)(2,1)S(1)}, u32[]{:S(2)}, u32[]{:S(2)}) %collective-permute-start.9) | collective-permute-done | bytes 131104 | tf_op jit(solution)/shard_map/ppermute | solution.py:496
  79.2 0.0 collective-permute-done.refs_1_
  79.4 0.5 copy-done.14
  79.9 0.2 copy-done
  80.1 0.2 copy-done.1
  80.3 0.1 copy-done.2
  80.4 4.9 %shard_map.48 = (bf16[2,8,16,128]{3,2,1,0:T(8,128)(2,1)}, bf16[2,8,16,128]{3,2,1,0:T(8,128)(2,1)}, bf16[2,8,16,128]{3,2,1,0:T(8,128)(2,1)}, bf16[2,8,16,128]{3,2,1,0:T(8,128)(2,1)}) custom-call(bf16[64,8,512]{2,1,0:T(8,128)(2,1)} %get-tuple-element.29.refs_0_, bf16[64,8,512]{2,1,0:T(8,128)(2,1)} %copy-done, bf16[64,8,512]{2,1,0:T(8,128)(2,1)} %copy-done.1, ...), custom_call_target="tpu_custom_call" | custom-call | tf_op jit(solution)/shard_map/pallas_call | solution.py:451
  85.3 0.2 collective-permute-start.16
  85.5 1.9 %collective-permute-start.18 = (bf16[2,8,16,128]{3,2,1,0:T(8,128)(2,1)}, bf16[2,8,16,128]{3,2,1,0:T(8,128)(2,1)S(1)}, u32[]{:S(2)}, u32[]{:S(2)}) collective-permute-start(bf16[2,8,16,128]{3,2,1,0:T(8,128)(2,1)} %get-tuple-element.50), channel_id=1, source_target_pairs={{0,8},{1,9},{2,10},{3,11},{4,12},{5,13},{6,14},{7,15},{8,0},{9,1},... | collective-permute-start | bytes 196616 | tf_op jit(solution)/shard_map/ppermute | solution.py:496
  87.4 2.3 %collective-permute-start.20 = (bf16[2,8,16,128]{3,2,1,0:T(8,128)(2,1)}, bf16[2,8,16,128]{3,2,1,0:T(8,128)(2,1)S(1)}, u32[]{:S(2)}, u32[]{:S(2)}) collective-permute-start(bf16[2,8,16,128]{3,2,1,0:T(8,128)(2,1)} %get-tuple-element.52), channel_id=1, source_target_pairs={{0,12},{1,13},{2,14},{3,15},{4,8},{5,9},{6,10},{7,11},{8,4},{9,5},... | collective-permute-start | bytes 196616 | tf_op jit(solution)/shard_map/ppermute | solution.py:496
  89.7 4.9 %shard_map.47 = (bf16[2,8,16,128]{3,2,1,0:T(8,128)(2,1)}, bf16[2,8,16,128]{3,2,1,0:T(8,128)(2,1)}, bf16[2,8,16,128]{3,2,1,0:T(8,128)(2,1)}, bf16[2,8,16,128]{3,2,1,0:T(8,128)(2,1)}) custom-call(bf16[64,8,512]{2,1,0:T(8,128)(2,1)} %get-tuple-element.29.refs_0_, bf16[64,8,512]{2,1,0:T(8,128)(2,1)} %copy-done, bf16[64,8,512]{2,1,0:T(8,128)(2,1)} %copy-done.1, ...), custom_call_target="tpu_custom_call" | custom-call | tf_op jit(solution)/shard_map/pallas_call | solution.py:451
  94.6 2.1 %collective-permute-start.17 = (bf16[2,8,16,128]{3,2,1,0:T(8,128)(2,1)}, bf16[2,8,16,128]{3,2,1,0:T(8,128)(2,1)S(1)}, u32[]{:S(2)}, u32[]{:S(2)}) collective-permute-start(bf16[2,8,16,128]{3,2,1,0:T(8,128)(2,1)} %get-tuple-element.49), channel_id=1, source_target_pairs={{0,8},{1,9},{2,10},{3,11},{4,12},{5,13},{6,14},{7,15},{8,0},{9,1},... | collective-permute-start | bytes 196616 | tf_op jit(solution)/shard_map/ppermute | solution.py:496
  96.7 2.3 %collective-permute-start.19 = (bf16[2,8,16,128]{3,2,1,0:T(8,128)(2,1)}, bf16[2,8,16,128]{3,2,1,0:T(8,128)(2,1)S(1)}, u32[]{:S(2)}, u32[]{:S(2)}) collective-permute-start(bf16[2,8,16,128]{3,2,1,0:T(8,128)(2,1)} %get-tuple-element.51), channel_id=1, source_target_pairs={{0,12},{1,13},{2,14},{3,15},{4,8},{5,9},{6,10},{7,11},{8,4},{9,5},... | collective-permute-start | bytes 196616 | tf_op jit(solution)/shard_map/ppermute | solution.py:496
  99.0 5.4 %shard_map.46.own_ref = bf16[1,64,16,128]{3,2,1,0:T(8,128)(2,1)} custom-call(bf16[64,8,512]{2,1,0:T(8,128)(2,1)} %get-tuple-element.29.refs_0_, bf16[64,8,512]{2,1,0:T(8,128)(2,1)} %copy-done, bf16[64,8,512]{2,1,0:T(8,128)(2,1)} %copy-done.1, bf16[64,8,512]{2,1,0:T(8,128)(2,1)} %copy-done.2), custom_call_target="tpu_custom_call" | custom-call | tf_op jit(solution)/shard_map/pallas_call | solution.py:451
  104.4 0.0 collective-permute-done.20.refs_7_
  104.4 0.0 collective-permute-done.19.refs_6_
  104.4 0.5 copy-done.16
  105.0 0.0 copy-done.17
  105.0 0.0 copy-done.18
  105.0 0.0 copy-done.19
  105.1 2.0 %assemble.1 = bf16[3,64,16,128]{3,2,1,0:T(8,128)(2,1)} custom-call(bf16[1,64,16,128]{3,2,1,0:T(8,128)(2,1)} %shard_map.46.own_ref, bf16[2,8,16,128]{3,2,1,0:T(8,128)(2,1)} %get-tuple-element.45.refs_0_, bf16[2,8,16,128]{3,2,1,0:T(8,128)(2,1)} %get-tuple-element.46.refs_1_, bf16[2,8,16,128]{3,2,1,0:T(8,128)(2,1)} %copy-done.18, ...), custom_call_target="tpu_custom_call" | custom-call | tf_op jit(solution)/shard_map/assemble/pallas_call | solution.py:481
  (41 shorter events, 0.1 us)
Async XLA Ops:
  15.4 11.5 %collective-permute-start.10 = (bf16[16,8,512]{2,1,0:T(8,128)(2,1)}, bf16[16,8,512]{2,1,0:T(8,128)(2,1)S(1)}, u32[]{:S(2)}, u32[]{:S(2)}) collective-permute-start(bf16[16,8,512]{2,1,0:T(8,128)(2,1)} %get-tuple-element.40), channel_id=1, source_target_pairs={{0,7},{1,6},{2,5},{3,4},{4,3},{5,2},{6,1},{7,0},{8,15},{9,14},{10,... | collective-permute-start | bytes 393224 | tf_op jit(solution)/shard_map/ppermute | solution.py:496
  18.9 9.9 %collective-permute-start.11 = (bf16[16,8,512]{2,1,0:T(8,128)(2,1)}, bf16[16,8,512]{2,1,0:T(8,128)(2,1)S(1)}, u32[]{:S(2)}, u32[]{:S(2)}) collective-permute-start(bf16[16,8,512]{2,1,0:T(8,128)(2,1)} %get-tuple-element.41), channel_id=1, source_target_pairs={{0,12},{1,13},{2,14},{3,15},{4,8},{5,9},{6,10},{7,11},{8,4},{9,5},... | collective-permute-start | bytes 393224 | tf_op jit(solution)/shard_map/ppermute | solution.py:496
  21.4 10.2 %collective-permute-start.12 = (bf16[16,8,512]{2,1,0:T(8,128)(2,1)}, bf16[16,8,512]{2,1,0:T(8,128)(2,1)S(1)}, u32[]{:S(2)}, u32[]{:S(2)}) collective-permute-start(bf16[16,8,512]{2,1,0:T(8,128)(2,1)} %get-tuple-element.42), channel_id=1, source_target_pairs={{0,13},{1,12},{2,15},{3,14},{4,9},{5,8},{6,11},{7,10},{8,5},{9,4},... | collective-permute-start | bytes 393224 | tf_op jit(solution)/shard_map/ppermute | solution.py:496
  22.7 11.9 %collective-permute-start.13 = (bf16[16,8,512]{2,1,0:T(8,128)(2,1)}, bf16[16,8,512]{2,1,0:T(8,128)(2,1)S(1)}, u32[]{:S(2)}, u32[]{:S(2)}) collective-permute-start(bf16[16,8,512]{2,1,0:T(8,128)(2,1)} %get-tuple-element.43), channel_id=1, source_target_pairs={{0,14},{1,15},{2,12},{3,13},{4,10},{5,11},{6,8},{7,9},{8,6},{9,7},... | collective-permute-start | bytes 393224 | tf_op jit(solution)/shard_map/ppermute | solution.py:496
  25.2 12.0 %collective-permute-start.14 = (bf16[16,8,512]{2,1,0:T(8,128)(2,1)}, bf16[16,8,512]{2,1,0:T(8,128)(2,1)S(1)}, u32[]{:S(2)}, u32[]{:S(2)}) collective-permute-start(bf16[16,8,512]{2,1,0:T(8,128)(2,1)} %get-tuple-element.44), channel_id=1, source_target_pairs={{0,15},{1,14},{2,13},{3,12},{4,11},{5,10},{6,9},{7,8},{8,7},{9,6},... | collective-permute-start | bytes 393224 | tf_op jit(solution)/shard_map/ppermute | solution.py:496
  26.9 52.4 %copy-start.3 = (bf16[16,8,512]{2,1,0:T(8,128)(2,1)}, bf16[16,8,512]{2,1,0:T(8,128)(2,1)S(1)}, u32[]{:S(2)}) copy-start(bf16[16,8,512]{2,1,0:T(8,128)(2,1)S(1)} %collective-permute-done.10.refs_11_) | copy-start | bytes 393220
  26.9 24.5 %collective-permute-start.3 = (bf16[16,8,512]{2,1,0:T(8,128)(2,1)}, bf16[16,8,512]{2,1,0:T(8,128)(2,1)S(1)}, u32[]{:S(2)}, u32[]{:S(2)}) collective-permute-start(bf16[16,8,512]{2,1,0:T(8,128)(2,1)} %get-tuple-element.33), channel_id=1, source_target_pairs={{0,8},{1,9},{2,10},{3,11},{4,12},{5,13},{6,14},{7,15},{8,0},{9,1},... | collective-permute-start | bytes 393224 | tf_op jit(solution)/shard_map/ppermute | solution.py:496
  28.8 50.4 %copy-start.4 = (bf16[16,8,512]{2,1,0:T(8,128)(2,1)}, bf16[16,8,512]{2,1,0:T(8,128)(2,1)S(1)}, u32[]{:S(2)}) copy-start(bf16[16,8,512]{2,1,0:T(8,128)(2,1)S(1)} %collective-permute-done.11.refs_12_) | copy-start | bytes 393220
  28.8 50.4 %collective-permute-start = (bf16[64,8,512]{2,1,0:T(8,128)(2,1)}, bf16[64,8,512]{2,1,0:T(8,128)(2,1)S(1)}, u32[]{:S(2)}, u32[]{:S(2)}) collective-permute-start(bf16[64,8,512]{2,1,0:T(8,128)(2,1)} %get-tuple-element.30), channel_id=1, source_target_pairs={{0,1},{1,0},{2,3},{3,2},{4,5},{5,4},{6,7},{7,6},{8,9},{9,8},{10,11... | collective-permute-start | bytes 1572872 | tf_op jit(solution)/shard_map/ppermute | solution.py:496
  31.6 47.7 %copy-start.5 = (bf16[16,8,512]{2,1,0:T(8,128)(2,1)}, bf16[16,8,512]{2,1,0:T(8,128)(2,1)S(1)}, u32[]{:S(2)}) copy-start(bf16[16,8,512]{2,1,0:T(8,128)(2,1)S(1)} %collective-permute-done.12.refs_13_) | copy-start | bytes 393220
  31.6 47.6 %collective-permute-start.1 = (bf16[64,8,512]{2,1,0:T(8,128)(2,1)}, bf16[64,8,512]{2,1,0:T(8,128)(2,1)S(1)}, u32[]{:S(2)}, u32[]{:S(2)}) collective-permute-start(bf16[64,8,512]{2,1,0:T(8,128)(2,1)} %get-tuple-element.31), channel_id=1, source_target_pairs={{0,2},{1,3},{2,0},{3,1},{4,6},{5,7},{6,4},{7,5},{8,10},{9,11},{10,... | collective-permute-start | bytes 1572872 | tf_op jit(solution)/shard_map/ppermute | solution.py:496
  34.6 44.7 %copy-start.6 = (bf16[16,8,512]{2,1,0:T(8,128)(2,1)}, bf16[16,8,512]{2,1,0:T(8,128)(2,1)S(1)}, u32[]{:S(2)}) copy-start(bf16[16,8,512]{2,1,0:T(8,128)(2,1)S(1)} %collective-permute-done.13.refs_14_) | copy-start | bytes 393220
  34.6 44.7 %collective-permute-start.2 = (bf16[64,8,512]{2,1,0:T(8,128)(2,1)}, bf16[64,8,512]{2,1,0:T(8,128)(2,1)S(1)}, u32[]{:S(2)}, u32[]{:S(2)}) collective-permute-start(bf16[64,8,512]{2,1,0:T(8,128)(2,1)} %get-tuple-element.32), channel_id=1, source_target_pairs={{0,3},{1,2},{2,1},{3,0},{4,7},{5,6},{6,5},{7,4},{8,11},{9,10},{10,... | collective-permute-start | bytes 1572872 | tf_op jit(solution)/shard_map/ppermute | solution.py:496
  37.2 42.1 %copy-start.7 = (bf16[16,8,512]{2,1,0:T(8,128)(2,1)}, bf16[16,8,512]{2,1,0:T(8,128)(2,1)S(1)}, u32[]{:S(2)}) copy-start(bf16[16,8,512]{2,1,0:T(8,128)(2,1)S(1)} %collective-permute-done.14.refs_15_) | copy-start | bytes 393220
  37.2 22.4 %collective-permute-start.4 = (bf16[16,8,512]{2,1,0:T(8,128)(2,1)}, bf16[16,8,512]{2,1,0:T(8,128)(2,1)S(1)}, u32[]{:S(2)}, u32[]{:S(2)}) collective-permute-start(bf16[16,8,512]{2,1,0:T(8,128)(2,1)} %get-tuple-element.34), channel_id=1, source_target_pairs={{0,9},{1,8},{2,11},{3,10},{4,13},{5,12},{6,15},{7,14},{8,1},{9,0},... | collective-permute-start | bytes 393224 | tf_op jit(solution)/shard_map/ppermute | solution.py:496
  51.3 28.0 %copy-start.8 = (bf16[16,8,512]{2,1,0:T(8,128)(2,1)}, bf16[16,8,512]{2,1,0:T(8,128)(2,1)S(1)}, u32[]{:S(2)}) copy-start(bf16[16,8,512]{2,1,0:T(8,128)(2,1)S(1)} %collective-permute-done.3.refs_4_) | copy-start | bytes 393220
  51.3 12.2 %collective-permute-start.5 = (bf16[16,8,512]{2,1,0:T(8,128)(2,1)}, bf16[16,8,512]{2,1,0:T(8,128)(2,1)S(1)}, u32[]{:S(2)}, u32[]{:S(2)}) collective-permute-start(bf16[16,8,512]{2,1,0:T(8,128)(2,1)} %get-tuple-element.35), channel_id=1, source_target_pairs={{0,10},{1,11},{2,8},{3,9},{4,14},{5,15},{6,12},{7,13},{8,2},{9,3},... | collective-permute-start | bytes 393224 | tf_op jit(solution)/shard_map/ppermute | solution.py:496
  59.5 19.8 %copy-start.9 = (bf16[16,8,512]{2,1,0:T(8,128)(2,1)}, bf16[16,8,512]{2,1,0:T(8,128)(2,1)S(1)}, u32[]{:S(2)}) copy-start(bf16[16,8,512]{2,1,0:T(8,128)(2,1)S(1)} %collective-permute-done.4.refs_5_) | copy-start | bytes 393220
  59.5 10.3 %collective-permute-start.6 = (bf16[16,8,512]{2,1,0:T(8,128)(2,1)}, bf16[16,8,512]{2,1,0:T(8,128)(2,1)S(1)}, u32[]{:S(2)}, u32[]{:S(2)}) collective-permute-start(bf16[16,8,512]{2,1,0:T(8,128)(2,1)} %get-tuple-element.36), channel_id=1, source_target_pairs={{0,11},{1,10},{2,9},{3,8},{4,15},{5,14},{6,13},{7,12},{8,3},{9,2},... | collective-permute-start | bytes 393224 | tf_op jit(solution)/shard_map/ppermute | solution.py:496
  63.6 15.7 %copy-start.10 = (bf16[16,8,512]{2,1,0:T(8,128)(2,1)}, bf16[16,8,512]{2,1,0:T(8,128)(2,1)S(1)}, u32[]{:S(2)}) copy-start(bf16[16,8,512]{2,1,0:T(8,128)(2,1)S(1)} %collective-permute-done.5.refs_6_) | copy-start | bytes 393220
  63.6 8.1 %collective-permute-start.7 = (bf16[16,8,512]{2,1,0:T(8,128)(2,1)}, bf16[16,8,512]{2,1,0:T(8,128)(2,1)S(1)}, u32[]{:S(2)}, u32[]{:S(2)}) collective-permute-start(bf16[16,8,512]{2,1,0:T(8,128)(2,1)} %get-tuple-element.37), channel_id=1, source_target_pairs={{0,4},{1,5},{2,6},{3,7},{4,0},{5,1},{6,2},{7,3},{8,12},{9,13},{10,... | collective-permute-start | bytes 393224 | tf_op jit(solution)/shard_map/ppermute | solution.py:496
  69.8 9.5 %copy-start.11 = (bf16[16,8,512]{2,1,0:T(8,128)(2,1)}, bf16[16,8,512]{2,1,0:T(8,128)(2,1)S(1)}, u32[]{:S(2)}) copy-start(bf16[16,8,512]{2,1,0:T(8,128)(2,1)S(1)} %collective-permute-done.6.refs_7_) | copy-start | bytes 393220
  69.8 5.8 %collective-permute-start.8 = (bf16[16,8,512]{2,1,0:T(8,128)(2,1)}, bf16[16,8,512]{2,1,0:T(8,128)(2,1)S(1)}, u32[]{:S(2)}, u32[]{:S(2)}) collective-permute-start(bf16[16,8,512]{2,1,0:T(8,128)(2,1)} %get-tuple-element.38), channel_id=1, source_target_pairs={{0,5},{1,4},{2,7},{3,6},{4,1},{5,0},{6,3},{7,2},{8,13},{9,12},{10,... | collective-permute-start | bytes 393224 | tf_op jit(solution)/shard_map/ppermute | solution.py:496
  71.7 7.6 %copy-start.12 = (bf16[16,8,512]{2,1,0:T(8,128)(2,1)}, bf16[16,8,512]{2,1,0:T(8,128)(2,1)S(1)}, u32[]{:S(2)}) copy-start(bf16[16,8,512]{2,1,0:T(8,128)(2,1)S(1)} %collective-permute-done.7.refs_8_) | copy-start | bytes 393220
  71.7 7.5 %collective-permute-start.9 = (bf16[16,8,512]{2,1,0:T(8,128)(2,1)}, bf16[16,8,512]{2,1,0:T(8,128)(2,1)S(1)}, u32[]{:S(2)}, u32[]{:S(2)}) collective-permute-start(bf16[16,8,512]{2,1,0:T(8,128)(2,1)} %get-tuple-element.39), channel_id=1, source_target_pairs={{0,6},{1,7},{2,4},{3,5},{4,2},{5,3},{6,0},{7,1},{8,14},{9,15},{10,... | collective-permute-start | bytes 393224 | tf_op jit(solution)/shard_map/ppermute | solution.py:496
  75.6 3.8 %copy-start.13 = (bf16[16,8,512]{2,1,0:T(8,128)(2,1)}, bf16[16,8,512]{2,1,0:T(8,128)(2,1)S(1)}, u32[]{:S(2)}) copy-start(bf16[16,8,512]{2,1,0:T(8,128)(2,1)S(1)} %collective-permute-done.8.refs_9_) | copy-start | bytes 393220
  79.2 0.7 copy-start.14
  79.2 0.8 copy-start
  79.2 1.0 copy-start.1
  79.2 1.2 %copy-start.2 = (bf16[64,8,512]{2,1,0:T(8,128)(2,1)}, bf16[64,8,512]{2,1,0:T(8,128)(2,1)S(1)}, u32[]{:S(2)}) copy-start(bf16[64,8,512]{2,1,0:T(8,128)(2,1)S(1)} %collective-permute-done.2.refs_3_) | copy-start | bytes 1572868
  85.3 11.4 %collective-permute-start.16 = (bf16[2,8,16,128]{3,2,1,0:T(8,128)(2,1)}, bf16[2,8,16,128]{3,2,1,0:T(8,128)(2,1)S(1)}, u32[]{:S(2)}, u32[]{:S(2)}) collective-permute-start(bf16[2,8,16,128]{3,2,1,0:T(8,128)(2,1)} %get-tuple-element.48), channel_id=1, source_target_pairs={{0,4},{1,5},{2,6},{3,7},{4,0},{5,1},{6,2},{7,3},{8,12},{9,13},{10,... | collective-permute-start | bytes 196616 | tf_op jit(solution)/shard_map/ppermute | solution.py:496
  85.5 18.8 %collective-permute-start.18 = (bf16[2,8,16,128]{3,2,1,0:T(8,128)(2,1)}, bf16[2,8,16,128]{3,2,1,0:T(8,128)(2,1)S(1)}, u32[]{:S(2)}, u32[]{:S(2)}) collective-permute-start(bf16[2,8,16,128]{3,2,1,0:T(8,128)(2,1)} %get-tuple-element.50), channel_id=1, source_target_pairs={{0,8},{1,9},{2,10},{3,11},{4,12},{5,13},{6,14},{7,15},{8,0},{9,1},... | collective-permute-start | bytes 196616 | tf_op jit(solution)/shard_map/ppermute | solution.py:496
  87.4 16.9 %collective-permute-start.20 = (bf16[2,8,16,128]{3,2,1,0:T(8,128)(2,1)}, bf16[2,8,16,128]{3,2,1,0:T(8,128)(2,1)S(1)}, u32[]{:S(2)}, u32[]{:S(2)}) collective-permute-start(bf16[2,8,16,128]{3,2,1,0:T(8,128)(2,1)} %get-tuple-element.52), channel_id=1, source_target_pairs={{0,12},{1,13},{2,14},{3,15},{4,8},{5,9},{6,10},{7,11},{8,4},{9,5},... | collective-permute-start | bytes 196616 | tf_op jit(solution)/shard_map/ppermute | solution.py:496
  94.6 9.8 %collective-permute-start.15 = (bf16[2,8,16,128]{3,2,1,0:T(8,128)(2,1)}, bf16[2,8,16,128]{3,2,1,0:T(8,128)(2,1)S(1)}, u32[]{:S(2)}, u32[]{:S(2)}) collective-permute-start(bf16[2,8,16,128]{3,2,1,0:T(8,128)(2,1)} %get-tuple-element.47), channel_id=1, source_target_pairs={{0,4},{1,5},{2,6},{3,7},{4,0},{5,1},{6,2},{7,3},{8,12},{9,13},{10,... | collective-permute-start | bytes 196616 | tf_op jit(solution)/shard_map/ppermute | solution.py:496
  94.6 9.8 %collective-permute-start.17 = (bf16[2,8,16,128]{3,2,1,0:T(8,128)(2,1)}, bf16[2,8,16,128]{3,2,1,0:T(8,128)(2,1)S(1)}, u32[]{:S(2)}, u32[]{:S(2)}) collective-permute-start(bf16[2,8,16,128]{3,2,1,0:T(8,128)(2,1)} %get-tuple-element.49), channel_id=1, source_target_pairs={{0,8},{1,9},{2,10},{3,11},{4,12},{5,13},{6,14},{7,15},{8,0},{9,1},... | collective-permute-start | bytes 196616 | tf_op jit(solution)/shard_map/ppermute | solution.py:496
  96.7 7.7 %copy-start.15 = (bf16[2,8,16,128]{3,2,1,0:T(8,128)(2,1)}, bf16[2,8,16,128]{3,2,1,0:T(8,128)(2,1)S(1)}, u32[]{:S(2)}) copy-start(bf16[2,8,16,128]{3,2,1,0:T(8,128)(2,1)S(1)} %collective-permute-done.16.refs_3_) | copy-start | bytes 196612
  96.7 7.7 %collective-permute-start.19 = (bf16[2,8,16,128]{3,2,1,0:T(8,128)(2,1)}, bf16[2,8,16,128]{3,2,1,0:T(8,128)(2,1)S(1)}, u32[]{:S(2)}, u32[]{:S(2)}) collective-permute-start(bf16[2,8,16,128]{3,2,1,0:T(8,128)(2,1)} %get-tuple-element.51), channel_id=1, source_target_pairs={{0,12},{1,13},{2,14},{3,15},{4,8},{5,9},{6,10},{7,11},{8,4},{9,5},... | collective-permute-start | bytes 196616 | tf_op jit(solution)/shard_map/ppermute | solution.py:496
  104.4 0.6 copy-start.16
  104.4 0.6 copy-start.17
  104.4 0.6 copy-start.18
  104.4 0.7 copy-start.19
  104.4 0.6 copy-start.20

commit v3 on v2

--- a/solution.py
+++ b/solution.py
@@ -118,10 +118,11 @@
 SKEW = SUB + 1
 
 
-def spectra_kernel(tw_ref, t_ref, x_ref, taps_ref, *refs, sizes, sends, turned):
-    inputs, frames, tiles, per_step, spectra_count, tap_count, stations, chans = sizes
-    outs = refs[: len(sends)]
-    w_ref, a_ref, f_ref, xp_ref, s_ref, z_ref, sems = refs[len(sends) :]
+def spectra_kernel(tw_ref, t_ref, x_ref, taps_ref, *refs, sizes, sends, merged, turned):
+    inputs, first_frame, tiles, per_step, spectra_count, tap_count, stations, chans = sizes
+    earlier = refs[: len(merged)]
+    outs = refs[len(merged) : len(merged) + len(sends)]
+    w_ref, a_ref, f_ref, xp_ref, s_ref, z_ref, sems = refs[len(merged) + len(sends) :]
     half = tiles // 2
     kept = LANES // 2
     rows = (half + 1) * spectra_count
@@ -132,7 +133,8 @@
 
     def one_tile(here, carry):
         lanes = pl.ds(pl.multiple_of(here * LANES, LANES), LANES)
-        x = [x_ref[frame, :, lanes].astype(f32) for frame in range(frames)]
+        frames = range(first_frame, first_frame + spectra_count + tap_count - 1)
+        x = [x_ref[frame, :, lanes].astype(f32) for frame in frames]
         weights = [jnp.broadcast_to(taps_ref[t : t + 1, lanes], (inputs, LANES)) for t in range(tap_count)]
         at = (step * per_step + here) * SUB
         for s, total in enumerate(filtered(x, weights, spectra_count)):
@@ -202,25 +204,23 @@
                 high = value.astype(bf16)
                 xp_ref[:, c * LANES : (c + 1) * LANES] = high
                 xp_ref[:, (2 + c) * LANES : (3 + c) * LANES] = (value - high.astype(f32)).astype(bf16)
-            for j in range(parts):
-                if j < parts // 2:
-                    first = j * block
-                    which = 0
-                else:
-                    first = ((parts - 1 - j) * AVG + 1) * spectra_count
-                    which = 1
-                high = xp_ref[first : first + block, : 2 * LANES]
-                low = xp_ref[first : first + block, 2 * LANES :]
-                dims = (((1,), (1,)), ((), ()))
+            dims = (((1,), (1,)), ((), ()))
+            for which in range(2):
+                first = which * spectra_count
+                high = xp_ref[first : first + parts // 2 * block, : 2 * LANES]
+                low = xp_ref[first : first + parts // 2 * block, 2 * LANES :]
                 both = lax.dot_general(t_ref[which], high, dims, preferred_element_type=f32)
                 more = lax.dot_general(t_ref[which, : 2 * kept], low, dims, preferred_element_type=f32)
                 out = both[: 2 * kept] + (both[2 * kept :] + more)
-                for c in range(2):
-                    for h in range(block // LANES):
-                        tile = (j * 2 + c) * (block // LANES) + h
-                        s_ref[pl.ds(tile * kept * SKEW + one, kept, stride=SKEW), :] = out[
-                            c * kept : (c + 1) * kept, h * LANES : (h + 1) * LANES
-                        ]
+                for u in range(parts // 2):
+                    j = parts - 1 - u if which else u
+                    for c in range(2):
+                        for h in range(block // LANES):
+                            tile = (j * 2 + c) * (block // LANES) + h
+                            at = u * block + h * LANES
+                            s_ref[pl.ds(tile * kept * SKEW + one, kept, stride=SKEW), :] = out[
+                                c * kept : (c + 1) * kept, at : at + LANES
+                            ]
             return carry
 
         lax.fori_loop(0, inputs, one_input, 0)
@@ -236,6 +236,15 @@
                     ].astype(bf16)
 
         copies = []
+        for index, which in enumerate(merged):
+            copies.append(
+                pltpu.make_async_copy(
+                    earlier[index],
+                    outs[which].at[:, :, pl.ds(0, wide * LANES)],
+                    sems.at[len(sends) + index],
+                )
+            )
+            copies[-1].start()
         for dc in range(chans):
             chan = lax.bitwise_xor(lax.axis_index("chan"), dc) if turned else dc
 
@@ -245,16 +254,17 @@
                 return carry
 
             lax.fori_loop(0, kept // chans // near, some_rows, 0)
-            for index, (dz, of, skip, count) in enumerate(sends):
+            for index, (dz, of, count) in enumerate(sends):
                 if of != dc:
                     continue
-                first = chan * (kept // chans * parts) + skip
+                first = chan * (kept // chans * parts)
                 if dz is not None:
                     station = lax.bitwise_xor(lax.axis_index("stn"), dz)
                     first = first + station * (kept // chans * parts // stations)
-                copies.append(
-                    pltpu.make_async_copy(z_ref.at[pl.ds(first, count)], outs[index], sems.at[index])
-                )
+                to = outs[index]
+                if index in merged:
+                    to = to.at[:, :, pl.ds(wide * LANES, wide * LANES)]
+                copies.append(pltpu.make_async_copy(z_ref.at[pl.ds(first, count)], to, sems.at[index]))
                 copies[-1].start()
         for copy in copies:
             copy.wait()
@@ -288,10 +298,10 @@
 HBM = pl.BlockSpec(memory_space=pl.ANY)
 
 
-def make_spectra(voltages, taps, sends, stations, chans, turned):
+def make_spectra(voltages, taps, sends, stations, chans, turned, first_frame=0, halves=1, merged=()):
     frames, inputs, frame_len = voltages.shape
     tap_count = taps.shape[0]
-    spectra_count = frames - tap_count + 1
+    spectra_count = (frames - tap_count + 1) // halves
     tiles = frame_len // LANES
     half = tiles // 2
     rows = (half + 1) * spectra_count
@@ -299,9 +309,14 @@
     groups = frame_len // 2 // AVG
     per_step = 8
     tw, t = tables(frame_len)
-    sizes = (inputs, frames, tiles, per_step, spectra_count, tap_count, stations, chans)
+    sizes = (inputs, first_frame, tiles, per_step, spectra_count, tap_count, stations, chans)
+    places = tuple(index for index, _ in merged)
+    shapes = [
+        jax.ShapeDtypeStruct((count, inputs, (4 if index in places else 2) * block), bf16)
+        for index, (_, _, count) in enumerate(sends)
+    ]
     return pl.pallas_call(
-        functools.partial(spectra_kernel, sizes=sizes, sends=sends, turned=turned),
+        functools.partial(spectra_kernel, sizes=sizes, sends=sends, merged=places, turned=turned),
         name="spectra",
         grid=(tiles // per_step,),
         in_specs=[
@@ -309,9 +324,10 @@
             pl.BlockSpec(t.shape, lambda q: (0, 0, 0)),
             pl.BlockSpec((frames, inputs, per_step * LANES), lambda q: (0, 0, q)),
             pl.BlockSpec((tap_count, per_step * LANES), lambda q: (0, q)),
-        ],
+        ]
+        + [pl.BlockSpec(value.shape, lambda q: (0, 0, 0)) for _, value in merged],
         out_specs=[HBM] * len(sends),
-        out_shape=[jax.ShapeDtypeStruct((count, inputs, 2 * block), bf16) for _, _, _, count in sends],
+        out_shape=shapes,
         scratch_shapes=[
             pltpu.VMEM((spectra_count * tiles * SUB, LANES), f32),
             pltpu.VMEM((5 * (tiles // 8) * 2 * SUB, LANES), f32),
@@ -319,19 +335,23 @@
             pltpu.VMEM((rows, 4 * LANES), bf16),
             pltpu.VMEM((groups * (2 * block // LANES) * SKEW, LANES), f32),
             pltpu.VMEM((groups, inputs, 2 * block), bf16),
-            pltpu.SemaphoreType.DMA((len(sends),)),
+            pltpu.SemaphoreType.DMA((len(sends) + len(merged),)),
         ],
-    )(jnp.asarray(tw), jnp.asarray(t), voltages, taps)
-
-
-def lefts(own):
-    wide = own.shape[1]
-    return [own, jnp.concatenate([own[:, wide // 2 :], -own[:, : wide // 2]], axis=1)]
-
-
-def products(p_ref, slot, owns):
+    )(jnp.asarray(tw), jnp.asarray(t), voltages, taps, *[value for _, value in merged])
+
+
+def lefts(own, halves):
+    width = own.shape[1] // (2 * halves)
+    crossed = []
+    for half in range(halves):
+        at = 2 * half * width
+        crossed += [own[:, at + width : at + 2 * width], -own[:, at : at + width]]
+    return [own, jnp.concatenate(crossed, axis=1)]
+
+
+def products(p_ref, slot, owns, halves):
     right = jnp.concatenate(owns, axis=0)
-    left = jnp.concatenate([piece for own in owns for piece in lefts(own)], axis=0)
+    left = jnp.concatenate([piece for own in owns for piece in lefts(own, halves)], axis=0)
     out = lax.dot_general(left, right, (((1,), (1,)), ((), ())), preferred_element_type=f32)
     p_ref[slot, :, : right.shape[0]] = out
 
@@ -368,7 +388,7 @@
         for d in range(reach):
             other = lax.rem(b + d, stations)
             right = fetch(other)
-            left = jnp.concatenate(lefts(own), axis=0)
+            left = jnp.concatenate(lefts(own, 1), axis=0)
             p_ref[d, :, :block_inputs] = lax.dot_general(
                 left, right, (((1,), (1,)), ((), ())), preferred_element_type=f32
             )
@@ -401,24 +421,32 @@
     blocks, chans, groups, distances, scale, per_step = sizes
     arrived = refs[: len(pieces)]
     outs = refs[len(pieces) : len(pieces) + blocks]
-    r_ref, p_ref, q_ref = refs[len(pieces) + blocks :]
+    r_ref, p_ref, q_ref, sems = refs[len(pieces) + blocks :]
     here = lax.axis_index("stn") if blocks > 1 else 0
     block_inputs = chans * r_ref.shape[2]
-    together = math.gcd(groups, 8)
-
-    def collect(at, carry):
-        for index, (dz, dc, mine, first) in enumerate(pieces):
+    stages = 2
+    part = groups // stages
+    copies = []
+    for stage in range(stages):
+        for index, (dz, dc, mine, lane) in enumerate(pieces):
             chan = lax.bitwise_xor(lax.axis_index("chan"), dc)
             block = lax.bitwise_xor(here, dz) if blocks > 1 else 0
-            start = first + at * together
+            start = stage * part
             if mine:
                 start = start + lax.axis_index("stn") * mine
-            r_ref[block * chans + chan, pl.ds(at * together, together), :, :] = arrived[index][
-                pl.ds(start, together), :, :
-            ]
-        return carry
-
-    lax.fori_loop(0, groups // together, collect, 0)
+            copies.append(
+                pltpu.make_async_copy(
+                    arrived[index].at[pl.ds(start, part)],
+                    r_ref.at[
+                        block * chans + chan,
+                        pl.ds(stage * part, part),
+                        :,
+                        pl.ds(lane, arrived[index].shape[-1]),
+                    ],
+                    sems.at[stage * len(pieces) + index],
+                )
+            )
+            copies[-1].start()
 
     def some_groups(at, carry):
         for one in range(per_step):
@@ -427,7 +455,7 @@
                 jnp.concatenate([r_ref[block * chans + c, g] for c in range(chans)], axis=0)
                 for block in range(blocks)
             ]
-            products(p_ref, one, owns)
+            products(p_ref, one, owns, HALVES)
             for turn_by in range(blocks):
                 block = lax.bitwise_xor(here, turn_by) if blocks > 1 else 0
                 targets = [lax.rem(block + d, blocks) if blocks > 1 else 0 for d in distances]
@@ -437,26 +465,30 @@
                     outs[turn_by][d, g, :, :] = tile
         return carry
 
-    lax.fori_loop(0, groups // per_step, some_groups, 0)
+    for stage in range(stages):
+        for copy in copies[stage * len(pieces) : (stage + 1) * len(pieces)]:
+            copy.wait()
+        lax.fori_loop(stage * part // per_step, (stage + 1) * part // per_step, some_groups, 0)
 
 
 def correlate_pieces(arrays, pieces, blocks, chans, groups, distances, scale):
-    inputs, wide = arrays[0].shape[1:]
+    inputs = arrays[0].shape[1]
+    wide = max(lane + value.shape[2] for value, (_, _, _, lane) in zip(arrays, pieces))
     block_inputs = chans * inputs
     out_rows = block_inputs * block_inputs // LANES
-    per_step = math.gcd(groups, 8 // blocks)
+    per_step = math.gcd(groups // 2, 8 // blocks)
     sizes = (blocks, chans, groups, distances, scale, per_step)
     shape = (len(distances), groups, 2 * out_rows, LANES)
-    vmem = pl.BlockSpec(memory_space=pltpu.VMEM)
     return pl.pallas_call(
         functools.partial(pieces_kernel, sizes=sizes, pieces=pieces),
-        in_specs=[vmem] * len(arrays),
-        out_specs=[vmem] * blocks,
+        in_specs=[HBM] * len(arrays),
+        out_specs=[pl.BlockSpec(memory_space=pltpu.VMEM)] * blocks,
         out_shape=[jax.ShapeDtypeStruct(shape, bf16)] * blocks,
         scratch_shapes=[
             pltpu.VMEM((blocks * chans, groups, inputs, wide), bf16),
             pltpu.VMEM((per_step, blocks * 2 * block_inputs, LANES), f32),
             pltpu.VMEM((per_step * blocks * len(distances), 2 * out_rows, LANES), f32),
+            pltpu.SemaphoreType.DMA((2 * len(pieces),)),
         ],
     )(*arrays)
 
@@ -509,7 +541,7 @@
     scale = 1.0 / (spectra_count * AVG)
     frames_first = voltages.transpose(1, 0, 2)
     if not direct(stations, chans):
-        sends = tuple((None, dc, 0, groups // chans) for dc in range(chans))
+        sends = tuple((None, dc, groups // chans) for dc in range(chans))
         slices = make_spectra(frames_first, taps, sends, stations, chans, False)
         send = jnp.concatenate(slices, axis=0).reshape(chans * stations, here, inputs_here, -1)
         turned = lax.all_to_all(send, ("chan", "stn"), 0, 0, tiled=True)
@@ -517,35 +549,45 @@
         back = lax.all_to_all(tiles, "stn", 0, 0, tiled=True)
         out = back.transpose(1, 0, 2, 3, 4)
     else:
-        part = here // CHUNKS
-        sends = [(None, dc, 0, here * stations) for dc in range(chans)]
-        sends += [(dz, dc, 0, here) for dz in (2, 1, 3) for dc in range(chans)]
-        sent = make_spectra(frames_first, taps, tuple(sends), stations, chans, True)
-        whole, far = [], {}
-        for (dz, dc, _, _), value in zip(sends, sent):
-            if dz is None:
-                whole.append(shifted(value, stations, chans, 0, dc) if dc else value)
-            else:
-                far[dz, dc] = shifted(value, stations, chans, dz, dc)
-        pieces = [(0, dc, 0, 0) for dc in range(chans)]
-        (own,) = correlate_pieces(whole, pieces, 1, chans, here * stations, (0,), scale)
-        distances = tuple(range(1, reach))
-        back = {}
-        for chunk in range(CHUNKS):
-            pieces = [(0, dc, here, chunk * part) for dc in range(chans)]
-            pieces += [(dz, dc, 0, chunk * part) for dz, dc in far]
-            arrays = whole + list(far.values())
-            outs = correlate_pieces(arrays, pieces, stations, chans, part, distances, scale)
-            for dz in range(stations):
-                back[dz, chunk] = outs[0] if dz == 0 else shifted(outs[dz], stations, chans, dz, 0)
-        out = assemble(
-            own, [back[dz, chunk] for dz in range(stations) for chunk in range(CHUNKS)], stations, CHUNKS
-        )
+        near = [(None, dc, here * stations) for dc in range(chans)]
+        far = [(dz, dc, here) for dz in (2, 3) for dc in range(chans)]
+        mid = [(1, dc, here) for dc in range(chans)]
+        sends = tuple(far + near + mid)
+        own_pieces, own_arrays, pieces, arrays = [], [], [], []
+        kept_back = ()
+        for half in range(HALVES):
+            sent = make_spectra(
+                frames_first,
+                taps,
+                sends,
+                stations,
+                chans,
+                True,
+                half * spectra_count // HALVES,
+                HALVES,
+                kept_back,
+            )
+            if half == 0:
+                kept_back = tuple((len(far + near) + index, value) for index, value in enumerate(sent[-chans:]))
+            lane = half * 2 * AVG * spectra_count // HALVES
+            for (dz, dc, _), value in zip(sends, sent):
+                if dz == 1 and half == 0:
+                    continue
+                moved = value if dz is None and dc == 0 else shifted(value, stations, chans, dz or 0, dc)
+                if dz is None:
+                    own_pieces.append((0, dc, 0, lane))
+                    own_arrays.append(moved)
+                pieces.append((dz or 0, dc, here if dz is None else 0, 0 if dz == 1 else lane))
+                arrays.append(moved)
+        (own,) = correlate_pieces(own_arrays, own_pieces, 1, chans, here * stations, (0,), scale)
+        outs = correlate_pieces(arrays, pieces, stations, chans, here, tuple(range(1, reach)), scale)
+        back = [outs[dz] if dz == 0 else shifted(outs[dz], stations, chans, dz, 0) for dz in range(stations)]
+        out = assemble(own, back, stations, 1)
     out = out.reshape(reach, stations * here, pairs // LANES, 2, LANES)
     return out.transpose(0, 1, 3, 2, 4).reshape(1, reach, stations * here, 2, pairs)
 
 
-CHUNKS = 2
+HALVES = 2
 
 
 def direct(stations, chans):

time: 107 us -> 126 us (1.18)
  starting transfers between devices: 35.2 us -> 49.1 us
  Pallas kernels: 32.6 us -> 36.8 us
    ppermute x21 -> x29, starting transfers between devices: 35.2 us -> 49.1 us  [shifted(): return lax.ppermute(value, ('stn', 'chan'), pairs)]
    pallas_call x1 -> x2, Pallas kernels: 15.4 us -> 22.9 us  [make_spectra(): pl.pallas_call(functools.partial(spectra_kernel, sizes=sizes, sends=sends...]
    pallas_call x3 -> x2, Pallas kernels: 15.2 us -> 11.8 us  [correlate_pieces(): pl.pallas_call(functools.partial(pieces_kernel, sizes=sizes, pieces=piece...]
    ppermute x21 -> x29, waiting for transfers between devices: 37.4 us -> 37.7 us  [shifted(): return lax.ppermute(value, ('stn', 'chan'), pairs)]
  transfers between devices with their start and end apart: 21 -> 29, of which waited for: 11 -> 13; matrix products, arithmetic and copies ran while one was open for 0% -> 0% of each run, Pallas kernels for 10% -> 13%
where the time goes in v3:
time: 126 us; the launch traced here: 125 us
  starting transfers between devices  49.1 us (39%)
  waiting for transfers between devices  37.7 us (30%)
  Pallas kernels  36.8 us (29%)
  local copies, waits for them, and re-layouts  1.28 us (1%)
    ppermute x29, starting transfers between devices, shifted(): return lax.ppermute(value, ('stn', 'chan'), pairs)  49.1 us
    ppermute x29, waiting for transfers between devices, shifted(): return lax.ppermute(value, ('stn', 'chan'), pairs)  37.7 us
    pallas_call x2, Pallas kernels, make_spectra(): pl.pallas_call(functools.partial(spectra_kernel, sizes=sizes, sends=sends...  22.9 us
    pallas_call x2, Pallas kernels, correlate_pieces(): pl.pallas_call(functools.partial(pieces_kernel, sizes=sizes, pieces=piece...  11.8 us
  transfers between devices with their start and end apart: 29, of which 13 were waited for; matrix products, arithmetic and copies ran while one was open for 0% of the time, Pallas kernels for 13%

profile of v3, /device:TPU:0, one launch (start us, length us, event | category | flops | bytes accessed | tf_op | source)
XLA Modules:
  0.0 125.2 jit_solution(13851901509410363091)
XLA Ops:
  0.0 11.4 %spectra.2 = (bf16[16,8,256]{2,1,0:T(8,128)(2,1)}, bf16[16,8,256]{2,1,0:T(8,128)(2,1)}, bf16[16,8,256]{2,1,0:T(8,128)(2,1)}, bf16[16,8,256]{2,1,0:T(8,128)(2,1)}...) custom-call(f32[528,128]{1,0:T(8,128)} %constant.4.clone.tw_ref, ...), custom_call_target="tpu_custom_call" | custom-call | tf_op jit(solution)/shard_map/spectra/pallas_call | solution.py:318
  11.4 4.1 %collective-permute-start.6 = (bf16[16,8,256]{2,1,0:T(8,128)(2,1)}, bf16[16,8,256]{2,1,0:T(8,128)(2,1)S(1)}, u32[]{:S(2)}, u32[]{:S(2)}) collective-permute-start(bf16[16,8,256]{2,1,0:T(8,128)(2,1)} %get-tuple-element.53), channel_id=1, source_target_pairs={{0,8},{1,9},{2,10},{3,11},{4,12},{5,13},{6,14},{7,15},{8,0},{9,1},... | collective-permute-start | bytes 196616 | tf_op jit(solution)/shard_map/ppermute | solution.py:528
  15.5 3.0 %collective-permute-start.8 = (bf16[16,8,256]{2,1,0:T(8,128)(2,1)}, bf16[16,8,256]{2,1,0:T(8,128)(2,1)S(1)}, u32[]{:S(2)}, u32[]{:S(2)}) collective-permute-start(bf16[16,8,256]{2,1,0:T(8,128)(2,1)} %get-tuple-element.55), channel_id=1, source_target_pairs={{0,10},{1,11},{2,8},{3,9},{4,14},{5,15},{6,12},{7,13},{8,2},{9,3},... | collective-permute-start | bytes 196616 | tf_op jit(solution)/shard_map/ppermute | solution.py:528
  18.5 0.6 collective-permute-start.9
  19.1 3.6 %collective-permute-start.10 = (bf16[16,8,256]{2,1,0:T(8,128)(2,1)}, bf16[16,8,256]{2,1,0:T(8,128)(2,1)S(1)}, u32[]{:S(2)}, u32[]{:S(2)}) collective-permute-start(bf16[16,8,256]{2,1,0:T(8,128)(2,1)} %get-tuple-element.57), channel_id=1, source_target_pairs={{0,12},{1,13},{2,14},{3,15},{4,8},{5,9},{6,10},{7,11},{8,4},{9,5},... | collective-permute-start | bytes 196616 | tf_op jit(solution)/shard_map/ppermute | solution.py:528
  22.7 1.1 collective-permute-start.11
  23.8 2.8 %collective-permute-done.7.refs_1_ = bf16[16,8,256]{2,1,0:T(8,128)(2,1)S(1)} collective-permute-done((bf16[16,8,256]{2,1,0:T(8,128)(2,1)}, bf16[16,8,256]{2,1,0:T(8,128)(2,1)S(1)}, u32[]{:S(2)}, u32[]{:S(2)}) %collective-permute-start.7) | collective-permute-done | bytes 65568 | tf_op jit(solution)/shard_map/ppermute | solution.py:528
  26.6 3.9 %collective-permute-start.12 = (bf16[16,8,256]{2,1,0:T(8,128)(2,1)}, bf16[16,8,256]{2,1,0:T(8,128)(2,1)S(1)}, u32[]{:S(2)}, u32[]{:S(2)}) collective-permute-start(bf16[16,8,256]{2,1,0:T(8,128)(2,1)} %get-tuple-element.59), channel_id=1, source_target_pairs={{0,14},{1,15},{2,12},{3,13},{4,10},{5,11},{6,8},{7,9},{8,6},{9,7},... | collective-permute-start | bytes 196616 | tf_op jit(solution)/shard_map/ppermute | solution.py:528
  30.5 1.9 %collective-permute-start.13 = (bf16[16,8,256]{2,1,0:T(8,128)(2,1)}, bf16[16,8,256]{2,1,0:T(8,128)(2,1)S(1)}, u32[]{:S(2)}, u32[]{:S(2)}) collective-permute-start(bf16[16,8,256]{2,1,0:T(8,128)(2,1)} %get-tuple-element.60), channel_id=1, source_target_pairs={{0,15},{1,14},{2,13},{3,12},{4,11},{5,10},{6,9},{7,8},{8,7},{9,6},... | collective-permute-start | bytes 196616 | tf_op jit(solution)/shard_map/ppermute | solution.py:528
  32.4 11.5 %spectra.3 = (bf16[16,8,256]{2,1,0:T(8,128)(2,1)}, bf16[16,8,256]{2,1,0:T(8,128)(2,1)}, bf16[16,8,256]{2,1,0:T(8,128)(2,1)}, bf16[16,8,256]{2,1,0:T(8,128)(2,1)}...) custom-call(f32[528,128]{1,0:T(8,128)} %constant.4.clone.tw_ref, ...), custom_call_target="tpu_custom_call" | custom-call | tf_op jit(solution)/shard_map/spectra/pallas_call | solution.py:318
  44.0 0.1 collective-permute-start.14
  44.1 2.8 %collective-permute-start.15 = (bf16[16,8,256]{2,1,0:T(8,128)(2,1)}, bf16[16,8,256]{2,1,0:T(8,128)(2,1)S(1)}, u32[]{:S(2)}, u32[]{:S(2)}) collective-permute-start(bf16[16,8,256]{2,1,0:T(8,128)(2,1)} %get-tuple-element.62), channel_id=1, source_target_pairs={{0,9},{1,8},{2,11},{3,10},{4,13},{5,12},{6,15},{7,14},{8,1},{9,0},... | collective-permute-start | bytes 196616 | tf_op jit(solution)/shard_map/ppermute | solution.py:528
  46.9 0.7 collective-permute-start.16
  47.6 2.6 %collective-permute-start.17 = (bf16[16,8,256]{2,1,0:T(8,128)(2,1)}, bf16[16,8,256]{2,1,0:T(8,128)(2,1)S(1)}, u32[]{:S(2)}, u32[]{:S(2)}) collective-permute-start(bf16[16,8,256]{2,1,0:T(8,128)(2,1)} %get-tuple-element.64), channel_id=1, source_target_pairs={{0,11},{1,10},{2,9},{3,8},{4,15},{5,14},{6,13},{7,12},{8,3},{9,2},... | collective-permute-start | bytes 196616 | tf_op jit(solution)/shard_map/ppermute | solution.py:528
  50.2 0.6 collective-permute-start
  50.9 2.7 %collective-permute-done.14.refs_12_ = bf16[16,8,256]{2,1,0:T(8,128)(2,1)S(1)} collective-permute-done((bf16[16,8,256]{2,1,0:T(8,128)(2,1)}, bf16[16,8,256]{2,1,0:T(8,128)(2,1)S(1)}, u32[]{:S(2)}, u32[]{:S(2)}) %collective-permute-start.14) | collective-permute-done | bytes 65568 | tf_op jit(solution)/shard_map/ppermute | solution.py:528
  53.6 1.6 %collective-permute-start.18 = (bf16[16,8,256]{2,1,0:T(8,128)(2,1)}, bf16[16,8,256]{2,1,0:T(8,128)(2,1)S(1)}, u32[]{:S(2)}, u32[]{:S(2)}) collective-permute-start(bf16[16,8,256]{2,1,0:T(8,128)(2,1)} %get-tuple-element.65), channel_id=1, source_target_pairs={{0,12},{1,13},{2,14},{3,15},{4,8},{5,9},{6,10},{7,11},{8,4},{9,5},... | collective-permute-start | bytes 196616 | tf_op jit(solution)/shard_map/ppermute | solution.py:528
  55.1 1.2 collective-permute-done.15.refs_13_
  56.3 1.3 %collective-permute-start.19 = (bf16[16,8,256]{2,1,0:T(8,128)(2,1)}, bf16[16,8,256]{2,1,0:T(8,128)(2,1)S(1)}, u32[]{:S(2)}, u32[]{:S(2)}) collective-permute-start(bf16[16,8,256]{2,1,0:T(8,128)(2,1)} %get-tuple-element.66), channel_id=1, source_target_pairs={{0,13},{1,12},{2,15},{3,14},{4,9},{5,8},{6,11},{7,10},{8,5},{9,4},... | collective-permute-start | bytes 196616 | tf_op jit(solution)/shard_map/ppermute | solution.py:528
  57.6 0.3 collective-permute-done.16.refs_14_
  57.9 2.4 %collective-permute-start.20 = (bf16[16,8,256]{2,1,0:T(8,128)(2,1)}, bf16[16,8,256]{2,1,0:T(8,128)(2,1)S(1)}, u32[]{:S(2)}, u32[]{:S(2)}) collective-permute-start(bf16[16,8,256]{2,1,0:T(8,128)(2,1)} %get-tuple-element.67), channel_id=1, source_target_pairs={{0,14},{1,15},{2,12},{3,13},{4,10},{5,11},{6,8},{7,9},{8,6},{9,7},... | collective-permute-start | bytes 196616 | tf_op jit(solution)/shard_map/ppermute | solution.py:528
  60.3 0.4 collective-permute-done.17.refs_15_
  60.7 2.1 %collective-permute-start.21 = (bf16[16,8,256]{2,1,0:T(8,128)(2,1)}, bf16[16,8,256]{2,1,0:T(8,128)(2,1)S(1)}, u32[]{:S(2)}, u32[]{:S(2)}) collective-permute-start(bf16[16,8,256]{2,1,0:T(8,128)(2,1)} %get-tuple-element.68), channel_id=1, source_target_pairs={{0,15},{1,14},{2,13},{3,12},{4,11},{5,10},{6,9},{7,8},{8,7},{9,6},... | collective-permute-start | bytes 196616 | tf_op jit(solution)/shard_map/ppermute | solution.py:528
  62.7 1.2 collective-permute-start.22
  64.0 2.5 %collective-permute-start.23 = (bf16[16,8,512]{2,1,0:T(8,128)(2,1)}, bf16[16,8,512]{2,1,0:T(8,128)(2,1)S(1)}, u32[]{:S(2)}, u32[]{:S(2)}) collective-permute-start(bf16[16,8,512]{2,1,0:T(8,128)(2,1)} %get-tuple-element.70), channel_id=1, source_target_pairs={{0,5},{1,4},{2,7},{3,6},{4,1},{5,0},{6,3},{7,2},{8,13},{9,12},{10,... | collective-permute-start | bytes 393224 | tf_op jit(solution)/shard_map/ppermute | solution.py:528
  66.4 4.0 %collective-permute-start.24 = (bf16[16,8,512]{2,1,0:T(8,128)(2,1)}, bf16[16,8,512]{2,1,0:T(8,128)(2,1)S(1)}, u32[]{:S(2)}, u32[]{:S(2)}) collective-permute-start(bf16[16,8,512]{2,1,0:T(8,128)(2,1)} %get-tuple-element.71), channel_id=1, source_target_pairs={{0,6},{1,7},{2,4},{3,5},{4,2},{5,3},{6,0},{7,1},{8,14},{9,15},{10,... | collective-permute-start | bytes 393224 | tf_op jit(solution)/shard_map/ppermute | solution.py:528
  70.5 1.1 collective-permute-start.25
  71.5 0.7 collective-permute-start.1
  72.2 0.2 collective-permute-done.23.refs_25_
  72.4 1.3 %collective-permute-start.2 = (bf16[64,8,256]{2,1,0:T(8,128)(2,1)S(1)}, bf16[64,8,256]{2,1,0:T(8,128)(2,1)S(1)}, u32[]{:S(2)}, u32[]{:S(2)}) collective-permute-start(bf16[64,8,256]{2,1,0:T(8,128)(2,1)S(1)} %copy-done.29), channel_id=1, source_target_pairs={{0,3},{1,2},{2,1},{3,0},{4,7},{5,6},{6,5},{7,4},{8,11},{9,10},{10,... | collective-permute-start | bytes 786440 | tf_op jit(solution)/shard_map/ppermute | solution.py:528
  73.7 2.9 %collective-permute-done.24.refs_26_ = bf16[16,8,512]{2,1,0:T(8,128)(2,1)S(1)} collective-permute-done((bf16[16,8,512]{2,1,0:T(8,128)(2,1)}, bf16[16,8,512]{2,1,0:T(8,128)(2,1)S(1)}, u32[]{:S(2)}, u32[]{:S(2)}) %collective-permute-start.24) | collective-permute-done | bytes 131104 | tf_op jit(solution)/shard_map/ppermute | solution.py:528
  76.6 2.1 %collective-permute-done.25.refs_27_ = bf16[16,8,512]{2,1,0:T(8,128)(2,1)S(1)} collective-permute-done((bf16[16,8,512]{2,1,0:T(8,128)(2,1)}, bf16[16,8,512]{2,1,0:T(8,128)(2,1)S(1)}, u32[]{:S(2)}, u32[]{:S(2)}) %collective-permute-start.25) | collective-permute-done | bytes 131104 | tf_op jit(solution)/shard_map/ppermute | solution.py:528
  78.7 0.8 collective-permute-start.4
  79.6 0.7 collective-permute-start.5
  80.2 4.4 %collective-permute-done.1.refs_2_.refs_10_ = bf16[64,8,256]{2,1,0:T(8,128)(2,1)S(1)} collective-permute-done((bf16[64,8,256]{2,1,0:T(8,128)(2,1)}, bf16[64,8,256]{2,1,0:T(8,128)(2,1)S(1)}, u32[]{:S(2)}, u32[]{:S(2)}) %collective-permute-start.1) | collective-permute-done | bytes 262176 | tf_op jit(solution)/shard_map/ppermute | solution.py:528
  84.6 5.5 %collective-permute-done.2.refs_3_.refs_11_ = bf16[64,8,256]{2,1,0:T(8,128)(2,1)S(1)} collective-permute-done((bf16[64,8,256]{2,1,0:T(8,128)(2,1)S(1)}, bf16[64,8,256]{2,1,0:T(8,128)(2,1)S(1)}, u32[]{:S(2)}, u32[]{:S(2)}) %collective-permute-start.2) | collective-permute-done | bytes 262176 | tf_op jit(solution)/shard_map/ppermute | solution.py:528
  90.2 5.7 %collective-permute-done.4.refs_6_.refs_22_ = bf16[64,8,256]{2,1,0:T(8,128)(2,1)S(1)} collective-permute-done((bf16[64,8,256]{2,1,0:T(8,128)(2,1)}, bf16[64,8,256]{2,1,0:T(8,128)(2,1)S(1)}, u32[]{:S(2)}, u32[]{:S(2)}) %collective-permute-start.4) | collective-permute-done | bytes 262176 | tf_op jit(solution)/shard_map/ppermute | solution.py:528
  95.9 5.5 %collective-permute-done.5.refs_7_.refs_23_ = bf16[64,8,256]{2,1,0:T(8,128)(2,1)S(1)} collective-permute-done((bf16[64,8,256]{2,1,0:T(8,128)(2,1)}, bf16[64,8,256]{2,1,0:T(8,128)(2,1)S(1)}, u32[]{:S(2)}, u32[]{:S(2)}) %collective-permute-start.5) | collective-permute-done | bytes 262176 | tf_op jit(solution)/shard_map/ppermute | solution.py:528
  101.6 0.5 copy-done.5
  102.1 6.8 %shard_map.65 = (bf16[2,16,16,128]{3,2,1,0:T(8,128)(2,1)}, bf16[2,16,16,128]{3,2,1,0:T(8,128)(2,1)}, bf16[2,16,16,128]{3,2,1,0:T(8,128)(2,1)}, bf16[2,16,16,128]{3,2,1,0:T(8,128)(2,1)}) custom-call(bf16[16,8,256]{2,1,0:T(8,128)(2,1)} %copy-done.13, bf16[16,8,256]{2,1,0:T(8,128)(2,1)} %copy-done.14, bf16[16,8,256]{2,1,0:T(8,128)(2,1)} %copy-done.15, ...), custom_call_target="tpu_custom_call" | custom-call | tf_op jit(solution)/shard_map/pallas_call | solution.py:482
  108.9 0.4 collective-permute-start.26
  109.3 2.2 %collective-permute-start.27 = (bf16[2,16,16,128]{3,2,1,0:T(8,128)(2,1)}, bf16[2,16,16,128]{3,2,1,0:T(8,128)(2,1)S(1)}, u32[]{:S(2)}, u32[]{:S(2)}) collective-permute-start(bf16[2,16,16,128]{3,2,1,0:T(8,128)(2,1)} %get-tuple-element.75), channel_id=1, source_target_pairs={{0,8},{1,9},{2,10},{3,11},{4,12},{5,13},{6,14},{7,15},{8,0},{9,1},... | collective-permute-start | bytes 393224 | tf_op jit(solution)/shard_map/ppermute | solution.py:528
  111.5 1.9 %collective-permute-start.28 = (bf16[2,16,16,128]{3,2,1,0:T(8,128)(2,1)}, bf16[2,16,16,128]{3,2,1,0:T(8,128)(2,1)S(1)}, u32[]{:S(2)}, u32[]{:S(2)}) collective-permute-start(bf16[2,16,16,128]{3,2,1,0:T(8,128)(2,1)} %get-tuple-element.76), channel_id=1, source_target_pairs={{0,12},{1,13},{2,14},{3,15},{4,8},{5,9},{6,10},{7,11},{8,4},{9,5},... | collective-permute-start | bytes 393224 | tf_op jit(solution)/shard_map/ppermute | solution.py:528
  113.3 5.1 %shard_map.64.own_ref = bf16[1,64,16,128]{3,2,1,0:T(8,128)(2,1)} custom-call(bf16[64,8,256]{2,1,0:T(8,128)(2,1)} %get-tuple-element.41.refs_0_.refs_8_, bf16[64,8,256]{2,1,0:T(8,128)(2,1)} %copy-done, bf16[64,8,256]{2,1,0:T(8,128)(2,1)} %copy-done.1, bf16[64,8,256]{2,1,0:T(8,128)(2,1)} %copy-done.2, bf16[64,8,256]{2,1,0:T(8,128)(2,1)} %get-tuple-element.49.refs_4_.refs_20_, ...), custom_call_target="tpu_custom_call" | custom-call | tf_op jit(solution)/shard_map/pallas_call | solution.py:482
  118.4 4.0 %collective-permute-done.27.refs_2_ = bf16[2,16,16,128]{3,2,1,0:T(8,128)(2,1)S(1)} collective-permute-done((bf16[2,16,16,128]{3,2,1,0:T(8,128)(2,1)}, bf16[2,16,16,128]{3,2,1,0:T(8,128)(2,1)S(1)}, u32[]{:S(2)}, u32[]{:S(2)}) %collective-permute-start.27) | collective-permute-done | bytes 131104 | tf_op jit(solution)/shard_map/ppermute | solution.py:528
  122.4 0.6 copy-done.11
  123.1 0.1 copy-done.12
  123.1 2.1 %assemble.1 = bf16[3,64,16,128]{3,2,1,0:T(8,128)(2,1)} custom-call(bf16[1,64,16,128]{3,2,1,0:T(8,128)(2,1)} %shard_map.64.own_ref, bf16[2,16,16,128]{3,2,1,0:T(8,128)(2,1)} %get-tuple-element.73.refs_0_, bf16[2,16,16,128]{3,2,1,0:T(8,128)(2,1)} %copy-done.10, bf16[2,16,16,128]{3,2,1,0:T(8,128)(2,1)} %copy-done.11, bf16[2,16,16,128]{3,2,1,0:T(8,128)(2,1)} %copy-done.12), custom_call_target="tpu_custom_call" | custom-call | tf_op jit(solution)/shard_map/assemble/pallas_call | solution.py:513
  (77 shorter events, 0.2 us)
Async XLA Ops:
  11.4 38.9 %copy-start.30 = (bf16[64,8,256]{2,1,0:T(8,128)(2,1)S(1)}, bf16[64,8,256]{2,1,0:T(8,128)(2,1)}, u32[]{:S(2)}) copy-start(bf16[64,8,256]{2,1,0:T(8,128)(2,1)} %get-tuple-element.42) | copy-start | bytes 786436
  11.4 61.0 %copy-start.29 = (bf16[64,8,256]{2,1,0:T(8,128)(2,1)S(1)}, bf16[64,8,256]{2,1,0:T(8,128)(2,1)}, u32[]{:S(2)}) copy-start(bf16[64,8,256]{2,1,0:T(8,128)(2,1)} %get-tuple-element.44) | copy-start | bytes 786436
  11.4 11.3 %collective-permute-start.6 = (bf16[16,8,256]{2,1,0:T(8,128)(2,1)}, bf16[16,8,256]{2,1,0:T(8,128)(2,1)S(1)}, u32[]{:S(2)}, u32[]{:S(2)}) collective-permute-start(bf16[16,8,256]{2,1,0:T(8,128)(2,1)} %get-tuple-element.53), channel_id=1, source_target_pairs={{0,8},{1,9},{2,10},{3,11},{4,12},{5,13},{6,14},{7,15},{8,0},{9,1},... | collective-permute-start | bytes 196616 | tf_op jit(solution)/shard_map/ppermute | solution.py:528
  15.5 11.1 %collective-permute-start.7 = (bf16[16,8,256]{2,1,0:T(8,128)(2,1)}, bf16[16,8,256]{2,1,0:T(8,128)(2,1)S(1)}, u32[]{:S(2)}, u32[]{:S(2)}) collective-permute-start(bf16[16,8,256]{2,1,0:T(8,128)(2,1)} %get-tuple-element.54), channel_id=1, source_target_pairs={{0,9},{1,8},{2,11},{3,10},{4,13},{5,12},{6,15},{7,14},{8,1},{9,0},... | collective-permute-start | bytes 196616 | tf_op jit(solution)/shard_map/ppermute | solution.py:528
  15.5 15.0 %collective-permute-start.8 = (bf16[16,8,256]{2,1,0:T(8,128)(2,1)}, bf16[16,8,256]{2,1,0:T(8,128)(2,1)S(1)}, u32[]{:S(2)}, u32[]{:S(2)}) collective-permute-start(bf16[16,8,256]{2,1,0:T(8,128)(2,1)} %get-tuple-element.55), channel_id=1, source_target_pairs={{0,10},{1,11},{2,8},{3,9},{4,14},{5,15},{6,12},{7,13},{8,2},{9,3},... | collective-permute-start | bytes 196616 | tf_op jit(solution)/shard_map/ppermute | solution.py:528
  18.5 25.4 %collective-permute-start.9 = (bf16[16,8,256]{2,1,0:T(8,128)(2,1)}, bf16[16,8,256]{2,1,0:T(8,128)(2,1)S(1)}, u32[]{:S(2)}, u32[]{:S(2)}) collective-permute-start(bf16[16,8,256]{2,1,0:T(8,128)(2,1)} %get-tuple-element.56), channel_id=1, source_target_pairs={{0,11},{1,10},{2,9},{3,8},{4,15},{5,14},{6,13},{7,12},{8,3},{9,2},... | collective-permute-start | bytes 196616 | tf_op jit(solution)/shard_map/ppermute | solution.py:528
  19.1 24.9 %collective-permute-start.10 = (bf16[16,8,256]{2,1,0:T(8,128)(2,1)}, bf16[16,8,256]{2,1,0:T(8,128)(2,1)S(1)}, u32[]{:S(2)}, u32[]{:S(2)}) collective-permute-start(bf16[16,8,256]{2,1,0:T(8,128)(2,1)} %get-tuple-element.57), channel_id=1, source_target_pairs={{0,12},{1,13},{2,14},{3,15},{4,8},{5,9},{6,10},{7,11},{8,4},{9,5},... | collective-permute-start | bytes 196616 | tf_op jit(solution)/shard_map/ppermute | solution.py:528
  22.7 78.7 %copy-start.13 = (bf16[16,8,256]{2,1,0:T(8,128)(2,1)}, bf16[16,8,256]{2,1,0:T(8,128)(2,1)S(1)}, u32[]{:S(2)}) copy-start(bf16[16,8,256]{2,1,0:T(8,128)(2,1)S(1)} %collective-permute-done.6.refs_0_) | copy-start | bytes 196612
  22.7 24.1 %collective-permute-start.11 = (bf16[16,8,256]{2,1,0:T(8,128)(2,1)}, bf16[16,8,256]{2,1,0:T(8,128)(2,1)S(1)}, u32[]{:S(2)}, u32[]{:S(2)}) collective-permute-start(bf16[16,8,256]{2,1,0:T(8,128)(2,1)} %get-tuple-element.58), channel_id=1, source_target_pairs={{0,13},{1,12},{2,15},{3,14},{4,9},{5,8},{6,11},{7,10},{8,5},{9,4},... | collective-permute-start | bytes 196616 | tf_op jit(solution)/shard_map/ppermute | solution.py:528
  26.6 74.7 %copy-start.14 = (bf16[16,8,256]{2,1,0:T(8,128)(2,1)}, bf16[16,8,256]{2,1,0:T(8,128)(2,1)S(1)}, u32[]{:S(2)}) copy-start(bf16[16,8,256]{2,1,0:T(8,128)(2,1)S(1)} %collective-permute-done.7.refs_1_) | copy-start | bytes 196612
  26.6 20.9 %collective-permute-start.12 = (bf16[16,8,256]{2,1,0:T(8,128)(2,1)}, bf16[16,8,256]{2,1,0:T(8,128)(2,1)S(1)}, u32[]{:S(2)}, u32[]{:S(2)}) collective-permute-start(bf16[16,8,256]{2,1,0:T(8,128)(2,1)} %get-tuple-element.59), channel_id=1, source_target_pairs={{0,14},{1,15},{2,12},{3,13},{4,10},{5,11},{6,8},{7,9},{8,6},{9,7},... | collective-permute-start | bytes 196616 | tf_op jit(solution)/shard_map/ppermute | solution.py:528
  30.5 70.9 %copy-start.15 = (bf16[16,8,256]{2,1,0:T(8,128)(2,1)}, bf16[16,8,256]{2,1,0:T(8,128)(2,1)S(1)}, u32[]{:S(2)}) copy-start(bf16[16,8,256]{2,1,0:T(8,128)(2,1)S(1)} %collective-permute-done.8.refs_2_) | copy-start | bytes 196612
  30.5 19.7 %collective-permute-start.13 = (bf16[16,8,256]{2,1,0:T(8,128)(2,1)}, bf16[16,8,256]{2,1,0:T(8,128)(2,1)S(1)}, u32[]{:S(2)}, u32[]{:S(2)}) collective-permute-start(bf16[16,8,256]{2,1,0:T(8,128)(2,1)} %get-tuple-element.60), channel_id=1, source_target_pairs={{0,15},{1,14},{2,13},{3,12},{4,11},{5,10},{6,9},{7,8},{8,7},{9,6},... | collective-permute-start | bytes 196616 | tf_op jit(solution)/shard_map/ppermute | solution.py:528
  44.0 57.5 %copy-start.16 = (bf16[16,8,256]{2,1,0:T(8,128)(2,1)}, bf16[16,8,256]{2,1,0:T(8,128)(2,1)S(1)}, u32[]{:S(2)}) copy-start(bf16[16,8,256]{2,1,0:T(8,128)(2,1)S(1)} %collective-permute-done.9.refs_3_) | copy-start | bytes 196612
  44.0 9.6 %collective-permute-start.14 = (bf16[16,8,256]{2,1,0:T(8,128)(2,1)}, bf16[16,8,256]{2,1,0:T(8,128)(2,1)S(1)}, u32[]{:S(2)}, u32[]{:S(2)}) collective-permute-start(bf16[16,8,256]{2,1,0:T(8,128)(2,1)} %get-tuple-element.61), channel_id=1, source_target_pairs={{0,8},{1,9},{2,10},{3,11},{4,12},{5,13},{6,14},{7,15},{8,0},{9,1},... | collective-permute-start | bytes 196616 | tf_op jit(solution)/shard_map/ppermute | solution.py:528
  44.0 57.4 %copy-start.17 = (bf16[16,8,256]{2,1,0:T(8,128)(2,1)}, bf16[16,8,256]{2,1,0:T(8,128)(2,1)S(1)}, u32[]{:S(2)}) copy-start(bf16[16,8,256]{2,1,0:T(8,128)(2,1)S(1)} %collective-permute-done.10.refs_4_) | copy-start | bytes 196612
  44.1 12.2 %collective-permute-start.15 = (bf16[16,8,256]{2,1,0:T(8,128)(2,1)}, bf16[16,8,256]{2,1,0:T(8,128)(2,1)S(1)}, u32[]{:S(2)}, u32[]{:S(2)}) collective-permute-start(bf16[16,8,256]{2,1,0:T(8,128)(2,1)} %get-tuple-element.62), channel_id=1, source_target_pairs={{0,9},{1,8},{2,11},{3,10},{4,13},{5,12},{6,15},{7,14},{8,1},{9,0},... | collective-permute-start | bytes 196616 | tf_op jit(solution)/shard_map/ppermute | solution.py:528
  46.9 54.5 %copy-start.18 = (bf16[16,8,256]{2,1,0:T(8,128)(2,1)}, bf16[16,8,256]{2,1,0:T(8,128)(2,1)S(1)}, u32[]{:S(2)}) copy-start(bf16[16,8,256]{2,1,0:T(8,128)(2,1)S(1)} %collective-permute-done.11.refs_5_) | copy-start | bytes 196612
  46.9 11.0 %collective-permute-start.16 = (bf16[16,8,256]{2,1,0:T(8,128)(2,1)}, bf16[16,8,256]{2,1,0:T(8,128)(2,1)S(1)}, u32[]{:S(2)}, u32[]{:S(2)}) collective-permute-start(bf16[16,8,256]{2,1,0:T(8,128)(2,1)} %get-tuple-element.63), channel_id=1, source_target_pairs={{0,10},{1,11},{2,8},{3,9},{4,14},{5,15},{6,12},{7,13},{8,2},{9,3},... | collective-permute-start | bytes 196616 | tf_op jit(solution)/shard_map/ppermute | solution.py:528
  47.6 53.8 %copy-start.19 = (bf16[16,8,256]{2,1,0:T(8,128)(2,1)}, bf16[16,8,256]{2,1,0:T(8,128)(2,1)S(1)}, u32[]{:S(2)}) copy-start(bf16[16,8,256]{2,1,0:T(8,128)(2,1)S(1)} %collective-permute-done.12.refs_6_) | copy-start | bytes 196612
  47.6 13.1 %collective-permute-start.17 = (bf16[16,8,256]{2,1,0:T(8,128)(2,1)}, bf16[16,8,256]{2,1,0:T(8,128)(2,1)S(1)}, u32[]{:S(2)}, u32[]{:S(2)}) collective-permute-start(bf16[16,8,256]{2,1,0:T(8,128)(2,1)} %get-tuple-element.64), channel_id=1, source_target_pairs={{0,11},{1,10},{2,9},{3,8},{4,15},{5,14},{6,13},{7,12},{8,3},{9,2},... | collective-permute-start | bytes 196616 | tf_op jit(solution)/shard_map/ppermute | solution.py:528
  50.2 51.2 %copy-start.20 = (bf16[16,8,256]{2,1,0:T(8,128)(2,1)}, bf16[16,8,256]{2,1,0:T(8,128)(2,1)S(1)}, u32[]{:S(2)}) copy-start(bf16[16,8,256]{2,1,0:T(8,128)(2,1)S(1)} %collective-permute-done.13.refs_7_) | copy-start | bytes 196612
  50.2 29.3 %collective-permute-start = (bf16[64,8,256]{2,1,0:T(8,128)(2,1)S(1)}, bf16[64,8,256]{2,1,0:T(8,128)(2,1)S(1)}, u32[]{:S(2)}, u32[]{:S(2)}) collective-permute-start(bf16[64,8,256]{2,1,0:T(8,128)(2,1)S(1)} %copy-done.30), channel_id=1, source_target_pairs={{0,1},{1,0},{2,3},{3,2},{4,5},{5,4},{6,7},{7,6},{8,9},{9,8},{10,11... | collective-permute-start | bytes 786440 | tf_op jit(solution)/shard_map/ppermute | solution.py:528
  53.6 47.9 %copy-start.21 = (bf16[16,8,256]{2,1,0:T(8,128)(2,1)}, bf16[16,8,256]{2,1,0:T(8,128)(2,1)S(1)}, u32[]{:S(2)}) copy-start(bf16[16,8,256]{2,1,0:T(8,128)(2,1)S(1)} %collective-permute-done.14.refs_12_) | copy-start | bytes 196612
  53.6 9.2 %collective-permute-start.18 = (bf16[16,8,256]{2,1,0:T(8,128)(2,1)}, bf16[16,8,256]{2,1,0:T(8,128)(2,1)S(1)}, u32[]{:S(2)}, u32[]{:S(2)}) collective-permute-start(bf16[16,8,256]{2,1,0:T(8,128)(2,1)} %get-tuple-element.65), channel_id=1, source_target_pairs={{0,12},{1,13},{2,14},{3,15},{4,8},{5,9},{6,10},{7,11},{8,4},{9,5},... | collective-permute-start | bytes 196616 | tf_op jit(solution)/shard_map/ppermute | solution.py:528
  56.3 45.2 %copy-start.22 = (bf16[16,8,256]{2,1,0:T(8,128)(2,1)}, bf16[16,8,256]{2,1,0:T(8,128)(2,1)S(1)}, u32[]{:S(2)}) copy-start(bf16[16,8,256]{2,1,0:T(8,128)(2,1)S(1)} %collective-permute-done.15.refs_13_) | copy-start | bytes 196612
  56.3 7.7 %collective-permute-start.19 = (bf16[16,8,256]{2,1,0:T(8,128)(2,1)}, bf16[16,8,256]{2,1,0:T(8,128)(2,1)S(1)}, u32[]{:S(2)}, u32[]{:S(2)}) collective-permute-start(bf16[16,8,256]{2,1,0:T(8,128)(2,1)} %get-tuple-element.66), channel_id=1, source_target_pairs={{0,13},{1,12},{2,15},{3,14},{4,9},{5,8},{6,11},{7,10},{8,5},{9,4},... | collective-permute-start | bytes 196616 | tf_op jit(solution)/shard_map/ppermute | solution.py:528
  57.9 43.6 %copy-start.23 = (bf16[16,8,256]{2,1,0:T(8,128)(2,1)}, bf16[16,8,256]{2,1,0:T(8,128)(2,1)S(1)}, u32[]{:S(2)}) copy-start(bf16[16,8,256]{2,1,0:T(8,128)(2,1)S(1)} %collective-permute-done.16.refs_14_) | copy-start | bytes 196612
  57.9 8.6 %collective-permute-start.20 = (bf16[16,8,256]{2,1,0:T(8,128)(2,1)}, bf16[16,8,256]{2,1,0:T(8,128)(2,1)S(1)}, u32[]{:S(2)}, u32[]{:S(2)}) collective-permute-start(bf16[16,8,256]{2,1,0:T(8,128)(2,1)} %get-tuple-element.67), channel_id=1, source_target_pairs={{0,14},{1,15},{2,12},{3,13},{4,10},{5,11},{6,8},{7,9},{8,6},{9,7},... | collective-permute-start | bytes 196616 | tf_op jit(solution)/shard_map/ppermute | solution.py:528
  60.7 40.8 %copy-start.24 = (bf16[16,8,256]{2,1,0:T(8,128)(2,1)}, bf16[16,8,256]{2,1,0:T(8,128)(2,1)S(1)}, u32[]{:S(2)}) copy-start(bf16[16,8,256]{2,1,0:T(8,128)(2,1)S(1)} %collective-permute-done.17.refs_15_) | copy-start | bytes 196612
  60.7 9.8 %collective-permute-start.21 = (bf16[16,8,256]{2,1,0:T(8,128)(2,1)}, bf16[16,8,256]{2,1,0:T(8,128)(2,1)S(1)}, u32[]{:S(2)}, u32[]{:S(2)}) collective-permute-start(bf16[16,8,256]{2,1,0:T(8,128)(2,1)} %get-tuple-element.68), channel_id=1, source_target_pairs={{0,15},{1,14},{2,13},{3,12},{4,11},{5,10},{6,9},{7,8},{8,7},{9,6},... | collective-permute-start | bytes 196616 | tf_op jit(solution)/shard_map/ppermute | solution.py:528
  62.7 38.8 %copy-start.25 = (bf16[16,8,256]{2,1,0:T(8,128)(2,1)}, bf16[16,8,256]{2,1,0:T(8,128)(2,1)S(1)}, u32[]{:S(2)}) copy-start(bf16[16,8,256]{2,1,0:T(8,128)(2,1)S(1)} %collective-permute-done.18.refs_16_) | copy-start | bytes 196612
  62.7 8.8 %collective-permute-start.22 = (bf16[16,8,512]{2,1,0:T(8,128)(2,1)}, bf16[16,8,512]{2,1,0:T(8,128)(2,1)S(1)}, u32[]{:S(2)}, u32[]{:S(2)}) collective-permute-start(bf16[16,8,512]{2,1,0:T(8,128)(2,1)} %get-tuple-element.69), channel_id=1, source_target_pairs={{0,4},{1,5},{2,6},{3,7},{4,0},{5,1},{6,2},{7,3},{8,12},{9,13},{10,... | collective-permute-start | bytes 393224 | tf_op jit(solution)/shard_map/ppermute | solution.py:528
  64.0 37.5 %copy-start.26 = (bf16[16,8,256]{2,1,0:T(8,128)(2,1)}, bf16[16,8,256]{2,1,0:T(8,128)(2,1)S(1)}, u32[]{:S(2)}) copy-start(bf16[16,8,256]{2,1,0:T(8,128)(2,1)S(1)} %collective-permute-done.19.refs_17_) | copy-start | bytes 196612
  64.0 8.4 %collective-permute-start.23 = (bf16[16,8,512]{2,1,0:T(8,128)(2,1)}, bf16[16,8,512]{2,1,0:T(8,128)(2,1)S(1)}, u32[]{:S(2)}, u32[]{:S(2)}) collective-permute-start(bf16[16,8,512]{2,1,0:T(8,128)(2,1)} %get-tuple-element.70), channel_id=1, source_target_pairs={{0,5},{1,4},{2,7},{3,6},{4,1},{5,0},{6,3},{7,2},{8,13},{9,12},{10,... | collective-permute-start | bytes 393224 | tf_op jit(solution)/shard_map/ppermute | solution.py:528
  66.4 35.1 %copy-start.27 = (bf16[16,8,256]{2,1,0:T(8,128)(2,1)}, bf16[16,8,256]{2,1,0:T(8,128)(2,1)S(1)}, u32[]{:S(2)}) copy-start(bf16[16,8,256]{2,1,0:T(8,128)(2,1)S(1)} %collective-permute-done.20.refs_18_) | copy-start | bytes 196612
  66.4 10.2 %collective-permute-start.24 = (bf16[16,8,512]{2,1,0:T(8,128)(2,1)}, bf16[16,8,512]{2,1,0:T(8,128)(2,1)S(1)}, u32[]{:S(2)}, u32[]{:S(2)}) collective-permute-start(bf16[16,8,512]{2,1,0:T(8,128)(2,1)} %get-tuple-element.71), channel_id=1, source_target_pairs={{0,6},{1,7},{2,4},{3,5},{4,2},{5,3},{6,0},{7,1},{8,14},{9,15},{10,... | collective-permute-start | bytes 393224 | tf_op jit(solution)/shard_map/ppermute | solution.py:528
  70.5 31.0 %copy-start.28 = (bf16[16,8,256]{2,1,0:T(8,128)(2,1)}, bf16[16,8,256]{2,1,0:T(8,128)(2,1)S(1)}, u32[]{:S(2)}) copy-start(bf16[16,8,256]{2,1,0:T(8,128)(2,1)S(1)} %collective-permute-done.21.refs_19_) | copy-start | bytes 196612
  70.5 8.3 %collective-permute-start.25 = (bf16[16,8,512]{2,1,0:T(8,128)(2,1)}, bf16[16,8,512]{2,1,0:T(8,128)(2,1)S(1)}, u32[]{:S(2)}, u32[]{:S(2)}) collective-permute-start(bf16[16,8,512]{2,1,0:T(8,128)(2,1)} %get-tuple-element.72), channel_id=1, source_target_pairs={{0,7},{1,6},{2,5},{3,4},{4,3},{5,2},{6,1},{7,0},{8,15},{9,14},{10,... | collective-permute-start | bytes 393224 | tf_op jit(solution)/shard_map/ppermute | solution.py:528
  71.5 30.0 %copy-start.6 = (bf16[16,8,512]{2,1,0:T(8,128)(2,1)}, bf16[16,8,512]{2,1,0:T(8,128)(2,1)S(1)}, u32[]{:S(2)}) copy-start(bf16[16,8,512]{2,1,0:T(8,128)(2,1)S(1)} %collective-permute-done.22.refs_24_) | copy-start | bytes 393220
  71.5 13.1 %collective-permute-start.1 = (bf16[64,8,256]{2,1,0:T(8,128)(2,1)}, bf16[64,8,256]{2,1,0:T(8,128)(2,1)S(1)}, u32[]{:S(2)}, u32[]{:S(2)}) collective-permute-start(bf16[64,8,256]{2,1,0:T(8,128)(2,1)} %get-tuple-element.43), channel_id=1, source_target_pairs={{0,2},{1,3},{2,0},{3,1},{4,6},{5,7},{6,4},{7,5},{8,10},{9,11},{10,... | collective-permute-start | bytes 786440 | tf_op jit(solution)/shard_map/ppermute | solution.py:528
  72.4 17.7 %collective-permute-start.2 = (bf16[64,8,256]{2,1,0:T(8,128)(2,1)S(1)}, bf16[64,8,256]{2,1,0:T(8,128)(2,1)S(1)}, u32[]{:S(2)}, u32[]{:S(2)}) collective-permute-start(bf16[64,8,256]{2,1,0:T(8,128)(2,1)S(1)} %copy-done.29), channel_id=1, source_target_pairs={{0,3},{1,2},{2,1},{3,0},{4,7},{5,6},{6,5},{7,4},{8,11},{9,10},{10,... | collective-permute-start | bytes 786440 | tf_op jit(solution)/shard_map/ppermute | solution.py:528
  76.6 13.6 %collective-permute-start.3 = (bf16[64,8,256]{2,1,0:T(8,128)(2,1)}, bf16[64,8,256]{2,1,0:T(8,128)(2,1)S(1)}, u32[]{:S(2)}, u32[]{:S(2)}) collective-permute-start(bf16[64,8,256]{2,1,0:T(8,128)(2,1)} %get-tuple-element.50), channel_id=1, source_target_pairs={{0,1},{1,0},{2,3},{3,2},{4,5},{5,4},{6,7},{7,6},{8,9},{9,8},{10,11... | collective-permute-start | bytes 786440 | tf_op jit(solution)/shard_map/ppermute | solution.py:528
  78.7 17.1 %collective-permute-start.4 = (bf16[64,8,256]{2,1,0:T(8,128)(2,1)}, bf16[64,8,256]{2,1,0:T(8,128)(2,1)S(1)}, u32[]{:S(2)}, u32[]{:S(2)}) collective-permute-start(bf16[64,8,256]{2,1,0:T(8,128)(2,1)} %get-tuple-element.51), channel_id=1, source_target_pairs={{0,2},{1,3},{2,0},{3,1},{4,6},{5,7},{6,4},{7,5},{8,10},{9,11},{10,... | collective-permute-start | bytes 786440 | tf_op jit(solution)/shard_map/ppermute | solution.py:528
  79.6 21.8 %collective-permute-start.5 = (bf16[64,8,256]{2,1,0:T(8,128)(2,1)}, bf16[64,8,256]{2,1,0:T(8,128)(2,1)S(1)}, u32[]{:S(2)}, u32[]{:S(2)}) collective-permute-start(bf16[64,8,256]{2,1,0:T(8,128)(2,1)} %get-tuple-element.52), channel_id=1, source_target_pairs={{0,3},{1,2},{2,1},{3,0},{4,7},{5,6},{6,5},{7,4},{8,11},{9,10},{10,... | collective-permute-start | bytes 786440 | tf_op jit(solution)/shard_map/ppermute | solution.py:528
  108.9 9.5 %collective-permute-start.26 = (bf16[2,16,16,128]{3,2,1,0:T(8,128)(2,1)}, bf16[2,16,16,128]{3,2,1,0:T(8,128)(2,1)S(1)}, u32[]{:S(2)}, u32[]{:S(2)}) collective-permute-start(bf16[2,16,16,128]{3,2,1,0:T(8,128)(2,1)} %get-tuple-element.74), channel_id=1, source_target_pairs={{0,4},{1,5},{2,6},{3,7},{4,0},{5,1},{6,2},{7,3},{8,12},{9,13},{10,... | collective-permute-start | bytes 393224 | tf_op jit(solution)/shard_map/ppermute | solution.py:528
  109.3 13.1 %collective-permute-start.27 = (bf16[2,16,16,128]{3,2,1,0:T(8,128)(2,1)}, bf16[2,16,16,128]{3,2,1,0:T(8,128)(2,1)S(1)}, u32[]{:S(2)}, u32[]{:S(2)}) collective-permute-start(bf16[2,16,16,128]{3,2,1,0:T(8,128)(2,1)} %get-tuple-element.75), channel_id=1, source_target_pairs={{0,8},{1,9},{2,10},{3,11},{4,12},{5,13},{6,14},{7,15},{8,0},{9,1},... | collective-permute-start | bytes 393224 | tf_op jit(solution)/shard_map/ppermute | solution.py:528
  111.5 10.9 %collective-permute-start.28 = (bf16[2,16,16,128]{3,2,1,0:T(8,128)(2,1)}, bf16[2,16,16,128]{3,2,1,0:T(8,128)(2,1)S(1)}, u32[]{:S(2)}, u32[]{:S(2)}) collective-permute-start(bf16[2,16,16,128]{3,2,1,0:T(8,128)(2,1)} %get-tuple-element.76), channel_id=1, source_target_pairs={{0,12},{1,13},{2,14},{3,15},{4,8},{5,9},{6,10},{7,11},{8,4},{9,5},... | collective-permute-start | bytes 393224 | tf_op jit(solution)/shard_map/ppermute | solution.py:528
  (12 other events, 150.5 us)

commit v4 on v3

--- a/solution.py
+++ b/solution.py
@@ -254,10 +254,10 @@
                 return carry
 
             lax.fori_loop(0, kept // chans // near, some_rows, 0)
-            for index, (dz, of, count) in enumerate(sends):
+            for index, (dz, of, skip, count) in enumerate(sends):
                 if of != dc:
                     continue
-                first = chan * (kept // chans * parts)
+                first = chan * (kept // chans * parts) + skip
                 if dz is not None:
                     station = lax.bitwise_xor(lax.axis_index("stn"), dz)
                     first = first + station * (kept // chans * parts // stations)
@@ -313,7 +313,7 @@
     places = tuple(index for index, _ in merged)
     shapes = [
         jax.ShapeDtypeStruct((count, inputs, (4 if index in places else 2) * block), bf16)
-        for index, (_, _, count) in enumerate(sends)
+        for index, (_, _, _, count) in enumerate(sends)
     ]
     return pl.pallas_call(
         functools.partial(spectra_kernel, sizes=sizes, sends=sends, merged=places, turned=turned),
@@ -428,21 +428,16 @@
     part = groups // stages
     copies = []
     for stage in range(stages):
-        for index, (dz, dc, mine, lane) in enumerate(pieces):
+        for index, (dz, dc, mine, first) in enumerate(pieces):
             chan = lax.bitwise_xor(lax.axis_index("chan"), dc)
             block = lax.bitwise_xor(here, dz) if blocks > 1 else 0
-            start = stage * part
+            start = first + stage * part
             if mine:
                 start = start + lax.axis_index("stn") * mine
             copies.append(
                 pltpu.make_async_copy(
                     arrived[index].at[pl.ds(start, part)],
-                    r_ref.at[
-                        block * chans + chan,
-                        pl.ds(stage * part, part),
-                        :,
-                        pl.ds(lane, arrived[index].shape[-1]),
-                    ],
+                    r_ref.at[block * chans + chan, pl.ds(stage * part, part)],
                     sems.at[stage * len(pieces) + index],
                 )
             )
@@ -472,8 +467,7 @@
 
 
 def correlate_pieces(arrays, pieces, blocks, chans, groups, distances, scale):
-    inputs = arrays[0].shape[1]
-    wide = max(lane + value.shape[2] for value, (_, _, _, lane) in zip(arrays, pieces))
+    inputs, wide = arrays[0].shape[1:]
     block_inputs = chans * inputs
     out_rows = block_inputs * block_inputs // LANES
     per_step = math.gcd(groups // 2, 8 // blocks)
@@ -541,7 +535,7 @@
     scale = 1.0 / (spectra_count * AVG)
     frames_first = voltages.transpose(1, 0, 2)
     if not direct(stations, chans):
-        sends = tuple((None, dc, groups // chans) for dc in range(chans))
+        sends = tuple((None, dc, 0, groups // chans) for dc in range(chans))
         slices = make_spectra(frames_first, taps, sends, stations, chans, False)
         send = jnp.concatenate(slices, axis=0).reshape(chans * stations, here, inputs_here, -1)
         turned = lax.all_to_all(send, ("chan", "stn"), 0, 0, tiled=True)
@@ -549,45 +543,37 @@
         back = lax.all_to_all(tiles, "stn", 0, 0, tiled=True)
         out = back.transpose(1, 0, 2, 3, 4)
     else:
-        near = [(None, dc, here * stations) for dc in range(chans)]
-        far = [(dz, dc, here) for dz in (2, 3) for dc in range(chans)]
-        mid = [(1, dc, here) for dc in range(chans)]
-        sends = tuple(far + near + mid)
-        own_pieces, own_arrays, pieces, arrays = [], [], [], []
-        kept_back = ()
-        for half in range(HALVES):
-            sent = make_spectra(
-                frames_first,
-                taps,
-                sends,
-                stations,
-                chans,
-                True,
-                half * spectra_count // HALVES,
-                HALVES,
-                kept_back,
-            )
-            if half == 0:
-                kept_back = tuple((len(far + near) + index, value) for index, value in enumerate(sent[-chans:]))
-            lane = half * 2 * AVG * spectra_count // HALVES
-            for (dz, dc, _), value in zip(sends, sent):
-                if dz == 1 and half == 0:
+        part = here // CHUNKS
+        sends = [(dz, dc, chunk * part, part) for chunk in range(CHUNKS) for dz in (2, 3) for dc in range(chans)]
+        sends += [(None, dc, 0, here * stations) for dc in range(chans)]
+        sends += [(1, dc, 0, here) for dc in range(chans)]
+        sent = make_spectra(frames_first, taps, tuple(sends), stations, chans, True)
+        got = {}
+        for (dz, dc, skip, _), value in zip(sends, sent):
+            stays = dz is None and dc == 0
+            got[dz, dc, skip // part] = value if stays else shifted(value, stations, chans, dz or 0, dc)
+        pieces = [(0, dc, 0, 0) for dc in range(chans)]
+        arrays = [got[None, dc, 0] for dc in range(chans)]
+        (own,) = correlate_pieces(arrays, pieces, 1, chans, here * stations, (0,), scale)
+        back = {}
+        for chunk in range(CHUNKS):
+            pieces, arrays = [], []
+            for (dz, dc, which), value in got.items():
+                if dz in (2, 3) and which != chunk:
                     continue
-                moved = value if dz is None and dc == 0 else shifted(value, stations, chans, dz or 0, dc)
-                if dz is None:
-                    own_pieces.append((0, dc, 0, lane))
-                    own_arrays.append(moved)
-                pieces.append((dz or 0, dc, here if dz is None else 0, 0 if dz == 1 else lane))
-                arrays.append(moved)
-        (own,) = correlate_pieces(own_arrays, own_pieces, 1, chans, here * stations, (0,), scale)
-        outs = correlate_pieces(arrays, pieces, stations, chans, here, tuple(range(1, reach)), scale)
-        back = [outs[dz] if dz == 0 else shifted(outs[dz], stations, chans, dz, 0) for dz in range(stations)]
-        out = assemble(own, back, stations, 1)
+                pieces.append((dz or 0, dc, 0 if dz else here, 0 if dz in (2, 3) else chunk * part))
+                arrays.append(value)
+            outs = correlate_pieces(arrays, pieces, stations, chans, part, tuple(range(1, reach)), scale)
+            for dz in range(stations):
+                back[dz, chunk] = outs[dz] if dz == 0 else shifted(outs[dz], stations, chans, dz, 0)
+        parts = [back[dz, chunk] for dz in range(stations) for chunk in range(CHUNKS)]
+        out = assemble(own, parts, stations, CHUNKS)
     out = out.reshape(reach, stations * here, pairs // LANES, 2, LANES)
     return out.transpose(0, 1, 3, 2, 4).reshape(1, reach, stations * here, 2, pairs)
 
 
-HALVES = 2
+HALVES = 1
+CHUNKS = 2
 
 
 def direct(stations, chans):

time: 126 us -> 104 us (0.83)
  waiting for transfers between devices: 37.7 us -> 26.6 us
  Pallas kernels: 36.8 us -> 30.7 us
  starting transfers between devices: 49.1 us -> 44.2 us
    ppermute x29, waiting for transfers between devices: 37.7 us -> 26.6 us  [shifted(): return lax.ppermute(value, ('stn', 'chan'), pairs)]
    pallas_call x2 -> x1, Pallas kernels: 22.9 us -> 15.5 us  [make_spectra(): pl.pallas_call(functools.partial(spectra_kernel, sizes=sizes, sends=sends...]
    ppermute x29, starting transfers between devices: 49.1 us -> 44.2 us  [shifted(): return lax.ppermute(value, ('stn', 'chan'), pairs)]
    pallas_call x2 -> x3, Pallas kernels: 11.8 us -> 13.1 us  [correlate_pieces(): pl.pallas_call(functools.partial(pieces_kernel, sizes=sizes, pieces=piece...]
  transfers between devices with their start and end apart: 29 -> 29, of which waited for: 13 -> 10; matrix products, arithmetic and copies ran while one was open for 0% -> 0% of each run, Pallas kernels for 13% -> 13%
where the time goes in v4:
time: 104 us
  starting transfers between devices  44.2 us (42%)
  Pallas kernels  30.7 us (30%)
  waiting for transfers between devices  26.6 us (26%)
  local copies, waits for them, and re-layouts  1.91 us (2%)
    ppermute x29, starting transfers between devices, shifted(): return lax.ppermute(value, ('stn', 'chan'), pairs)  44.2 us
    ppermute x29, waiting for transfers between devices, shifted(): return lax.ppermute(value, ('stn', 'chan'), pairs)  26.6 us
    pallas_call x1, Pallas kernels, make_spectra(): pl.pallas_call(functools.partial(spectra_kernel, sizes=sizes, sends=sends...  15.5 us
    pallas_call x3, Pallas kernels, correlate_pieces(): pl.pallas_call(functools.partial(pieces_kernel, sizes=sizes, pieces=piece...  13.1 us
  transfers between devices with their start and end apart: 29, of which 10 were waited for; matrix products, arithmetic and copies ran while one was open for 0% of the time, Pallas kernels for 13%

profile of v4, /device:TPU:0, one launch (start us, length us, event | category | flops | bytes accessed | tf_op | source)
XLA Modules:
  0.0 103.8 jit_solution(13111061912292505514)
XLA Ops:
  0.0 15.5 %spectra.1 = (bf16[8,8,512]{2,1,0:T(8,128)(2,1)}, bf16[8,8,512]{2,1,0:T(8,128)(2,1)}, bf16[8,8,512]{2,1,0:T(8,128)(2,1)}, bf16[8,8,512]{2,1,0:T(8,128)(2,1)}, bf...) custom-call(f32[528,128]{1,0:T(8,128)} %constant.4.clone.tw_ref, ...), custom_call_target="tpu_custom_call" | custom-call | tf_op jit(solution)/shard_map/spectra/pallas_call | solution.py:318
  15.5 4.1 %collective-permute-start.3 = (bf16[8,8,512]{2,1,0:T(8,128)(2,1)}, bf16[8,8,512]{2,1,0:T(8,128)(2,1)S(1)}, u32[]{:S(2)}, u32[]{:S(2)}) collective-permute-start(bf16[8,8,512]{2,1,0:T(8,128)(2,1)} %get-tuple-element.41), channel_id=1, source_target_pairs={{0,8},{1,9},{2,10},{3,11},{4,12},{5,13},{6,14},{7,15},{8,0},{9,1},... | collective-permute-start | bytes 196616 | tf_op jit(solution)/shard_map/ppermute | solution.py:522
  19.6 0.0 collective-permute-start.4
  19.6 3.0 %collective-permute-start.5 = (bf16[8,8,512]{2,1,0:T(8,128)(2,1)}, bf16[8,8,512]{2,1,0:T(8,128)(2,1)S(1)}, u32[]{:S(2)}, u32[]{:S(2)}) collective-permute-start(bf16[8,8,512]{2,1,0:T(8,128)(2,1)} %get-tuple-element.43), channel_id=1, source_target_pairs={{0,10},{1,11},{2,8},{3,9},{4,14},{5,15},{6,12},{7,13},{8,2},{9,3},... | collective-permute-start | bytes 196616 | tf_op jit(solution)/shard_map/ppermute | solution.py:522
  22.6 0.8 collective-permute-start.15
  23.5 2.1 %collective-permute-start.16 = (bf16[8,8,512]{2,1,0:T(8,128)(2,1)}, bf16[8,8,512]{2,1,0:T(8,128)(2,1)S(1)}, u32[]{:S(2)}, u32[]{:S(2)}) collective-permute-start(bf16[8,8,512]{2,1,0:T(8,128)(2,1)} %get-tuple-element.55), channel_id=1, source_target_pairs={{0,9},{1,8},{2,11},{3,10},{4,13},{5,12},{6,15},{7,14},{8,1},{9,0},... | collective-permute-start | bytes 196616 | tf_op jit(solution)/shard_map/ppermute | solution.py:522
  25.6 0.8 collective-permute-start.17
  26.4 1.5 %collective-permute-done.4.refs_1_ = bf16[8,8,512]{2,1,0:T(8,128)(2,1)S(1)} collective-permute-done((bf16[8,8,512]{2,1,0:T(8,128)(2,1)}, bf16[8,8,512]{2,1,0:T(8,128)(2,1)S(1)}, u32[]{:S(2)}, u32[]{:S(2)}) %collective-permute-start.4) | collective-permute-done | bytes 65568 | tf_op jit(solution)/shard_map/ppermute | solution.py:522
  27.9 0.0 collective-permute-start
  27.9 5.1 %collective-permute-done.5.refs_2_ = bf16[8,8,512]{2,1,0:T(8,128)(2,1)S(1)} collective-permute-done((bf16[8,8,512]{2,1,0:T(8,128)(2,1)}, bf16[8,8,512]{2,1,0:T(8,128)(2,1)S(1)}, u32[]{:S(2)}, u32[]{:S(2)}) %collective-permute-start.5) | collective-permute-done | bytes 65568 | tf_op jit(solution)/shard_map/ppermute | solution.py:522
  33.0 0.1 collective-permute-start.1
  33.1 0.0 collective-permute-done.15.refs_0_
  33.1 1.6 %collective-permute-start.2 = (bf16[64,8,512]{2,1,0:T(8,128)(2,1)}, bf16[64,8,512]{2,1,0:T(8,128)(2,1)S(1)}, u32[]{:S(2)}, u32[]{:S(2)}) collective-permute-start(bf16[64,8,512]{2,1,0:T(8,128)(2,1)} %get-tuple-element.40), channel_id=1, source_target_pairs={{0,3},{1,2},{2,1},{3,0},{4,7},{5,6},{6,5},{7,4},{8,11},{9,10},{10,... | collective-permute-start | bytes 1572872 | tf_op jit(solution)/shard_map/ppermute | solution.py:522
  34.7 0.3 collective-permute-done.16.refs_1_
  34.9 0.3 collective-permute-start.18
  35.2 3.5 %collective-permute-done.17.refs_2_ = bf16[8,8,512]{2,1,0:T(8,128)(2,1)S(1)} collective-permute-done((bf16[8,8,512]{2,1,0:T(8,128)(2,1)}, bf16[8,8,512]{2,1,0:T(8,128)(2,1)S(1)}, u32[]{:S(2)}, u32[]{:S(2)}) %collective-permute-start.17) | collective-permute-done | bytes 65568 | tf_op jit(solution)/shard_map/ppermute | solution.py:522
  38.7 4.6 %collective-permute-start.19 = (bf16[8,8,512]{2,1,0:T(8,128)(2,1)}, bf16[8,8,512]{2,1,0:T(8,128)(2,1)S(1)}, u32[]{:S(2)}, u32[]{:S(2)}) collective-permute-start(bf16[8,8,512]{2,1,0:T(8,128)(2,1)} %get-tuple-element.58), channel_id=1, source_target_pairs={{0,12},{1,13},{2,14},{3,15},{4,8},{5,9},{6,10},{7,11},{8,4},{9,5},... | collective-permute-start | bytes 196616 | tf_op jit(solution)/shard_map/ppermute | solution.py:522
  43.3 3.4 %collective-permute-start.20 = (bf16[8,8,512]{2,1,0:T(8,128)(2,1)}, bf16[8,8,512]{2,1,0:T(8,128)(2,1)S(1)}, u32[]{:S(2)}, u32[]{:S(2)}) collective-permute-start(bf16[8,8,512]{2,1,0:T(8,128)(2,1)} %get-tuple-element.59), channel_id=1, source_target_pairs={{0,13},{1,12},{2,15},{3,14},{4,9},{5,8},{6,11},{7,10},{8,5},{9,4},... | collective-permute-start | bytes 196616 | tf_op jit(solution)/shard_map/ppermute | solution.py:522
  46.7 2.9 %collective-permute-start.21 = (bf16[8,8,512]{2,1,0:T(8,128)(2,1)}, bf16[8,8,512]{2,1,0:T(8,128)(2,1)S(1)}, u32[]{:S(2)}, u32[]{:S(2)}) collective-permute-start(bf16[8,8,512]{2,1,0:T(8,128)(2,1)} %get-tuple-element.60), channel_id=1, source_target_pairs={{0,14},{1,15},{2,12},{3,13},{4,10},{5,11},{6,8},{7,9},{8,6},{9,7},... | collective-permute-start | bytes 196616 | tf_op jit(solution)/shard_map/ppermute | solution.py:522
  49.7 2.9 %collective-permute-start.22 = (bf16[8,8,512]{2,1,0:T(8,128)(2,1)}, bf16[8,8,512]{2,1,0:T(8,128)(2,1)S(1)}, u32[]{:S(2)}, u32[]{:S(2)}) collective-permute-start(bf16[8,8,512]{2,1,0:T(8,128)(2,1)} %get-tuple-element.61), channel_id=1, source_target_pairs={{0,15},{1,14},{2,13},{3,12},{4,11},{5,10},{6,9},{7,8},{8,7},{9,6},... | collective-permute-start | bytes 196616 | tf_op jit(solution)/shard_map/ppermute | solution.py:522
  52.5 1.5 %collective-permute-done.21.refs_6_ = bf16[8,8,512]{2,1,0:T(8,128)(2,1)S(1)} collective-permute-done((bf16[8,8,512]{2,1,0:T(8,128)(2,1)}, bf16[8,8,512]{2,1,0:T(8,128)(2,1)S(1)}, u32[]{:S(2)}, u32[]{:S(2)}) %collective-permute-start.21) | collective-permute-done | bytes 65568 | tf_op jit(solution)/shard_map/ppermute | solution.py:522
  54.0 2.9 %collective-permute-done.22.refs_7_ = bf16[8,8,512]{2,1,0:T(8,128)(2,1)S(1)} collective-permute-done((bf16[8,8,512]{2,1,0:T(8,128)(2,1)}, bf16[8,8,512]{2,1,0:T(8,128)(2,1)S(1)}, u32[]{:S(2)}, u32[]{:S(2)}) %collective-permute-start.22) | collective-permute-done | bytes 65568 | tf_op jit(solution)/shard_map/ppermute | solution.py:522
  56.9 2.3 %collective-permute-done.11.refs_12_ = bf16[16,8,512]{2,1,0:T(8,128)(2,1)S(1)} collective-permute-done((bf16[16,8,512]{2,1,0:T(8,128)(2,1)}, bf16[16,8,512]{2,1,0:T(8,128)(2,1)S(1)}, u32[]{:S(2)}, u32[]{:S(2)}) %collective-permute-start.11) | collective-permute-done | bytes 131104 | tf_op jit(solution)/shard_map/ppermute | solution.py:522
  59.2 0.7 collective-permute-start.13
  59.9 3.0 %collective-permute-done.12.refs_13_ = bf16[16,8,512]{2,1,0:T(8,128)(2,1)S(1)} collective-permute-done((bf16[16,8,512]{2,1,0:T(8,128)(2,1)}, bf16[16,8,512]{2,1,0:T(8,128)(2,1)S(1)}, u32[]{:S(2)}, u32[]{:S(2)}) %collective-permute-start.12) | collective-permute-done | bytes 131104 | tf_op jit(solution)/shard_map/ppermute | solution.py:522
  62.9 2.4 %collective-permute-done.13.refs_14_ = bf16[16,8,512]{2,1,0:T(8,128)(2,1)S(1)} collective-permute-done((bf16[16,8,512]{2,1,0:T(8,128)(2,1)}, bf16[16,8,512]{2,1,0:T(8,128)(2,1)S(1)}, u32[]{:S(2)}, u32[]{:S(2)}) %collective-permute-start.13) | collective-permute-done | bytes 131104 | tf_op jit(solution)/shard_map/ppermute | solution.py:522
  65.3 4.2 %collective-permute-done.14.refs_15_ = bf16[16,8,512]{2,1,0:T(8,128)(2,1)S(1)} collective-permute-done((bf16[16,8,512]{2,1,0:T(8,128)(2,1)}, bf16[16,8,512]{2,1,0:T(8,128)(2,1)S(1)}, u32[]{:S(2)}, u32[]{:S(2)}) %collective-permute-start.14) | collective-permute-done | bytes 131104 | tf_op jit(solution)/shard_map/ppermute | solution.py:522
  69.5 1.2 %collective-permute-start.7 = (bf16[8,8,512]{2,1,0:T(8,128)(2,1)}, bf16[8,8,512]{2,1,0:T(8,128)(2,1)S(1)}, u32[]{:S(2)}, u32[]{:S(2)}) collective-permute-start(bf16[8,8,512]{2,1,0:T(8,128)(2,1)} %get-tuple-element.45), channel_id=1, source_target_pairs={{0,12},{1,13},{2,14},{3,15},{4,8},{5,9},{6,10},{7,11},{8,4},{9,5},... | collective-permute-start | bytes 196616 | tf_op jit(solution)/shard_map/ppermute | solution.py:522
  70.7 2.0 %collective-permute-start.8 = (bf16[8,8,512]{2,1,0:T(8,128)(2,1)}, bf16[8,8,512]{2,1,0:T(8,128)(2,1)S(1)}, u32[]{:S(2)}, u32[]{:S(2)}) collective-permute-start(bf16[8,8,512]{2,1,0:T(8,128)(2,1)} %get-tuple-element.46), channel_id=1, source_target_pairs={{0,13},{1,12},{2,15},{3,14},{4,9},{5,8},{6,11},{7,10},{8,5},{9,4},... | collective-permute-start | bytes 196616 | tf_op jit(solution)/shard_map/ppermute | solution.py:522
  72.8 2.4 %collective-permute-start.9 = (bf16[8,8,512]{2,1,0:T(8,128)(2,1)}, bf16[8,8,512]{2,1,0:T(8,128)(2,1)S(1)}, u32[]{:S(2)}, u32[]{:S(2)}) collective-permute-start(bf16[8,8,512]{2,1,0:T(8,128)(2,1)} %get-tuple-element.47), channel_id=1, source_target_pairs={{0,14},{1,15},{2,12},{3,13},{4,10},{5,11},{6,8},{7,9},{8,6},{9,7},... | collective-permute-start | bytes 196616 | tf_op jit(solution)/shard_map/ppermute | solution.py:522
  75.2 2.3 %collective-permute-start.10 = (bf16[8,8,512]{2,1,0:T(8,128)(2,1)}, bf16[8,8,512]{2,1,0:T(8,128)(2,1)S(1)}, u32[]{:S(2)}, u32[]{:S(2)}) collective-permute-start(bf16[8,8,512]{2,1,0:T(8,128)(2,1)} %get-tuple-element.48), channel_id=1, source_target_pairs={{0,15},{1,14},{2,13},{3,12},{4,11},{5,10},{6,9},{7,8},{8,7},{9,6},... | collective-permute-start | bytes 196616 | tf_op jit(solution)/shard_map/ppermute | solution.py:522
  77.6 4.1 %shard_map.48 = (bf16[2,8,16,128]{3,2,1,0:T(8,128)(2,1)}, bf16[2,8,16,128]{3,2,1,0:T(8,128)(2,1)}, bf16[2,8,16,128]{3,2,1,0:T(8,128)(2,1)}, bf16[2,8,16,128]{3,2,1,0:T(8,128)(2,1)}) custom-call(bf16[8,8,512]{2,1,0:T(8,128)(2,1)} %copy-done.10, bf16[8,8,512]{2,1,0:T(8,128)(2,1)} %copy-done.11, bf16[8,8,512]{2,1,0:T(8,128)(2,1)} %copy-done.12, ...), custom_call_target="tpu_custom_call" | custom-call | tf_op jit(solution)/shard_map/pallas_call | solution.py:476
  81.8 0.1 collective-permute-start.24
  81.9 1.8 %collective-permute-start.26 = (bf16[2,8,16,128]{3,2,1,0:T(8,128)(2,1)}, bf16[2,8,16,128]{3,2,1,0:T(8,128)(2,1)S(1)}, u32[]{:S(2)}, u32[]{:S(2)}) collective-permute-start(bf16[2,8,16,128]{3,2,1,0:T(8,128)(2,1)} %get-tuple-element.66), channel_id=1, source_target_pairs={{0,8},{1,9},{2,10},{3,11},{4,12},{5,13},{6,14},{7,15},{8,0},{9,1},... | collective-permute-start | bytes 196616 | tf_op jit(solution)/shard_map/ppermute | solution.py:522
  83.7 2.6 %collective-permute-start.28 = (bf16[2,8,16,128]{3,2,1,0:T(8,128)(2,1)}, bf16[2,8,16,128]{3,2,1,0:T(8,128)(2,1)S(1)}, u32[]{:S(2)}, u32[]{:S(2)}) collective-permute-start(bf16[2,8,16,128]{3,2,1,0:T(8,128)(2,1)} %get-tuple-element.68), channel_id=1, source_target_pairs={{0,12},{1,13},{2,14},{3,15},{4,8},{5,9},{6,10},{7,11},{8,4},{9,5},... | collective-permute-start | bytes 196616 | tf_op jit(solution)/shard_map/ppermute | solution.py:522
  86.3 0.6 copy-done.24
  86.9 0.6 copy-done.25
  87.5 4.1 %shard_map.47 = (bf16[2,8,16,128]{3,2,1,0:T(8,128)(2,1)}, bf16[2,8,16,128]{3,2,1,0:T(8,128)(2,1)}, bf16[2,8,16,128]{3,2,1,0:T(8,128)(2,1)}, bf16[2,8,16,128]{3,2,1,0:T(8,128)(2,1)}) custom-call(bf16[8,8,512]{2,1,0:T(8,128)(2,1)} %copy-done.7, bf16[8,8,512]{2,1,0:T(8,128)(2,1)} %copy-done.8, bf16[8,8,512]{2,1,0:T(8,128)(2,1)} %copy-done.9, ...), custom_call_target="tpu_custom_call" | custom-call | tf_op jit(solution)/shard_map/pallas_call | solution.py:476
  91.7 0.1 collective-permute-start.23
  91.7 1.8 %collective-permute-start.25 = (bf16[2,8,16,128]{3,2,1,0:T(8,128)(2,1)}, bf16[2,8,16,128]{3,2,1,0:T(8,128)(2,1)S(1)}, u32[]{:S(2)}, u32[]{:S(2)}) collective-permute-start(bf16[2,8,16,128]{3,2,1,0:T(8,128)(2,1)} %get-tuple-element.65), channel_id=1, source_target_pairs={{0,8},{1,9},{2,10},{3,11},{4,12},{5,13},{6,14},{7,15},{8,0},{9,1},... | collective-permute-start | bytes 196616 | tf_op jit(solution)/shard_map/ppermute | solution.py:522
  93.5 2.6 %collective-permute-start.27 = (bf16[2,8,16,128]{3,2,1,0:T(8,128)(2,1)}, bf16[2,8,16,128]{3,2,1,0:T(8,128)(2,1)S(1)}, u32[]{:S(2)}, u32[]{:S(2)}) collective-permute-start(bf16[2,8,16,128]{3,2,1,0:T(8,128)(2,1)} %get-tuple-element.67), channel_id=1, source_target_pairs={{0,12},{1,13},{2,14},{3,15},{4,8},{5,9},{6,10},{7,11},{8,4},{9,5},... | collective-permute-start | bytes 196616 | tf_op jit(solution)/shard_map/ppermute | solution.py:522
  96.1 4.9 %shard_map.46.own_ref = bf16[1,64,16,128]{3,2,1,0:T(8,128)(2,1)} custom-call(bf16[64,8,512]{2,1,0:T(8,128)(2,1)} %get-tuple-element.37.refs_0_.refs_8_, bf16[64,8,512]{2,1,0:T(8,128)(2,1)} %copy-done, bf16[64,8,512]{2,1,0:T(8,128)(2,1)} %copy-done.1, bf16[64,8,512]{2,1,0:T(8,128)(2,1)} %copy-done.2), custom_call_target="tpu_custom_call" | custom-call | tf_op jit(solution)/shard_map/pallas_call | solution.py:476
  101.1 0.5 copy-done.21
  101.7 0.0 copy-done.23
  101.7 0.0 copy-done.26
  101.7 0.0 copy-done.27
  101.7 0.0 copy-done.28
  101.8 2.0 %assemble.1 = bf16[3,64,16,128]{3,2,1,0:T(8,128)(2,1)} custom-call(bf16[1,64,16,128]{3,2,1,0:T(8,128)(2,1)} %shard_map.46.own_ref, bf16[2,8,16,128]{3,2,1,0:T(8,128)(2,1)} %get-tuple-element.53.refs_0_, bf16[2,8,16,128]{3,2,1,0:T(8,128)(2,1)} %get-tuple-element.62.refs_1_, bf16[2,8,16,128]{3,2,1,0:T(8,128)(2,1)} %copy-done.26, ...), custom_call_target="tpu_custom_call" | custom-call | tf_op jit(solution)/shard_map/assemble/pallas_call | solution.py:507
  (73 shorter events, 0.2 us)
Async XLA Ops:
  15.5 10.1 %collective-permute-start.3 = (bf16[8,8,512]{2,1,0:T(8,128)(2,1)}, bf16[8,8,512]{2,1,0:T(8,128)(2,1)S(1)}, u32[]{:S(2)}, u32[]{:S(2)}) collective-permute-start(bf16[8,8,512]{2,1,0:T(8,128)(2,1)} %get-tuple-element.41), channel_id=1, source_target_pairs={{0,8},{1,9},{2,10},{3,11},{4,12},{5,13},{6,14},{7,15},{8,0},{9,1},... | collective-permute-start | bytes 196616 | tf_op jit(solution)/shard_map/ppermute | solution.py:522
  19.6 8.3 %collective-permute-start.4 = (bf16[8,8,512]{2,1,0:T(8,128)(2,1)}, bf16[8,8,512]{2,1,0:T(8,128)(2,1)S(1)}, u32[]{:S(2)}, u32[]{:S(2)}) collective-permute-start(bf16[8,8,512]{2,1,0:T(8,128)(2,1)} %get-tuple-element.42), channel_id=1, source_target_pairs={{0,9},{1,8},{2,11},{3,10},{4,13},{5,12},{6,15},{7,14},{8,1},{9,0},... | collective-permute-start | bytes 196616 | tf_op jit(solution)/shard_map/ppermute | solution.py:522
  19.6 13.4 %collective-permute-start.5 = (bf16[8,8,512]{2,1,0:T(8,128)(2,1)}, bf16[8,8,512]{2,1,0:T(8,128)(2,1)S(1)}, u32[]{:S(2)}, u32[]{:S(2)}) collective-permute-start(bf16[8,8,512]{2,1,0:T(8,128)(2,1)} %get-tuple-element.43), channel_id=1, source_target_pairs={{0,10},{1,11},{2,8},{3,9},{4,14},{5,15},{6,12},{7,13},{8,2},{9,3},... | collective-permute-start | bytes 196616 | tf_op jit(solution)/shard_map/ppermute | solution.py:522
  22.6 10.5 %collective-permute-start.15 = (bf16[8,8,512]{2,1,0:T(8,128)(2,1)}, bf16[8,8,512]{2,1,0:T(8,128)(2,1)S(1)}, u32[]{:S(2)}, u32[]{:S(2)}) collective-permute-start(bf16[8,8,512]{2,1,0:T(8,128)(2,1)} %get-tuple-element.54), channel_id=1, source_target_pairs={{0,8},{1,9},{2,10},{3,11},{4,12},{5,13},{6,14},{7,15},{8,0},{9,1},... | collective-permute-start | bytes 196616 | tf_op jit(solution)/shard_map/ppermute | solution.py:522
  23.5 11.5 %collective-permute-start.16 = (bf16[8,8,512]{2,1,0:T(8,128)(2,1)}, bf16[8,8,512]{2,1,0:T(8,128)(2,1)S(1)}, u32[]{:S(2)}, u32[]{:S(2)}) collective-permute-start(bf16[8,8,512]{2,1,0:T(8,128)(2,1)} %get-tuple-element.55), channel_id=1, source_target_pairs={{0,9},{1,8},{2,11},{3,10},{4,13},{5,12},{6,15},{7,14},{8,1},{9,0},... | collective-permute-start | bytes 196616 | tf_op jit(solution)/shard_map/ppermute | solution.py:522
  25.6 60.7 %copy-start.7 = (bf16[8,8,512]{2,1,0:T(8,128)(2,1)}, bf16[8,8,512]{2,1,0:T(8,128)(2,1)S(1)}, u32[]{:S(2)}) copy-start(bf16[8,8,512]{2,1,0:T(8,128)(2,1)S(1)} %collective-permute-done.3.refs_0_) | copy-start | bytes 196612
  25.6 13.2 %collective-permute-start.17 = (bf16[8,8,512]{2,1,0:T(8,128)(2,1)}, bf16[8,8,512]{2,1,0:T(8,128)(2,1)S(1)}, u32[]{:S(2)}, u32[]{:S(2)}) collective-permute-start(bf16[8,8,512]{2,1,0:T(8,128)(2,1)} %get-tuple-element.56), channel_id=1, source_target_pairs={{0,10},{1,11},{2,8},{3,9},{4,14},{5,15},{6,12},{7,13},{8,2},{9,3},... | collective-permute-start | bytes 196616 | tf_op jit(solution)/shard_map/ppermute | solution.py:522
  27.9 58.4 %copy-start.8 = (bf16[8,8,512]{2,1,0:T(8,128)(2,1)}, bf16[8,8,512]{2,1,0:T(8,128)(2,1)S(1)}, u32[]{:S(2)}) copy-start(bf16[8,8,512]{2,1,0:T(8,128)(2,1)S(1)} %collective-permute-done.4.refs_1_) | copy-start | bytes 196612
  27.9 42.8 %collective-permute-start = (bf16[64,8,512]{2,1,0:T(8,128)(2,1)}, bf16[64,8,512]{2,1,0:T(8,128)(2,1)S(1)}, u32[]{:S(2)}, u32[]{:S(2)}) collective-permute-start(bf16[64,8,512]{2,1,0:T(8,128)(2,1)} %get-tuple-element.38), channel_id=1, source_target_pairs={{0,1},{1,0},{2,3},{3,2},{4,5},{5,4},{6,7},{7,6},{8,9},{9,8},{10,11... | collective-permute-start | bytes 1572872 | tf_op jit(solution)/shard_map/ppermute | solution.py:522
  33.0 53.3 %copy-start.9 = (bf16[8,8,512]{2,1,0:T(8,128)(2,1)}, bf16[8,8,512]{2,1,0:T(8,128)(2,1)S(1)}, u32[]{:S(2)}) copy-start(bf16[8,8,512]{2,1,0:T(8,128)(2,1)S(1)} %collective-permute-done.5.refs_2_) | copy-start | bytes 196612
  33.0 39.8 %collective-permute-start.1 = (bf16[64,8,512]{2,1,0:T(8,128)(2,1)}, bf16[64,8,512]{2,1,0:T(8,128)(2,1)S(1)}, u32[]{:S(2)}, u32[]{:S(2)}) collective-permute-start(bf16[64,8,512]{2,1,0:T(8,128)(2,1)} %get-tuple-element.39), channel_id=1, source_target_pairs={{0,2},{1,3},{2,0},{3,1},{4,6},{5,7},{6,4},{7,5},{8,10},{9,11},{10,... | collective-permute-start | bytes 1572872 | tf_op jit(solution)/shard_map/ppermute | solution.py:522
  33.1 44.4 %copy-start.10 = (bf16[8,8,512]{2,1,0:T(8,128)(2,1)}, bf16[8,8,512]{2,1,0:T(8,128)(2,1)S(1)}, u32[]{:S(2)}) copy-start(bf16[8,8,512]{2,1,0:T(8,128)(2,1)S(1)} %collective-permute-done.15.refs_0_) | copy-start | bytes 196612
  33.1 42.1 %collective-permute-start.2 = (bf16[64,8,512]{2,1,0:T(8,128)(2,1)}, bf16[64,8,512]{2,1,0:T(8,128)(2,1)S(1)}, u32[]{:S(2)}, u32[]{:S(2)}) collective-permute-start(bf16[64,8,512]{2,1,0:T(8,128)(2,1)} %get-tuple-element.40), channel_id=1, source_target_pairs={{0,3},{1,2},{2,1},{3,0},{4,7},{5,6},{6,5},{7,4},{8,11},{9,10},{10,... | collective-permute-start | bytes 1572872 | tf_op jit(solution)/shard_map/ppermute | solution.py:522
  34.9 42.6 %copy-start.11 = (bf16[8,8,512]{2,1,0:T(8,128)(2,1)}, bf16[8,8,512]{2,1,0:T(8,128)(2,1)S(1)}, u32[]{:S(2)}) copy-start(bf16[8,8,512]{2,1,0:T(8,128)(2,1)S(1)} %collective-permute-done.16.refs_1_) | copy-start | bytes 196612
  34.9 8.4 %collective-permute-start.18 = (bf16[8,8,512]{2,1,0:T(8,128)(2,1)}, bf16[8,8,512]{2,1,0:T(8,128)(2,1)S(1)}, u32[]{:S(2)}, u32[]{:S(2)}) collective-permute-start(bf16[8,8,512]{2,1,0:T(8,128)(2,1)} %get-tuple-element.57), channel_id=1, source_target_pairs={{0,11},{1,10},{2,9},{3,8},{4,15},{5,14},{6,13},{7,12},{8,3},{9,2},... | collective-permute-start | bytes 196616 | tf_op jit(solution)/shard_map/ppermute | solution.py:522
  38.7 38.8 %copy-start.12 = (bf16[8,8,512]{2,1,0:T(8,128)(2,1)}, bf16[8,8,512]{2,1,0:T(8,128)(2,1)S(1)}, u32[]{:S(2)}) copy-start(bf16[8,8,512]{2,1,0:T(8,128)(2,1)S(1)} %collective-permute-done.17.refs_2_) | copy-start | bytes 196612
  38.7 8.0 %collective-permute-start.19 = (bf16[8,8,512]{2,1,0:T(8,128)(2,1)}, bf16[8,8,512]{2,1,0:T(8,128)(2,1)S(1)}, u32[]{:S(2)}, u32[]{:S(2)}) collective-permute-start(bf16[8,8,512]{2,1,0:T(8,128)(2,1)} %get-tuple-element.58), channel_id=1, source_target_pairs={{0,12},{1,13},{2,14},{3,15},{4,8},{5,9},{6,10},{7,11},{8,4},{9,5},... | collective-permute-start | bytes 196616 | tf_op jit(solution)/shard_map/ppermute | solution.py:522
  43.3 34.2 %copy-start.13 = (bf16[8,8,512]{2,1,0:T(8,128)(2,1)}, bf16[8,8,512]{2,1,0:T(8,128)(2,1)S(1)}, u32[]{:S(2)}) copy-start(bf16[8,8,512]{2,1,0:T(8,128)(2,1)S(1)} %collective-permute-done.18.refs_3_) | copy-start | bytes 196612
  43.3 6.3 %collective-permute-start.20 = (bf16[8,8,512]{2,1,0:T(8,128)(2,1)}, bf16[8,8,512]{2,1,0:T(8,128)(2,1)S(1)}, u32[]{:S(2)}, u32[]{:S(2)}) collective-permute-start(bf16[8,8,512]{2,1,0:T(8,128)(2,1)} %get-tuple-element.59), channel_id=1, source_target_pairs={{0,13},{1,12},{2,15},{3,14},{4,9},{5,8},{6,11},{7,10},{8,5},{9,4},... | collective-permute-start | bytes 196616 | tf_op jit(solution)/shard_map/ppermute | solution.py:522
  46.7 30.8 %copy-start.14 = (bf16[8,8,512]{2,1,0:T(8,128)(2,1)}, bf16[8,8,512]{2,1,0:T(8,128)(2,1)S(1)}, u32[]{:S(2)}) copy-start(bf16[8,8,512]{2,1,0:T(8,128)(2,1)S(1)} %collective-permute-done.19.refs_4_) | copy-start | bytes 196612
  46.7 7.3 %collective-permute-start.21 = (bf16[8,8,512]{2,1,0:T(8,128)(2,1)}, bf16[8,8,512]{2,1,0:T(8,128)(2,1)S(1)}, u32[]{:S(2)}, u32[]{:S(2)}) collective-permute-start(bf16[8,8,512]{2,1,0:T(8,128)(2,1)} %get-tuple-element.60), channel_id=1, source_target_pairs={{0,14},{1,15},{2,12},{3,13},{4,10},{5,11},{6,8},{7,9},{8,6},{9,7},... | collective-permute-start | bytes 196616 | tf_op jit(solution)/shard_map/ppermute | solution.py:522
  49.7 27.9 %copy-start.15 = (bf16[8,8,512]{2,1,0:T(8,128)(2,1)}, bf16[8,8,512]{2,1,0:T(8,128)(2,1)S(1)}, u32[]{:S(2)}) copy-start(bf16[8,8,512]{2,1,0:T(8,128)(2,1)S(1)} %collective-permute-done.20.refs_5_) | copy-start | bytes 196612
  49.7 7.2 %collective-permute-start.22 = (bf16[8,8,512]{2,1,0:T(8,128)(2,1)}, bf16[8,8,512]{2,1,0:T(8,128)(2,1)S(1)}, u32[]{:S(2)}, u32[]{:S(2)}) collective-permute-start(bf16[8,8,512]{2,1,0:T(8,128)(2,1)} %get-tuple-element.61), channel_id=1, source_target_pairs={{0,15},{1,14},{2,13},{3,12},{4,11},{5,10},{6,9},{7,8},{8,7},{9,6},... | collective-permute-start | bytes 196616 | tf_op jit(solution)/shard_map/ppermute | solution.py:522
  54.0 23.6 %copy-start.16 = (bf16[8,8,512]{2,1,0:T(8,128)(2,1)}, bf16[8,8,512]{2,1,0:T(8,128)(2,1)S(1)}, u32[]{:S(2)}) copy-start(bf16[8,8,512]{2,1,0:T(8,128)(2,1)S(1)} %collective-permute-done.21.refs_6_) | copy-start | bytes 196612
  54.0 5.2 %collective-permute-start.11 = (bf16[16,8,512]{2,1,0:T(8,128)(2,1)}, bf16[16,8,512]{2,1,0:T(8,128)(2,1)S(1)}, u32[]{:S(2)}, u32[]{:S(2)}) collective-permute-start(bf16[16,8,512]{2,1,0:T(8,128)(2,1)} %get-tuple-element.49), channel_id=1, source_target_pairs={{0,4},{1,5},{2,6},{3,7},{4,0},{5,1},{6,2},{7,3},{8,12},{9,13},{10,... | collective-permute-start | bytes 393224 | tf_op jit(solution)/shard_map/ppermute | solution.py:522
  56.9 20.7 %copy-start.19 = (bf16[8,8,512]{2,1,0:T(8,128)(2,1)}, bf16[8,8,512]{2,1,0:T(8,128)(2,1)S(1)}, u32[]{:S(2)}) copy-start(bf16[8,8,512]{2,1,0:T(8,128)(2,1)S(1)} %collective-permute-done.22.refs_7_) | copy-start | bytes 196612
  56.9 6.0 %collective-permute-start.12 = (bf16[16,8,512]{2,1,0:T(8,128)(2,1)}, bf16[16,8,512]{2,1,0:T(8,128)(2,1)S(1)}, u32[]{:S(2)}, u32[]{:S(2)}) collective-permute-start(bf16[16,8,512]{2,1,0:T(8,128)(2,1)} %get-tuple-element.50), channel_id=1, source_target_pairs={{0,5},{1,4},{2,7},{3,6},{4,1},{5,0},{6,3},{7,2},{8,13},{9,12},{10,... | collective-permute-start | bytes 393224 | tf_op jit(solution)/shard_map/ppermute | solution.py:522
  59.2 18.4 %copy-start.3 = (bf16[16,8,512]{2,1,0:T(8,128)(2,1)}, bf16[16,8,512]{2,1,0:T(8,128)(2,1)S(1)}, u32[]{:S(2)}) copy-start(bf16[16,8,512]{2,1,0:T(8,128)(2,1)S(1)} %collective-permute-done.11.refs_12_) | copy-start | bytes 393220
  59.2 6.1 %collective-permute-start.13 = (bf16[16,8,512]{2,1,0:T(8,128)(2,1)}, bf16[16,8,512]{2,1,0:T(8,128)(2,1)S(1)}, u32[]{:S(2)}, u32[]{:S(2)}) collective-permute-start(bf16[16,8,512]{2,1,0:T(8,128)(2,1)} %get-tuple-element.51), channel_id=1, source_target_pairs={{0,6},{1,7},{2,4},{3,5},{4,2},{5,3},{6,0},{7,1},{8,14},{9,15},{10,... | collective-permute-start | bytes 393224 | tf_op jit(solution)/shard_map/ppermute | solution.py:522
  62.9 14.7 %copy-start.4 = (bf16[16,8,512]{2,1,0:T(8,128)(2,1)}, bf16[16,8,512]{2,1,0:T(8,128)(2,1)S(1)}, u32[]{:S(2)}) copy-start(bf16[16,8,512]{2,1,0:T(8,128)(2,1)S(1)} %collective-permute-done.12.refs_13_) | copy-start | bytes 393220
  62.9 6.6 %collective-permute-start.14 = (bf16[16,8,512]{2,1,0:T(8,128)(2,1)}, bf16[16,8,512]{2,1,0:T(8,128)(2,1)S(1)}, u32[]{:S(2)}, u32[]{:S(2)}) collective-permute-start(bf16[16,8,512]{2,1,0:T(8,128)(2,1)} %get-tuple-element.52), channel_id=1, source_target_pairs={{0,7},{1,6},{2,5},{3,4},{4,3},{5,2},{6,1},{7,0},{8,15},{9,14},{10,... | collective-permute-start | bytes 393224 | tf_op jit(solution)/shard_map/ppermute | solution.py:522
  65.3 12.3 %copy-start.5 = (bf16[16,8,512]{2,1,0:T(8,128)(2,1)}, bf16[16,8,512]{2,1,0:T(8,128)(2,1)S(1)}, u32[]{:S(2)}) copy-start(bf16[16,8,512]{2,1,0:T(8,128)(2,1)S(1)} %collective-permute-done.13.refs_14_) | copy-start | bytes 393220
  65.3 16.5 %collective-permute-start.6 = (bf16[8,8,512]{2,1,0:T(8,128)(2,1)}, bf16[8,8,512]{2,1,0:T(8,128)(2,1)S(1)}, u32[]{:S(2)}, u32[]{:S(2)}) collective-permute-start(bf16[8,8,512]{2,1,0:T(8,128)(2,1)} %get-tuple-element.44), channel_id=1, source_target_pairs={{0,11},{1,10},{2,9},{3,8},{4,15},{5,14},{6,13},{7,12},{8,3},{9,2},... | collective-permute-start | bytes 196616 | tf_op jit(solution)/shard_map/ppermute | solution.py:522
  69.5 8.1 %copy-start.6 = (bf16[16,8,512]{2,1,0:T(8,128)(2,1)}, bf16[16,8,512]{2,1,0:T(8,128)(2,1)S(1)}, u32[]{:S(2)}) copy-start(bf16[16,8,512]{2,1,0:T(8,128)(2,1)S(1)} %collective-permute-done.14.refs_15_) | copy-start | bytes 393220
  69.5 12.4 %collective-permute-start.7 = (bf16[8,8,512]{2,1,0:T(8,128)(2,1)}, bf16[8,8,512]{2,1,0:T(8,128)(2,1)S(1)}, u32[]{:S(2)}, u32[]{:S(2)}) collective-permute-start(bf16[8,8,512]{2,1,0:T(8,128)(2,1)} %get-tuple-element.45), channel_id=1, source_target_pairs={{0,12},{1,13},{2,14},{3,15},{4,8},{5,9},{6,10},{7,11},{8,4},{9,5},... | collective-permute-start | bytes 196616 | tf_op jit(solution)/shard_map/ppermute | solution.py:522
  70.7 6.9 %copy-start = (bf16[64,8,512]{2,1,0:T(8,128)(2,1)}, bf16[64,8,512]{2,1,0:T(8,128)(2,1)S(1)}, u32[]{:S(2)}) copy-start(bf16[64,8,512]{2,1,0:T(8,128)(2,1)S(1)} %collective-permute-done.refs_1_.refs_9_) | copy-start | bytes 1572868
  70.7 12.9 %collective-permute-start.8 = (bf16[8,8,512]{2,1,0:T(8,128)(2,1)}, bf16[8,8,512]{2,1,0:T(8,128)(2,1)S(1)}, u32[]{:S(2)}, u32[]{:S(2)}) collective-permute-start(bf16[8,8,512]{2,1,0:T(8,128)(2,1)} %get-tuple-element.46), channel_id=1, source_target_pairs={{0,13},{1,12},{2,15},{3,14},{4,9},{5,8},{6,11},{7,10},{8,5},{9,4},... | collective-permute-start | bytes 196616 | tf_op jit(solution)/shard_map/ppermute | solution.py:522
  72.8 4.8 %copy-start.1 = (bf16[64,8,512]{2,1,0:T(8,128)(2,1)}, bf16[64,8,512]{2,1,0:T(8,128)(2,1)S(1)}, u32[]{:S(2)}) copy-start(bf16[64,8,512]{2,1,0:T(8,128)(2,1)S(1)} %collective-permute-done.1.refs_2_.refs_10_) | copy-start | bytes 1572868
  72.8 13.5 %collective-permute-start.9 = (bf16[8,8,512]{2,1,0:T(8,128)(2,1)}, bf16[8,8,512]{2,1,0:T(8,128)(2,1)S(1)}, u32[]{:S(2)}, u32[]{:S(2)}) collective-permute-start(bf16[8,8,512]{2,1,0:T(8,128)(2,1)} %get-tuple-element.47), channel_id=1, source_target_pairs={{0,14},{1,15},{2,12},{3,13},{4,10},{5,11},{6,8},{7,9},{8,6},{9,7},... | collective-permute-start | bytes 196616 | tf_op jit(solution)/shard_map/ppermute | solution.py:522
  75.2 11.0 %collective-permute-start.10 = (bf16[8,8,512]{2,1,0:T(8,128)(2,1)}, bf16[8,8,512]{2,1,0:T(8,128)(2,1)S(1)}, u32[]{:S(2)}, u32[]{:S(2)}) collective-permute-start(bf16[8,8,512]{2,1,0:T(8,128)(2,1)} %get-tuple-element.48), channel_id=1, source_target_pairs={{0,15},{1,14},{2,13},{3,12},{4,11},{5,10},{6,9},{7,8},{8,7},{9,6},... | collective-permute-start | bytes 196616 | tf_op jit(solution)/shard_map/ppermute | solution.py:522
  81.8 4.5 %copy-start.17 = (bf16[8,8,512]{2,1,0:T(8,128)(2,1)}, bf16[8,8,512]{2,1,0:T(8,128)(2,1)S(1)}, u32[]{:S(2)}) copy-start(bf16[8,8,512]{2,1,0:T(8,128)(2,1)S(1)} %collective-permute-done.6.refs_3_) | copy-start | bytes 196612
  81.8 11.7 %collective-permute-start.24 = (bf16[2,8,16,128]{3,2,1,0:T(8,128)(2,1)}, bf16[2,8,16,128]{3,2,1,0:T(8,128)(2,1)S(1)}, u32[]{:S(2)}, u32[]{:S(2)}) collective-permute-start(bf16[2,8,16,128]{3,2,1,0:T(8,128)(2,1)} %get-tuple-element.64), channel_id=1, source_target_pairs={{0,4},{1,5},{2,6},{3,7},{4,0},{5,1},{6,2},{7,3},{8,12},{9,13},{10,... | collective-permute-start | bytes 196616 | tf_op jit(solution)/shard_map/ppermute | solution.py:522
  81.9 19.1 %collective-permute-start.26 = (bf16[2,8,16,128]{3,2,1,0:T(8,128)(2,1)}, bf16[2,8,16,128]{3,2,1,0:T(8,128)(2,1)S(1)}, u32[]{:S(2)}, u32[]{:S(2)}) collective-permute-start(bf16[2,8,16,128]{3,2,1,0:T(8,128)(2,1)} %get-tuple-element.66), channel_id=1, source_target_pairs={{0,8},{1,9},{2,10},{3,11},{4,12},{5,13},{6,14},{7,15},{8,0},{9,1},... | collective-permute-start | bytes 196616 | tf_op jit(solution)/shard_map/ppermute | solution.py:522
  83.7 17.4 %collective-permute-start.28 = (bf16[2,8,16,128]{3,2,1,0:T(8,128)(2,1)}, bf16[2,8,16,128]{3,2,1,0:T(8,128)(2,1)S(1)}, u32[]{:S(2)}, u32[]{:S(2)}) collective-permute-start(bf16[2,8,16,128]{3,2,1,0:T(8,128)(2,1)} %get-tuple-element.68), channel_id=1, source_target_pairs={{0,12},{1,13},{2,14},{3,15},{4,8},{5,9},{6,10},{7,11},{8,4},{9,5},... | collective-permute-start | bytes 196616 | tf_op jit(solution)/shard_map/ppermute | solution.py:522
  91.7 9.4 %collective-permute-start.23 = (bf16[2,8,16,128]{3,2,1,0:T(8,128)(2,1)}, bf16[2,8,16,128]{3,2,1,0:T(8,128)(2,1)S(1)}, u32[]{:S(2)}, u32[]{:S(2)}) collective-permute-start(bf16[2,8,16,128]{3,2,1,0:T(8,128)(2,1)} %get-tuple-element.63), channel_id=1, source_target_pairs={{0,4},{1,5},{2,6},{3,7},{4,0},{5,1},{6,2},{7,3},{8,12},{9,13},{10,... | collective-permute-start | bytes 196616 | tf_op jit(solution)/shard_map/ppermute | solution.py:522
  91.7 9.4 %collective-permute-start.25 = (bf16[2,8,16,128]{3,2,1,0:T(8,128)(2,1)}, bf16[2,8,16,128]{3,2,1,0:T(8,128)(2,1)S(1)}, u32[]{:S(2)}, u32[]{:S(2)}) collective-permute-start(bf16[2,8,16,128]{3,2,1,0:T(8,128)(2,1)} %get-tuple-element.65), channel_id=1, source_target_pairs={{0,8},{1,9},{2,10},{3,11},{4,12},{5,13},{6,14},{7,15},{8,0},{9,1},... | collective-permute-start | bytes 196616 | tf_op jit(solution)/shard_map/ppermute | solution.py:522
  93.5 7.6 %copy-start.18 = (bf16[2,8,16,128]{3,2,1,0:T(8,128)(2,1)}, bf16[2,8,16,128]{3,2,1,0:T(8,128)(2,1)S(1)}, u32[]{:S(2)}) copy-start(bf16[2,8,16,128]{3,2,1,0:T(8,128)(2,1)S(1)} %collective-permute-done.24.refs_3_) | copy-start | bytes 196612
  93.5 7.6 %collective-permute-start.27 = (bf16[2,8,16,128]{3,2,1,0:T(8,128)(2,1)}, bf16[2,8,16,128]{3,2,1,0:T(8,128)(2,1)S(1)}, u32[]{:S(2)}, u32[]{:S(2)}) collective-permute-start(bf16[2,8,16,128]{3,2,1,0:T(8,128)(2,1)} %get-tuple-element.67), channel_id=1, source_target_pairs={{0,12},{1,13},{2,14},{3,15},{4,8},{5,9},{6,10},{7,11},{8,4},{9,5},... | collective-permute-start | bytes 196616 | tf_op jit(solution)/shard_map/ppermute | solution.py:522
  (10 other events, 13.9 us)
